TPU v7x, 32 devices: a whole 2x2x4 slice. The times are simulated.
32 devices in a mesh: mem: 4 (over x, core), gx: 4 (over z), gy: 2 (over y).
Axes of the slice: x: 2, y: 2, z: 4, core: 2. Of those that a mesh axis runs over, the one named last changes fastest.
Arguments:
- prior_sample_set: float32 [256, 2, 32, 256], P('mem', None, 'gx', 'gy'), may hold values from -6 to 6
- flow_speeds: float32 [2, 2, 32, 256], P(None, None, 'gx', 'gy'), may hold values from -0.6 to 0.6
- observed_cells: int32 [4, 2, 4, 1, 128], P('gx', 'gy', 'mem'), may hold values from 0 to 511
- observed_values: float32 [4, 2, 4, 1, 128], P('gx', 'gy', 'mem'), may hold values from -6 to 6
- error_variance: float32 [4, 2, 4, 1, 128], P('gx', 'gy', 'mem'), may hold values from 0.5 to 4
Outputs:
- analysis: bfloat16 [256, 2, 32, 256], P('mem', None, 'gx', 'gy')
All inputs are finite; a program needn't handle non-finite values.
Results may differ from a plain program's by a relative error of at most 0.001.
The roundings to bfloat16 on the way count: a program that leaves them out, or rounds other values in their place, can miss the bound.
Values may be sent and summed in bfloat16 or wider, within the bound.
No kernel may reach another device: no remote copies, remote signals or barrier semaphores. Data moves between devices by JAX's collectives and lax.ppermute only.
A program may use at most 64 MiB of HBM per device.

v0:
```python
import jax
import jax.numpy as jnp
from jax import lax
from jax.sharding import PartitionSpec as P

ROOT_STEPS = 4


diffusion = 0.1
coupling = 0.2


def with_halo(block, sides, width):
    for axis, dim in sides:
        count = lax.axis_size(axis)
        forward = [(i, i + 1) for i in range(count - 1)]
        forward.append((count - 1, 0))
        backward = [(target, source) for source, target in forward]
        low = lax.ppermute(
            lax.slice_in_dim(block, block.shape[dim] - width, None, axis=dim), axis, forward
        )
        high = lax.ppermute(lax.slice_in_dim(block, 0, width, axis=dim), axis, backward)
        block = jnp.concatenate([low, block, high], axis=dim)
    return block


def tendency(model_mesh_field, wind_x, wind_y):
    centre = model_mesh_field[:, :, 1:-1, 1:-1]
    north = model_mesh_field[:, :, 2:, 1:-1]
    south = model_mesh_field[:, :, :-2, 1:-1]
    east = model_mesh_field[:, :, 1:-1, 2:]
    west = model_mesh_field[:, :, 1:-1, :-2]
    layer_mean = jnp.mean(centre, axis=1, keepdims=True)
    return (
        -0.5 * wind_x * (north - south)
        - 0.5 * wind_y * (east - west)
        + diffusion * (north + south + east + west - 4.0 * centre)
        + coupling * (layer_mean - centre)
    )


def crop_margin(array, width):
    return array[:, :, width : array.shape[2] - width, width : array.shape[3] - width]


def deep_step(model_mesh_field, wind_pad):
    padded = with_halo(model_mesh_field, (("gx", 2), ("gy", 3)), 4)
    wind_three = crop_margin(wind_pad, 1)
    wind_two = crop_margin(wind_pad, 2)
    wind_one = crop_margin(wind_pad, 3)
    wind_zero = crop_margin(wind_pad, 4)
    section_one = tendency(padded, wind_three[0], wind_three[1])
    section_two = tendency(crop_margin(padded, 1) + 0.5 * section_one, wind_two[0], wind_two[1])
    section_three = tendency(crop_margin(padded, 2) + 0.5 * section_two, wind_one[0], wind_one[1])
    section_four = tendency(crop_margin(padded, 3) + section_three, wind_zero[0], wind_zero[1])
    return (
        crop_margin(padded, 4)
        + (
            crop_margin(section_one, 3)
            + 2.0 * crop_margin(section_two, 2)
            + 2.0 * crop_margin(section_three, 1)
            + section_four
        )
        / 6.0
    )


def transform_device(weights, rolled):
    return jnp.einsum("qik,ilsqc->klsqc", weights, rolled, preferred_element_type=jnp.float32)


def analyze(strip_block, cells, values, errors, transform):
    realization_vectors, layer_stack, rows, width = strip_block.shape
    patches, count = cells.shape
    patch = width // patches
    highest = lax.Precision.HIGHEST
    mean_field = jnp.mean(strip_block, axis=0, dtype=jnp.float32)
    layer_of = cells // (rows * patch)
    row_of = cells // patch % rows
    column = cells % patch
    starts = (jnp.arange(patches, dtype=jnp.int32) * patch)[:, None]
    flat_index = layer_of * (rows * width) + row_of * width + starts + column
    picked = jnp.take(
        strip_block.reshape(realization_vectors, layer_stack * rows * width),
        flat_index.reshape(-1),
        axis=1,
    )
    base = jnp.take(mean_field.reshape(-1), flat_index.reshape(-1)).reshape(patches, count)
    spread = picked.astype(jnp.float32).reshape(realization_vectors, patches, count) - base[None]
    innovation = values - base
    offset = column.astype(jnp.float32) - 0.5 * (patch - 1)
    spread_parts = []
    innovation_parts = []
    for shift in (-1, 0, 1):
        distance = (shift * patch + jnp.roll(offset, -shift, axis=0)) / patch
        scale = jnp.sqrt(jnp.exp(-0.5 * distance * distance) / jnp.roll(errors, -shift, axis=0))
        spread_parts.append(jnp.roll(spread, -shift, axis=1) * scale[None])
        innovation_parts.append(jnp.roll(innovation, -shift, axis=0) * scale)
    scaled = jnp.concatenate(spread_parts, axis=2)
    scaled_innovation = jnp.concatenate(innovation_parts, axis=1)
    identity = jnp.eye(realization_vectors, dtype=jnp.float32)
    gram = (
        jnp.einsum("kpj,ipj->pki", scaled, scaled, precision=highest)
        + (realization_vectors - 1.0) * identity
    )
    frob = jnp.sqrt(jnp.sum(gram * gram, axis=(1, 2)))
    current = gram / frob[:, None, None]
    root = jnp.broadcast_to(identity, gram.shape)
    for step in range(ROOT_STEPS):
        middle = 1.5 * identity - 0.5 * jnp.einsum("pab,pbc->pac", root, current, precision=highest)
        current = jnp.einsum("pab,pbc->pac", current, middle, precision=highest)
        root = jnp.einsum("pab,pbc->pac", middle, root, precision=highest)
    projected = jnp.einsum("kpj,pj->pk", scaled, scaled_innovation, precision=highest)
    once = jnp.einsum("pab,pb->pa", root, projected, precision=highest)
    twice = jnp.einsum("pab,pb->pa", root, once, precision=highest)
    mean_weights = twice / frob[:, None]
    weights = (
        jnp.sqrt(realization_vectors - 1.0) * root / jnp.sqrt(frob)[:, None, None]
        + mean_weights[:, :, None]
    ).astype(jnp.bfloat16)
    perturbation = (strip_block - mean_field[None]).astype(jnp.bfloat16)
    rolled = jnp.roll(perturbation, -(patch // 2), axis=3).reshape(
        realization_vectors, layer_stack, rows, patches, patch
    )
    first = transform(weights, rolled)
    second = transform(jnp.roll(weights, -1, axis=0), rolled)
    position = (jnp.arange(patch, dtype=jnp.float32) + 0.5) / patch
    increment = ((1.0 - position) * first + position * second).reshape(
        realization_vectors, layer_stack, rows, width
    )
    return (jnp.roll(increment, patch // 2, axis=3) + mean_field[None]).astype(jnp.bfloat16)


def on_device(prior_sample_set, flow_speeds, observed_cells, observed_values, error_variance):
    member_group_count = lax.axis_size("mem")
    northward_group_count = lax.axis_size("gy")
    local_member_states, layer_stack, rows_x, column_count_north = prior_sample_set.shape
    band_row_count = rows_x // (member_group_count * northward_group_count)
    all_members = local_member_states * member_group_count
    model_mesh_field = prior_sample_set
    wind_pad = with_halo(flow_speeds, (("gx", 2), ("gy", 3)), 4)
    model_mesh_field = deep_step(model_mesh_field, wind_pad)
    advance_sample_set = model_mesh_field.astype(jnp.bfloat16)
    flattened_realizations = advance_sample_set.reshape(
        local_member_states,
        layer_stack,
        northward_group_count,
        member_group_count,
        band_row_count,
        column_count_north,
    )
    flattened_realizations = flattened_realizations.transpose(3, 2, 0, 1, 4, 5).reshape(
        member_group_count * northward_group_count,
        local_member_states,
        layer_stack,
        band_row_count,
        column_count_north,
    )
    received = lax.all_to_all(
        flattened_realizations, ("mem", "gy"), split_axis=0, concat_axis=0, tiled=True
    )
    received = received.reshape(
        member_group_count,
        northward_group_count,
        local_member_states,
        layer_stack,
        band_row_count,
        column_count_north,
    )
    columns = received.transpose(0, 2, 3, 4, 1, 5).reshape(
        all_members, layer_stack, band_row_count, northward_group_count * column_count_north
    )
    cells = observed_cells.reshape(observed_cells.shape[-2], observed_cells.shape[-1])
    values = observed_values.reshape(observed_values.shape[-2], observed_values.shape[-1])
    errors = error_variance.reshape(error_variance.shape[-2], error_variance.shape[-1])
    analysed = analyze(columns, cells, values, errors, transform_device)
    outgoing = analysed.reshape(
        member_group_count,
        local_member_states,
        layer_stack,
        band_row_count,
        northward_group_count,
        column_count_north,
    )
    outgoing = outgoing.transpose(0, 4, 1, 2, 3, 5).reshape(
        member_group_count * northward_group_count,
        local_member_states,
        layer_stack,
        band_row_count,
        column_count_north,
    )
    returned = lax.all_to_all(outgoing, ("mem", "gy"), split_axis=0, concat_axis=0, tiled=True)
    returned = returned.reshape(
        member_group_count,
        northward_group_count,
        local_member_states,
        layer_stack,
        band_row_count,
        column_count_north,
    )
    return returned.transpose(2, 3, 1, 0, 4, 5).reshape(
        local_member_states, layer_stack, rows_x, column_count_north
    )


def solution(mesh):
    in_specs = (
        P("mem", None, "gx", "gy"),
        P(None, None, "gx", "gy"),
        P("gx", "gy", "mem", None, None),
        P("gx", "gy", "mem", None, None),
        P("gx", "gy", "mem", None, None),
    )
    out_specs = P("mem", None, "gx", "gy")
    return jax.shard_map(
        on_device, mesh=mesh, in_specs=in_specs, out_specs=out_specs, check_vma=False
    )
```

profile of v0, /device:TPU:0, one launch (start us, length us, event | category | flops | bytes accessed | tf_op | source)
XLA Modules:
  0.0 74.6 jit_solution(8725785093874270631)
XLA Ops:
  0.0 0.8 %fusion.50 = (f32[2,2,4,128]{3,2,1,0:T(4,128)S(1)}, f32[2,2,4,128]{3,2,1,0:T(4,128)S(1)}) fusion(f32[2,2,8,128]{3,2,1,0:T(8,128)} %param.6), kind=kLoop, calls=%fused_computation.140 | loop fusion | bytes 32768 | tf_op jit(solution)/shard_map/slice | solution.py:20
  0.8 3.1 %collective-permute-start = (f32[2,2,4,128]{3,2,1,0:T(4,128)S(1)}, f32[2,2,4,128]{3,2,1,0:T(4,128)S(1)}, u32[]{:S(2)}, u32[]{:S(2)}) collective-permute-start(f32[2,2,4,128]{3,2,1,0:T(4,128)S(1)} %get-tuple-element.39), channel_id=1, source_target_pairs={{0,2},{2,4},{4,6},{6,0},{1,3},{3,5},{5,7},{7,1},{8,10},{10,12},{12... | collective-permute-start | bytes 24584 | tf_op jit(solution)/shard_map/ppermute | solution.py:19
  3.9 2.1 %collective-permute-start.1 = (f32[2,2,4,128]{3,2,1,0:T(4,128)S(1)}, f32[2,2,4,128]{3,2,1,0:T(4,128)S(1)}, u32[]{:S(2)}, u32[]{:S(2)}) collective-permute-start(f32[2,2,4,128]{3,2,1,0:T(4,128)S(1)} %get-tuple-element.40), channel_id=1, source_target_pairs={{2,0},{4,2},{6,4},{0,6},{3,1},{5,3},{7,5},{1,7},{10,8},{12,10},{14... | collective-permute-start | bytes 24584 | tf_op jit(solution)/shard_map/ppermute | solution.py:22
  6.0 1.3 %fusion.47 = (f32[64,2,4,128]{3,2,1,0:T(4,128)S(1)}, f32[64,2,4,128]{3,2,1,0:T(4,128)S(1)}) fusion(f32[64,2,8,128]{3,2,1,0:T(8,128)} %param.5), kind=kLoop, calls=%fused_computation.137 | loop fusion | bytes 1048576 | tf_op jit(solution)/shard_map/slice | solution.py:22
  7.5 3.9 %collective-permute-start.5 = (f32[64,2,4,128]{3,0,2,1:T(8,128)S(1)}, f32[64,2,4,128]{3,0,2,1:T(8,128)S(1)}, u32[]{:S(2)}, u32[]{:S(2)}) collective-permute-start(f32[64,2,4,128]{3,0,2,1:T(8,128)S(1)} %copy.67), channel_id=1, source_target_pairs={{2,0},{4,2},{6,4},{0,6},{3,1},{5,3},{7,5},{1,7},{10,8},{12,10},{14... | collective-permute-start | bytes 786440 | tf_op jit(solution)/shard_map/ppermute | solution.py:22
  11.4 1.7 %collective-permute-start.2 = (f32[2,2,16,4]{3,2,1,0:T(8,128)S(1)}, f32[2,2,16,4]{3,2,1,0:T(8,128)S(1)}, u32[]{:S(2)}, u32[]{:S(2)}) collective-permute-start(f32[2,2,16,4]{3,2,1,0:T(8,128)S(1)} %get-tuple-element.35), channel_id=1, source_target_pairs={{0,1},{1,0},{2,3},{3,2},{4,5},{5,4},{6,7},{7,6},{8,9},{9,8},{10,11... | collective-permute-start | bytes 3080 | tf_op jit(solution)/shard_map/ppermute | solution.py:19
  13.5 1.9 %collective-permute-done.2 = f32[2,2,16,4]{3,2,1,0:T(8,128)S(1)} collective-permute-done((f32[2,2,16,4]{3,2,1,0:T(8,128)S(1)}, f32[2,2,16,4]{3,2,1,0:T(8,128)S(1)}, u32[]{:S(2)}, u32[]{:S(2)}) %collective-permute-start.2) | collective-permute-done | bytes 1056 | tf_op jit(solution)/shard_map/ppermute | solution.py:19
  15.4 1.7 %collective-permute-done.3 = f32[2,2,16,4]{3,2,1,0:T(8,128)S(1)} collective-permute-done((f32[2,2,16,4]{3,2,1,0:T(8,128)S(1)}, f32[2,2,16,4]{3,2,1,0:T(8,128)S(1)}, u32[]{:S(2)}, u32[]{:S(2)}) %collective-permute-start.3) | collective-permute-done | bytes 1056 | tf_op jit(solution)/shard_map/ppermute | solution.py:22
  17.3 1.0 %collective-permute-done.4 = f32[64,2,4,128]{3,0,2,1:T(8,128)S(1)} collective-permute-done((f32[64,2,4,128]{3,0,2,1:T(8,128)S(1)}, f32[64,2,4,128]{3,0,2,1:T(8,128)S(1)}, u32[]{:S(2)}, u32[]{:S(2)}) %collective-permute-start.4) | collective-permute-done | bytes 262176 | tf_op jit(solution)/shard_map/ppermute | solution.py:19
  18.6 2.3 %collective-permute-done.5 = f32[64,2,4,128]{3,0,2,1:T(8,128)S(1)} collective-permute-done((f32[64,2,4,128]{3,0,2,1:T(8,128)S(1)}, f32[64,2,4,128]{3,0,2,1:T(8,128)S(1)}, u32[]{:S(2)}, u32[]{:S(2)}) %collective-permute-start.5) | collective-permute-done | bytes 262176 | tf_op jit(solution)/shard_map/ppermute | solution.py:22
  20.9 1.4 %fusion.45 = (f32[64,2,16,4]{3,0,2,1:T(8,128)}, f32[64,2,16,4]{3,0,2,1:T(8,128)S(1)}) fusion(f32[64,2,16,128]{3,0,2,1:T(8,128)S(1)} %constant_dynamic-update-slice_fusion), kind=kLoop, calls=%fused_computation.135 | loop fusion | bytes 131072 | tf_op jit(solution)/shard_map/slice | solution.py:20
  22.3 1.6 %copy.46 = f32[64,2,16,4]{0,2,3,1:T(8,128)S(1)} copy(f32[64,2,16,4]{3,0,2,1:T(8,128)} %get-tuple-element.18) | data formatting | bytes 65536 | tf_op jit(solution)/shard_map/slice | solution.py:20
  23.9 1.6 %collective-permute-start.6 = (f32[64,2,16,4]{0,2,3,1:T(8,128)S(1)}, f32[64,2,16,4]{0,2,3,1:T(8,128)S(1)}, u32[]{:S(2)}, u32[]{:S(2)}) collective-permute-start(f32[64,2,16,4]{0,2,3,1:T(8,128)S(1)} %copy.46), channel_id=1, source_target_pairs={{0,1},{1,0},{2,3},{3,2},{4,5},{5,4},{6,7},{7,6},{8,9},{9,8},{10,11... | collective-permute-start | bytes 98312 | tf_op jit(solution)/shard_map/ppermute | solution.py:19
  25.8 0.6 collective-permute-start.7
  26.5 1.7 %collective-permute-done.6 = f32[64,2,16,4]{0,2,3,1:T(8,128)S(1)} collective-permute-done((f32[64,2,16,4]{0,2,3,1:T(8,128)S(1)}, f32[64,2,16,4]{0,2,3,1:T(8,128)S(1)}, u32[]{:S(2)}, u32[]{:S(2)}) %collective-permute-start.6) | collective-permute-done | bytes 32800 | tf_op jit(solution)/shard_map/ppermute | solution.py:19
  28.6 1.5 %collective-permute-done.7 = f32[64,2,16,4]{0,2,3,1:T(8,128)S(1)} collective-permute-done((f32[64,2,16,4]{0,2,3,1:T(8,128)S(1)}, f32[64,2,16,4]{0,2,3,1:T(8,128)S(1)}, u32[]{:S(2)}, u32[]{:S(2)}) %collective-permute-start.7) | collective-permute-done | bytes 32800 | tf_op jit(solution)/shard_map/ppermute | solution.py:22
  30.1 1.4 %copy.49 = f32[64,2,16,4]{3,0,2,1:T(8,128)} copy(f32[64,2,16,4]{0,2,3,1:T(8,128)S(1)} %collective-permute-done.7) | data formatting | bytes 65536 | tf_op jit(solution)/shard_map/ppermute | solution.py:22
  31.5 2.1 %pad_maximum_fusion = f32[64,2,16,136]{3,0,2,1:T(8,128)S(1)} fusion(f32[64,2,16,4]{3,0,2,1:T(8,128)} %copy.49, f32[64,2,16,128]{3,0,2,1:T(8,128)S(1)} %constant_dynamic-update-slice_fusion, f32[64,2,16,4]{3,0,2,1:T(8,128)S(1)} %copy.48), kind=kLoop, calls=%fused_computation.2 | loop fusion | flops 557056 | bytes 2228224 | tf_op jit(solution)/shard_map/concatenate | solution.py:23
  33.6 0.5 slice_reduce_fusion
  34.2 2.0 %multiply_add_fusion = (f32[64,2,14,134]{3,0,2,1:T(8,128)S(1)}, f32[64,2,14,134]{3,0,2,1:T(8,128)S(1)}) fusion(f32[64,2,16,136]{3,0,2,1:T(8,128)S(1)} %pad_maximum_fusion, f32[64,14,134]{2,0,1:T(8,128)S(1)} %broadcast_multiply_fusion, f32[2,14,134]{2,1,0:T(8,128)S(1)} %get-tuple-element.34, f32[2,14,134]{2,1,0:T(8,128)S(1)} %get-tuple-element.33), kind=kLoop, calls=%fused_computation.3 | loop fusion | flops 4082176 | bytes 7233856 | tf_op jit(solution)/shard_map/add | solution.py:53
  36.7 2.1 %slice_add_fusion = (f32[64,2,12,132]{3,0,2,1:T(8,128)S(1)}, f32[64,2,12,132]{3,0,2,1:T(8,128)S(1)}) fusion(f32[64,2,16,136]{3,0,2,1:T(8,128)S(1)} %pad_maximum_fusion, f32[64,12,132]{2,0,1:T(8,128)S(1)} %broadcast_multiply_fusion.1, f32[64,2,14,134]{3,0,2,1:T(8,128)S(1)} %get-tuple-element.16, f32[2,12,132]{2,1,0:T(8,128)S(1)} %get-tuple-element.32, ...), kind=kLoop, calls=%fused_computation.6 | loop fusion | flops 3446784 | bytes 6918912 | tf_op jit(solution)/shard_map/add | solution.py:54
  39.3 1.8 %slice_add_fusion.1 = (f32[64,2,10,130]{3,0,2,1:T(8,128)S(1)}, f32[64,2,10,130]{3,0,2,1:T(8,128)S(1)}) fusion(f32[64,2,16,136]{3,0,2,1:T(8,128)S(1)} %pad_maximum_fusion, f32[64,10,130]{2,0,1:T(8,128)S(1)} %broadcast_multiply_fusion.2, f32[64,2,12,132]{3,0,2,1:T(8,128)S(1)} %get-tuple-element.14, f32[2,10,130]{2,1,0:T(8,128)S(1)} %get-tuple-element.30, ...), kind=kLoop, calls=%fused_computation.9 | loop fusion | flops 2662400 | bytes 5678400 | tf_op jit(solution)/shard_map/add | solution.py:55
  41.3 1.0 %fusion.10 = bf16[64,2,8,128]{3,0,2,1:T(8,128)(2,1)S(1)} fusion(f32[64,2,10,130]{3,0,2,1:T(8,128)S(1)} %get-tuple-element.13, f32[64,2,12,132]{3,0,2,1:T(8,128)S(1)} %get-tuple-element.15, f32[64,2,14,134]{3,0,2,1:T(8,128)S(1)} %get-tuple-element.17, f32[64,2,10,130]{3,0,2,1:T(8,128)S(1)} %get-tuple-element.12, ...), kind=kLoop, calls=%fused_computation.31 | loop fusion | flops 3014656 | bytes 5259264 | tf_op jit(solution)/shard_map/convert_element_type | solution.py:143
  42.4 0.7 copy.51
  43.1 3.6 %all-to-all-start = ((bf16[8,64,2,1,128]{4,1,3,2,0:T(8,128)(2,1)}), bf16[8,64,2,1,128]{4,1,3,2,0:T(8,128)(2,1)S(1)}, u32[]{:S(2)}, u32[]{:S(2)}) async-start(bf16[8,64,2,1,128]{4,1,3,2,0:T(8,128)(2,1)} %bitcast.10), calls=%async_computation | async-start | bytes 524288 | tf_op jit(solution)/shard_map/all_to_all | solution.py:159
  46.8 5.7 %all-to-all-done = bf16[8,64,2,1,128]{4,1,3,2,0:T(8,128)(2,1)S(1)} async-done(((bf16[8,64,2,1,128]{4,1,3,2,0:T(8,128)(2,1)}), bf16[8,64,2,1,128]{4,1,3,2,0:T(8,128)(2,1)S(1)}, u32[]{:S(2)}, u32[]{:S(2)}) %all-to-all-start) | async-done | bytes 262176 | tf_op jit(solution)/shard_map/all_to_all | solution.py:159
  53.2 1.3 %gather_fusion.1 = f32[128]{0:T(128)S(1)} fusion(f32[512]{0:T(512)S(1)} %bitcast.183, s32[1024]{0:T(1024)S(1)} %pad_clamp_fusion), kind=kCustom, calls=%fused_computation.1 | custom fusion | bytes 1536 | tf_op jit(solution)/shard_map/jit(_take)/gather | solution.py:88
  54.5 0.8 %gather_fusion = bf16[128,256]{1,0:T(8,128)(2,1)S(1)} fusion(bf16[256,512]{0,1:T(8,128)(2,1)S(1)} %reshape.1158, s32[1024]{0:T(1024)S(1)} %pad_clamp_fusion), kind=kCustom, calls=%fused_computation | custom fusion | bytes 131584 | tf_op jit(solution)/shard_map/jit(_take)/gather | solution.py:83
  55.5 1.4 %multiply_reduce_fusion = (f32[]{:T(128)}, f32[256,256]{1,0:T(8,128)S(1)}) fusion(f32[256,1,128]{0,2,1:T(8,128)S(1)} %get-tuple-element.27, f32[256,1,128]{0,2,1:T(8,128)S(1)} %get-tuple-element.28, f32[256,1,128]{0,2,1:T(8,128)S(1)} %get-tuple-element.26), kind=kOutput, calls=%fused_computation.47 | convolution fusion | flops 302514176 | bytes 655364 | tf_op jit(solution)/shard_map/kpj,ipj->pki/dot_general | solution.py:103
  63.3 0.5 copy.53
  65.1 8.5 %all_to_all.10 = bf16[8,64,2,1,128]{4,1,3,2,0:T(8,128)(2,1)S(1)} all-to-all(bf16[8,64,2,1,128]{4,1,3,2,0:T(8,128)(2,1)S(1)} %bitcast.189), channel_id=1, replica_groups=mesh['mem'=4,'gx'=4,'gy'=2] {'mem','gy'}, dimensions={0} | all-to-all | bytes 524288 | tf_op jit(solution)/shard_map/all_to_all | solution.py:192
  73.7 0.9 %copy.61 = bf16[64,2,8,128]{3,2,1,0:T(8,128)(2,1)} copy(bf16[64,2,8,128]{3,0,2,1:T(8,128)(2,1)S(1)} %bitcast.191) | data formatting | bytes 524288 | tf_op jit(solution)/shard_map/reshape | solution.py:201
  (73 shorter events, 10.9 us)
Async XLA Ops:
  0.0 11.3 %copy-start.1 = (f32[2,2,8,128]{3,2,1,0:T(8,128)S(1)}, f32[2,2,8,128]{3,2,1,0:T(8,128)}, u32[]{:S(2)}) copy-start(f32[2,2,8,128]{3,2,1,0:T(8,128)} %param.6) | copy-start | bytes 49156
  0.0 13.5 %copy-start.3 = (s32[1,1,1,1,128]{4,3,2,1,0:T(1,128)S(1)}, s32[1,1,1,1,128]{4,3,2,1,0:T(1,128)}, u32[]{:S(2)}) copy-start(s32[1,1,1,1,128]{4,3,2,1,0:T(1,128)} %param.7) | copy-start | bytes 1540
  0.8 10.5 %collective-permute-start = (f32[2,2,4,128]{3,2,1,0:T(4,128)S(1)}, f32[2,2,4,128]{3,2,1,0:T(4,128)S(1)}, u32[]{:S(2)}, u32[]{:S(2)}) collective-permute-start(f32[2,2,4,128]{3,2,1,0:T(4,128)S(1)} %get-tuple-element.39), channel_id=1, source_target_pairs={{0,2},{2,4},{4,6},{6,0},{1,3},{3,5},{5,7},{7,1},{8,10},{10,12},{12... | collective-permute-start | bytes 24584 | tf_op jit(solution)/shard_map/ppermute | solution.py:19
  3.9 14.5 %copy-start = (f32[64,2,8,128]{3,2,1,0:T(8,128)S(1)}, f32[64,2,8,128]{3,2,1,0:T(8,128)}, u32[]{:S(2)}) copy-start(f32[64,2,8,128]{3,2,1,0:T(8,128)} %param.5) | copy-start | bytes 1572868
  3.9 7.4 %collective-permute-start.1 = (f32[2,2,4,128]{3,2,1,0:T(4,128)S(1)}, f32[2,2,4,128]{3,2,1,0:T(4,128)S(1)}, u32[]{:S(2)}, u32[]{:S(2)}) collective-permute-start(f32[2,2,4,128]{3,2,1,0:T(4,128)S(1)} %get-tuple-element.40), channel_id=1, source_target_pairs={{2,0},{4,2},{6,4},{0,6},{3,1},{5,3},{7,5},{1,7},{10,8},{12,10},{14... | collective-permute-start | bytes 24584 | tf_op jit(solution)/shard_map/ppermute | solution.py:22
  7.3 11.0 %collective-permute-start.4 = (f32[64,2,4,128]{3,0,2,1:T(8,128)S(1)}, f32[64,2,4,128]{3,0,2,1:T(8,128)S(1)}, u32[]{:S(2)}, u32[]{:S(2)}) collective-permute-start(f32[64,2,4,128]{3,0,2,1:T(8,128)S(1)} %copy.66), channel_id=1, source_target_pairs={{0,2},{2,4},{4,6},{6,0},{1,3},{3,5},{5,7},{7,1},{8,10},{10,12},{12... | collective-permute-start | bytes 786440 | tf_op jit(solution)/shard_map/ppermute | solution.py:19
  7.5 13.4 %collective-permute-start.5 = (f32[64,2,4,128]{3,0,2,1:T(8,128)S(1)}, f32[64,2,4,128]{3,0,2,1:T(8,128)S(1)}, u32[]{:S(2)}, u32[]{:S(2)}) collective-permute-start(f32[64,2,4,128]{3,0,2,1:T(8,128)S(1)} %copy.67), channel_id=1, source_target_pairs={{2,0},{4,2},{6,4},{0,6},{3,1},{5,3},{7,5},{1,7},{10,8},{12,10},{14... | collective-permute-start | bytes 786440 | tf_op jit(solution)/shard_map/ppermute | solution.py:22
  11.4 3.9 %collective-permute-start.2 = (f32[2,2,16,4]{3,2,1,0:T(8,128)S(1)}, f32[2,2,16,4]{3,2,1,0:T(8,128)S(1)}, u32[]{:S(2)}, u32[]{:S(2)}) collective-permute-start(f32[2,2,16,4]{3,2,1,0:T(8,128)S(1)} %get-tuple-element.35), channel_id=1, source_target_pairs={{0,1},{1,0},{2,3},{3,2},{4,5},{5,4},{6,7},{7,6},{8,9},{9,8},{10,11... | collective-permute-start | bytes 3080 | tf_op jit(solution)/shard_map/ppermute | solution.py:19
  13.1 3.9 %collective-permute-start.3 = (f32[2,2,16,4]{3,2,1,0:T(8,128)S(1)}, f32[2,2,16,4]{3,2,1,0:T(8,128)S(1)}, u32[]{:S(2)}, u32[]{:S(2)}) collective-permute-start(f32[2,2,16,4]{3,2,1,0:T(8,128)S(1)} %get-tuple-element.36), channel_id=1, source_target_pairs={{1,0},{0,1},{3,2},{2,3},{5,4},{4,5},{7,6},{6,7},{9,8},{8,9},{11,10... | collective-permute-start | bytes 3080 | tf_op jit(solution)/shard_map/ppermute | solution.py:22
  23.9 4.3 %collective-permute-start.6 = (f32[64,2,16,4]{0,2,3,1:T(8,128)S(1)}, f32[64,2,16,4]{0,2,3,1:T(8,128)S(1)}, u32[]{:S(2)}, u32[]{:S(2)}) collective-permute-start(f32[64,2,16,4]{0,2,3,1:T(8,128)S(1)} %copy.46), channel_id=1, source_target_pairs={{0,1},{1,0},{2,3},{3,2},{4,5},{5,4},{6,7},{7,6},{8,9},{9,8},{10,11... | collective-permute-start | bytes 98312 | tf_op jit(solution)/shard_map/ppermute | solution.py:19
  25.8 4.3 %collective-permute-start.7 = (f32[64,2,16,4]{0,2,3,1:T(8,128)S(1)}, f32[64,2,16,4]{0,2,3,1:T(8,128)S(1)}, u32[]{:S(2)}, u32[]{:S(2)}) collective-permute-start(f32[64,2,16,4]{0,2,3,1:T(8,128)S(1)} %copy.47), channel_id=1, source_target_pairs={{1,0},{0,1},{3,2},{2,3},{5,4},{4,5},{7,6},{6,7},{9,8},{8,9},{11,10... | collective-permute-start | bytes 98312 | tf_op jit(solution)/shard_map/ppermute | solution.py:22
  41.3 5.4 %copy-start.2 = (f32[1,1,1,1,128]{4,3,2,1,0:T(1,128)S(1)}, f32[1,1,1,1,128]{4,3,2,1,0:T(1,128)}, u32[]{:S(2)}) copy-start(f32[1,1,1,1,128]{4,3,2,1,0:T(1,128)} %param.9) | copy-start | bytes 1540
  43.1 9.4 %all-to-all-start = ((bf16[8,64,2,1,128]{4,1,3,2,0:T(8,128)(2,1)}), bf16[8,64,2,1,128]{4,1,3,2,0:T(8,128)(2,1)S(1)}, u32[]{:S(2)}, u32[]{:S(2)}) async-start(bf16[8,64,2,1,128]{4,1,3,2,0:T(8,128)(2,1)} %bitcast.10), calls=%async_computation | async-start | bytes 524288 | tf_op jit(solution)/shard_map/all_to_all | solution.py:159
  59.4 1.6 %copy-start.4 = (f32[1,1,1,1,128]{4,3,2,1,0:T(1,128)S(1)}, f32[1,1,1,1,128]{4,3,2,1,0:T(1,128)}, u32[]{:S(2)}) copy-start(f32[1,1,1,1,128]{4,3,2,1,0:T(1,128)} %param.8) | copy-start | bytes 1540
where the time goes:
time: 75 us; the launch traced here: 74.6 us
  starting transfers between devices  16.8 us (22%)
  waiting for transfers between devices  15.9 us (21%)
  local copies, waits for them, and re-layouts  13.5 us (18%)
  other arithmetic  11.9 us (16%)
  blocking collectives  8.54 us (11%)
  matrix products  6.68 us (9%)
  between operations  1.24 us (2%)
    all_to_all x1, blocking collectives, on_device(): lax.all_to_all(outgoing, ('mem', 'gy'), split_axis=0, concat_axis=0, tile...  8.54 us
    ppermute x4, starting transfers between devices, with_halo(): lax.ppermute(lax.slice_in_dim(block, 0, width, axis=dim), axis, backward)  6.84 us
    ppermute x4, starting transfers between devices, with_halo(): lax.ppermute(lax.slice_in_dim(block, block.shape[dim] - width, None, axis...  6.37 us
    all_to_all x1, waiting for transfers between devices, on_device(): lax.all_to_all(flattened_realizations, ('mem', 'gy'), split_axis=0, conca...  5.71 us
    ppermute x4, waiting for transfers between devices, with_halo(): lax.ppermute(lax.slice_in_dim(block, 0, width, axis=dim), axis, backward)  5.55 us
    ppermute x4, waiting for transfers between devices, with_halo(): lax.ppermute(lax.slice_in_dim(block, block.shape[dim] - width, None, axis...  4.63 us
    slice x4, local copies, waits for them, and re-layouts, with_halo(): lax.slice_in_dim(block, block.shape[dim] - width, None, axis=dim)  3.86 us
    all_to_all x1, starting transfers between devices, on_device(): lax.all_to_all(flattened_realizations, ('mem', 'gy'), split_axis=0, conca...  3.59 us
  transfers between devices with their start and end apart: 9, of which 7 were waited for; matrix products, arithmetic and copies ran while one was open for 4% of the time, Pallas kernels for 0%

commit v1 on v0

--- a/solution.py
+++ b/solution.py
@@ -1,6 +1,11 @@
+import functools
+import math
+
 import jax
 import jax.numpy as jnp
 from jax import lax
+from jax.experimental import pallas as pl
+from jax.experimental.pallas import tpu as pltpu
 from jax.sharding import PartitionSpec as P
 
 ROOT_STEPS = 4
@@ -131,7 +136,7 @@
     return (jnp.roll(increment, patch // 2, axis=3) + mean_field[None]).astype(jnp.bfloat16)
 
 
-def on_device(prior_sample_set, flow_speeds, observed_cells, observed_values, error_variance):
+def on_device_general(prior_sample_set, flow_speeds, observed_cells, observed_values, error_variance):
     member_group_count = lax.axis_size("mem")
     northward_group_count = lax.axis_size("gy")
     local_member_states, layer_stack, rows_x, column_count_north = prior_sample_set.shape
@@ -203,6 +208,522 @@
     )
 
 
+LANES = 128
+HALO = 4
+OCTET = 8
+GROUP = 32
+PACK = LANES // GROUP
+STAGE_FACTORS = (1.0 / 4.0, 1.0 / 3.0, 1.0 / 2.0, 1.0)
+
+
+def lane_iota(shape):
+    return lax.broadcasted_iota(jnp.int32, shape, len(shape) - 1)
+
+
+def lane_roll(x, shift):
+    shift = shift % LANES
+    return x if shift == 0 else pltpu.roll(x, shift, 1)
+
+
+def split_two(x):
+    high = x.astype(jnp.bfloat16)
+    return high, (x - high.astype(jnp.float32)).astype(jnp.bfloat16)
+
+
+def split_three(x):
+    high, rest = x.astype(jnp.bfloat16), None
+    rest = x - high.astype(jnp.float32)
+    middle = rest.astype(jnp.bfloat16)
+    low = (rest - middle.astype(jnp.float32)).astype(jnp.bfloat16)
+    return high, middle, low
+
+
+def tile_row(odd, j):
+    return jnp.where(odd == 1, 11 - j, j - HALO)
+
+
+class Sizes:
+    def __init__(self, local, layers, rows):
+        self.local = local
+        self.layers = layers
+        self.rows = rows
+        self.members = 2 * local
+        self.octets = self.members // OCTET
+        self.packs = self.octets // PACK
+        self.per_member = layers * rows
+        self.halo_rows = layers * (HALO + 1) * self.members
+        self.wind_rows = 2 * layers * HALO
+
+
+def member_rows(s, odd, own_ref, sib_ref, octet, layer, j):
+    half = s.octets // 2
+    start = layer * s.rows + tile_row(odd, j)
+    if isinstance(octet, int):
+        ref = own_ref if octet < half else sib_ref
+        return ref[pl.ds((octet % half) * OCTET * s.per_member + start, OCTET, stride=s.per_member), :]
+    raise ValueError("octet")
+
+
+def pack_halo_kernel(s, own_ref, sib_ref, wind_ref, out_ref, wind_rows_ref):
+    odd = lax.rem(lax.axis_index("mem"), 2)
+    for layer in range(s.layers):
+        for j in range(HALO):
+            base = (layer * (HALO + 1) + HALO - j) * s.members
+            for pair in range(s.octets // 2):
+                value = jnp.concatenate(
+                    [member_rows(s, odd, own_ref, sib_ref, 2 * pair + k, layer, 2 * HALO + j) for k in range(2)], axis=0
+                )
+                high, low = split_two(value)
+                out_ref[pl.ds(base + pair * 16, 16), :] = high
+                if j == HALO - 1:
+                    out_ref[pl.ds(layer * (HALO + 1) * s.members + pair * 16, 16), :] = low
+    copy_wind_rows(s, odd, wind_ref, wind_rows_ref)
+    for i, part in enumerate(split_three(wind_rows_ref[...])):
+        out_ref[pl.ds(s.halo_rows + i * s.wind_rows, s.wind_rows), :] = part
+
+
+def copy_wind_rows(s, odd, from_ref, to_ref):
+    for block in range(2 * s.layers):
+        for j in range(HALO):
+            row = block * s.rows + tile_row(odd, 2 * HALO + j)
+            to_ref[pl.ds(block * HALO + j, 1), :] = from_ref[pl.ds(row, 1), :]
+
+
+def to_strip(x_of):
+    total = None
+    for q in range(PACK):
+        x = x_of(q)
+        lane = lane_iota(x.shape)
+        first = lane_roll(x, HALO + GROUP * q)
+        last = lane_roll(x, 16 + GROUP * q - (LANES - 12))
+        at = lane - GROUP * q
+        if total is None:
+            total = jnp.zeros_like(x)
+        total = jnp.where((at >= HALO) & (at < 16), first, total)
+        total = jnp.where((at >= 16) & (at < 28), last, total)
+    return total
+
+
+def to_edges(strip, k, total):
+    lane = jnp.bitwise_and(lane_iota(strip.shape) + HALO - 8 * k, GROUP - 1)
+    low = lane_roll(strip, 8 * k - 24)
+    high = lane_roll(strip, 24 + 8 * k)
+    both = jnp.where(lane < HALO, high, low)
+    return jnp.where(lane < 2 * HALO, both, total)
+
+
+def with_edges(strip, edges, k):
+    lane = jnp.bitwise_and(lane_iota(strip.shape) + HALO, GROUP - 1)
+    return jnp.where(lane < 2 * HALO, lane_roll(edges, -8 * k), strip)
+
+
+def pack_edges_kernel(s, own_ref, sib_ref, wind_ref, strip_ref, side_ref, corner_ref, wind_strip_ref, rows_ref):
+    odd = lax.rem(lax.axis_index("mem"), 2)
+    size = OCTET
+    for layer in range(s.layers):
+        for block in range(2):
+            for p in range(s.packs):
+                total = jnp.zeros((size, LANES), jnp.float32)
+                for k in range(HALO):
+                    j = HALO + block * HALO + k
+                    strip = to_strip(lambda q: member_rows(s, odd, own_ref, sib_ref, PACK * p + q, layer, j))
+                    strip_ref[pl.ds(((layer * 2 * HALO + j - HALO) * s.packs + p) * size, size), :] = strip
+                    total = to_edges(strip, k, total)
+                side_ref[pl.ds(((layer * 2 + block) * s.packs + p) * size, size), :] = total
+    base = s.layers * 2 * s.packs * size
+    for block in range(2 * s.layers):
+        value = wind_ref[pl.ds(block * s.rows, s.rows), :]
+        strip = to_strip(lambda q: value)
+        wind_strip_ref[pl.ds(block * s.rows, s.rows), :] = strip
+        side_ref[pl.ds(base + block * s.rows, s.rows), :] = to_edges(strip, 0, jnp.zeros_like(strip))
+    for layer in range(s.layers):
+        rows = s.packs * size
+        corner_ref[pl.ds(layer * rows, rows), :] = side_ref[pl.ds((layer * 2 + 1) * rows, rows), :].astype(jnp.bfloat16)
+    for block in range(2 * s.layers):
+        for j in range(HALO):
+            row = base + block * s.rows + tile_row(odd, 2 * HALO + j)
+            rows_ref[pl.ds(block * HALO + j, 1), :] = side_ref[pl.ds(row, 1), :]
+    for i, part in enumerate(split_three(rows_ref[...])):
+        corner_ref[pl.ds(s.layers * s.packs * size + i * s.wind_rows, s.wind_rows), :] = part
+
+
+def coefficients(store, wind_x, wind_y):
+    for stage, factor in enumerate(STAGE_FACTORS):
+        values = (0.1 - 0.5 * wind_x, 0.1 + 0.5 * wind_x, 0.1 - 0.5 * wind_y, 0.1 + 0.5 * wind_y)
+        for kind, value in enumerate(values):
+            store(stage * 4 + kind, value * factor)
+
+
+def stages(s, field, row_of, shape):
+    current = field
+    for stage, factor in enumerate(STAGE_FACTORS):
+        low, high = stage + 1, 3 * HALO - 1 - stage
+        following = {}
+        for j in range(low, high):
+            if stage == len(STAGE_FACTORS) - 1 and not HALO <= j < 2 * HALO:
+                continue
+            for layer in range(s.layers):
+                centre = current[layer, j]
+                others = sum(current[k, j] for k in range(s.layers) if k != layer)
+                north, south, east, west = (row_of(stage * 4 + kind, layer, j, shape) for kind in range(4))
+                share = 0.2 / s.layers
+                total = north * current[layer, j + 1] + south * current[layer, j - 1]
+                total = total + east * lane_roll(centre, -1) + west * lane_roll(centre, 1)
+                total = total + (factor * (share - 0.6)) * centre + (factor * share) * others
+                following[layer, j] = field[layer, j] + total
+        current = following
+    return current
+
+
+def forecast_kernel(
+    s, own_ref, sib_ref, wind_ref, wind_strip_ref, strip_ref, halo_ref, side_ref, corner_ref,
+    out0_ref, out1_ref, out2_ref, out3_ref,
+    wide_ref, cut_ref, main_coef_ref, strip_coef_ref, halo32_ref, halo_strip_ref, edge_ref,
+):
+    mem = lax.axis_index("mem")
+    odd = lax.rem(mem, 2)
+    place = (mem // 2) * 2 + lax.axis_index("gy")
+    size = OCTET
+    span = 16
+
+    def three(ref, base, rows):
+        return sum(ref[pl.ds(base + i * rows, rows), :].astype(jnp.float32) for i in range(3))
+
+    near = three(halo_ref, s.halo_rows, s.wind_rows)
+    corner = three(corner_ref, s.layers * s.packs * size, s.wind_rows)
+    near_strip = with_edges(to_strip(lambda q: near), corner, 0)
+    base = s.layers * 2 * s.packs * size
+    wide_ref[...] = jnp.zeros_like(wide_ref)
+    cut_ref[...] = jnp.zeros_like(cut_ref)
+    for block in range(2 * s.layers):
+        at = block * span
+        wide_ref[pl.ds(at, HALO), :] = near[block * HALO : (block + 1) * HALO]
+        cut_ref[pl.ds(at, HALO), :] = near_strip[block * HALO : (block + 1) * HALO]
+        for j in range(HALO, 3 * HALO):
+            row = block * s.rows + tile_row(odd, j)
+            wide_ref[pl.ds(at + j, 1), :] = wind_ref[pl.ds(row, 1), :]
+            cut_ref[pl.ds(at + j, 1), :] = with_edges(
+                wind_strip_ref[pl.ds(row, 1), :], side_ref[pl.ds(base + row, 1), :], 0
+            )
+    sign = jnp.where(odd == 1, -1.0, 1.0)
+    half = s.layers * span
+    for from_ref, to_ref in ((wide_ref, main_coef_ref), (cut_ref, strip_coef_ref)):
+        def store(index, value):
+            to_ref[pl.ds(index * half, half), :] = value
+
+        coefficients(store, sign * from_ref[pl.ds(0, half), :], from_ref[pl.ds(half, half), :])
+
+    for layer in range(s.layers):
+        for j in range(HALO):
+            at = (layer * (HALO + 1) + HALO - j) * s.members
+            value = halo_ref[pl.ds(at, s.members), :].astype(jnp.float32)
+            if j == HALO - 1:
+                value = value + halo_ref[pl.ds(layer * (HALO + 1) * s.members, s.members), :].astype(jnp.float32)
+            halo32_ref[pl.ds((layer * HALO + j) * s.members, s.members), :] = value
+
+    def row_from(ref):
+        def row_of(index, layer, j, shape):
+            return jnp.broadcast_to(ref[pl.ds(index * half + layer * span + j, 1), :], shape)
+
+        return row_of
+
+    def halo_octet(layer, j, octet):
+        return halo32_ref[pl.ds((layer * HALO + j) * s.members + octet * size, size), :]
+
+    shape = (size, LANES)
+    for layer in range(s.layers):
+        for p in range(s.packs):
+            edges = corner_ref[pl.ds((layer * s.packs + p) * size, size), :].astype(jnp.float32)
+            for j in range(HALO):
+                strip = with_edges(to_strip(lambda q: halo_octet(layer, j, PACK * p + q)), edges, j)
+                halo_strip_ref[pl.ds(((layer * HALO + j) * s.packs + p) * size, size), :] = strip
+
+    def strip_step(p, carry):
+        field = {}
+        for layer in range(s.layers):
+            for j in range(HALO):
+                at = pl.multiple_of(((layer * HALO + j) * s.packs + p) * size, size)
+                field[layer, j] = halo_strip_ref[pl.ds(at, size), :]
+            for block in range(2):
+                at = pl.multiple_of(((layer * 2 + block) * s.packs + p) * size, size)
+                edges = side_ref[pl.ds(at, size), :]
+                for k in range(HALO):
+                    j = HALO + block * HALO + k
+                    at = pl.multiple_of(((layer * 2 * HALO + j - HALO) * s.packs + p) * size, size)
+                    field[layer, j] = with_edges(strip_ref[pl.ds(at, size), :], edges, k)
+        result = stages(s, field, row_from(strip_coef_ref), shape)
+        for layer in range(s.layers):
+            for t in range(HALO):
+                at = pl.multiple_of(((layer * HALO + t) * s.packs + p) * size, size)
+                edge_ref[pl.ds(at, size), :] = result[layer, HALO + t]
+        return carry
+
+    lax.fori_loop(0, s.packs, strip_step, 0)
+
+    swap_one = jnp.bitwise_and(place, 1) == 1
+    swap_two = place >= 2
+    lane = lane_iota(shape)
+    outs = (out0_ref, out1_ref, out2_ref, out3_ref)
+
+    def octet_result(ref, within, octet, q):
+        field = {}
+        for layer in range(s.layers):
+            for j in range(HALO):
+                at = pl.multiple_of((layer * HALO + j) * s.members + octet * size, size)
+                field[layer, j] = halo32_ref[pl.ds(at, size), :]
+            for j in range(HALO, 3 * HALO):
+                start = within * size * s.per_member + layer * s.rows + tile_row(odd, j)
+                field[layer, j] = ref[pl.ds(start, size, stride=s.per_member), :]
+        result = stages(s, field, row_from(main_coef_ref), shape)
+        for layer in range(s.layers):
+            for t in range(HALO):
+                at = pl.multiple_of(((layer * HALO + t) * s.packs + octet // PACK) * size, size)
+                edge = edge_ref[pl.ds(at, size), :]
+                first = lane_roll(edge, -(GROUP * q + HALO))
+                last = lane_roll(edge, LANES - HALO - 24 - GROUP * q)
+                value = jnp.where(lane < HALO, first, result[layer, HALO + t])
+                result[layer, HALO + t] = jnp.where(lane >= LANES - HALO, last, value)
+        return result
+
+    half_packs = s.packs // 2
+    for which, ref in enumerate((own_ref, sib_ref)):
+        def main_step(i, carry):
+            for pair in range(PACK // 2):
+                parts = []
+                for k in range(2):
+                    q = 2 * pair + k
+                    within = i * PACK + q
+                    octet = (which * half_packs + i) * PACK + q
+                    parts.append(octet_result(ref, within, octet, q))
+                at = pl.multiple_of(((which * half_packs + i) * PACK + 2 * pair) * size, 2 * size)
+                for layer in range(s.layers):
+                    rows = [
+                        jnp.concatenate([part[layer, HALO + t] for part in parts], axis=0).astype(jnp.bfloat16)
+                        for t in range(HALO)
+                    ]
+                    rows = [jnp.where(swap_one, rows[t ^ 1], rows[t]) for t in range(HALO)]
+                    rows = [jnp.where(swap_two, rows[t ^ 2], rows[t]) for t in range(HALO)]
+                    for d, out_ref in enumerate(outs):
+                        out_ref[layer, pl.ds(at, 2 * size), :] = rows[d]
+            return carry
+
+        lax.fori_loop(0, half_packs, main_step, 0)
+
+
+def dot(a, b, contract):
+    return lax.dot_general(a, b, ((contract[0], contract[1]), ((), ())), preferred_element_type=jnp.float32)
+
+
+def dot_three(a, b, contract=((1,), (0,))):
+    (a_high, a_low), (b_high, b_low) = a, b
+    return dot(a_high, b_low, contract) + dot(a_low, b_high, contract) + dot(a_high, b_high, contract)
+
+
+def analysis_kernel(s, total_members, piece0_ref, piece1_ref, piece2_ref, piece3_ref, obs_ref, out_ref):
+    mem, side = lax.axis_index("mem"), lax.axis_index("gy")
+    me = mem * 2 + side
+    pieces = (piece0_ref, piece1_ref, piece2_ref, piece3_ref)
+    width = 2 * LANES
+    cells_total = s.layers * width
+    inverse = 1.0 / total_members
+    members = jnp.concatenate(
+        [
+            jnp.concatenate([pieces[2 * dx + dy][layer] for layer in range(s.layers) for dy in range(2)], axis=1)
+            for dx in range(2)
+        ],
+        axis=0,
+    )
+    ones = jnp.ones((OCTET, total_members), jnp.bfloat16)
+    mean = dot(ones, members, ((1,), (0,)))[0:1] * inverse
+    perturbation = (members.astype(jnp.float32) - mean).astype(jnp.bfloat16)
+
+    cells = obs_ref[0:1, :].astype(jnp.int32)
+    values, errors = obs_ref[1:2, :], obs_ref[2:3, :]
+    column = jnp.bitwise_and(cells, width - 1)
+    layer_of = cells // width
+    half = jnp.bitwise_xor(column // LANES, side)
+    index = layer_of * width + half * LANES + jnp.bitwise_and(column, LANES - 1)
+    chosen = lax.broadcasted_iota(jnp.int32, (cells_total, cells.shape[1]), 0) == index
+    picked = dot(members, chosen.astype(jnp.bfloat16), ((1,), (0,)))
+    base = jnp.sum(picked, axis=0, keepdims=True) * inverse
+    offset = column.astype(jnp.float32) - 0.5 * (width - 1)
+    weight = jnp.zeros_like(values)
+    for shift in (-1, 0, 1):
+        distance = (shift * width + offset) / width
+        weight = weight + jnp.exp(-0.5 * distance * distance) / errors
+    scale = jnp.sqrt(weight)
+    scaled = (picked - base) * scale
+    innovation = (values - base) * scale
+    parts = split_two(scaled)
+    size = (total_members, total_members)
+    diagonal = lax.broadcasted_iota(jnp.int32, size, 0) == lax.broadcasted_iota(jnp.int32, size, 1)
+    identity = jnp.where(diagonal, 1.0, 0.0)
+    gram = dot_three(parts, parts, ((1,), (1,))) + (total_members - 1.0) * identity
+    square = jnp.sum(jnp.sum(gram * gram, axis=0, keepdims=True), axis=1, keepdims=True)
+    frob = jnp.sqrt(square)
+    current = gram / frob
+    middle = 1.5 * identity - 0.5 * current
+    root = middle
+    for step in range(1, ROOT_STEPS):
+        middle_parts = split_two(middle)
+        current = dot_three(split_two(current), middle_parts)
+        root_parts = split_two(root)
+        middle = 1.5 * identity - 0.5 * dot_three(root_parts, split_two(current))
+        root = dot_three(split_two(middle), root_parts)
+    projected = jnp.sum(scaled * innovation, axis=1, keepdims=True)
+    once = jnp.sum(root * projected, axis=0, keepdims=True)
+    twice = jnp.sum(root * once, axis=1, keepdims=True)
+    mean_weights = jnp.sum(jnp.where(diagonal, twice, 0.0), axis=0, keepdims=True) / frob
+    weights = (math.sqrt(total_members - 1.0) * root / jnp.sqrt(frob) + mean_weights).astype(jnp.bfloat16)
+    for dx in range(2):
+        for part in range(2):
+            rows = slice((2 * dx + part) * s.local, (2 * dx + part + 1) * s.local)
+            block = dot(weights[rows], perturbation, ((1,), (0,))) + mean
+            block = block.astype(jnp.bfloat16)
+            for dy in range(2):
+                target = jnp.bitwise_xor(me, dx * 4 + part * 2 + dy)
+                for layer in range(s.layers):
+                    at = (layer * 2 + dy) * LANES
+                    out_ref[target, layer] = block[:, at : at + LANES]
+
+
+def place_rows_kernel(s, in_ref, out_ref, rows_ref):
+    for source in range(8):
+        x, c, y = source // 4, (source // 2) % 2, source % 2
+        t = 2 * x + y
+        row = t if c == 0 else 7 - t
+        for layer in range(s.layers):
+            for octet in range(0, s.local // OCTET, 2):
+                value = in_ref[source, layer, octet * OCTET : (octet + 2) * OCTET, :].astype(jnp.float32)
+                start = octet * OCTET * s.per_member + layer * s.rows + row
+                rows_ref[pl.ds(start, 2 * OCTET, stride=s.per_member), :] = value
+    out_ref[...] = rows_ref[...].astype(jnp.bfloat16).reshape(out_ref.shape)
+
+
+def vmem_call(kernel, outs, scratch, *args):
+    spec = pl.BlockSpec(memory_space=pltpu.VMEM)
+    return pl.pallas_call(
+        kernel,
+        out_shape=outs,
+        in_specs=[spec] * len(args),
+        out_specs=jax.tree.map(lambda _: spec, outs),
+        scratch_shapes=[pltpu.VMEM(shape, dtype) for shape, dtype in scratch],
+    )(*args)
+
+
+def on_device_tile(prior_sample_set, flow_speeds, observed_cells, observed_values, error_variance):
+    local, layers, rows, columns = prior_sample_set.shape
+    s = Sizes(local, layers, rows)
+    n_gx = lax.axis_size("gx")
+    f32, bf16 = jnp.float32, jnp.bfloat16
+    shaped = jax.ShapeDtypeStruct
+    size = OCTET
+
+    pair = [(m, m ^ 1) for m in range(4)]
+    def step(m):
+        return 1 if m % 2 == 0 else n_gx - 1
+    along = [(m * n_gx + z, m * n_gx + (z + step(m)) % n_gx) for m in range(4) for z in range(n_gx)]
+    across = [(0, 1), (1, 0)]
+    diagonal = [
+        ((m * n_gx + z) * 2 + y, (m * n_gx + (z + step(m)) % n_gx) * 2 + 1 - y)
+        for m in range(4) for z in range(n_gx) for y in range(2)
+    ]
+    owners = []
+    for x in range(2):
+        for c in range(2):
+            for y in range(2):
+                source = (x, y, 0) if c == 0 else (1 - x, 1 - y, 1)
+                owners.append(((source[0] * 2 + source[1]) * 2 + source[2], (x * 2 + c) * 2 + y))
+
+    own = prior_sample_set.reshape(local * layers * rows, columns)
+    sib = lax.ppermute(prior_sample_set, "mem", pair).reshape(own.shape)
+    wind = flow_speeds.reshape(2 * layers * rows, columns)
+
+    halo_out = vmem_call(
+        functools.partial(pack_halo_kernel, s),
+        shaped((s.halo_rows + 3 * s.wind_rows, LANES), bf16),
+        [((s.wind_rows, LANES), f32)],
+        own, sib, wind,
+    )
+    halo = lax.ppermute(halo_out, ("mem", "gx"), along)
+    side_rows = layers * 2 * s.packs * size + 2 * layers * rows
+    corner_rows = layers * s.packs * size + 3 * s.wind_rows
+    strips, side_out, corner_out, wind_strip = vmem_call(
+        functools.partial(pack_edges_kernel, s),
+        (
+            shaped((layers * 2 * HALO * s.packs * size, LANES), f32),
+            shaped((side_rows, LANES), f32),
+            shaped((corner_rows, LANES), bf16),
+            shaped((2 * layers * rows, LANES), f32),
+        ),
+        [((s.wind_rows, LANES), f32)],
+        own, sib, wind,
+    )
+    side = lax.ppermute(side_out, "gy", across)
+    corner = lax.ppermute(corner_out, ("mem", "gx", "gy"), diagonal)
+
+    count = observed_cells.shape[-1]
+    obs = jnp.stack(
+        [observed_cells.reshape(count).astype(f32), observed_values.reshape(count), error_variance.reshape(count)]
+    )
+    obs = lax.ppermute(obs, ("mem", "gy"), owners)
+
+    span = 16
+    coef_rows = 16 * layers * span
+    piece = shaped((layers, s.members, LANES), bf16)
+    pieces = vmem_call(
+        functools.partial(forecast_kernel, s),
+        (piece, piece, piece, piece),
+        [
+            ((2 * layers * span, LANES), f32),
+            ((2 * layers * span, LANES), f32),
+            ((coef_rows, LANES), f32),
+            ((coef_rows, LANES), f32),
+            ((layers * HALO * s.members, LANES), f32),
+            ((layers * HALO * s.packs * size, LANES), f32),
+            ((layers * HALO * s.packs * size, LANES), f32),
+        ],
+        own, sib, wind, wind_strip, strips, halo, side, corner,
+    )
+
+    def flip(dx, dy):
+        return [((m * 2 + y), ((m ^ (2 * dx)) * 2 + (y ^ dy))) for m in range(4) for y in range(2)]
+
+    arrived = [
+        pieces[0],
+        lax.ppermute(pieces[1], ("mem", "gy"), flip(0, 1)),
+        lax.ppermute(pieces[2], ("mem", "gy"), flip(1, 0)),
+        lax.ppermute(pieces[3], ("mem", "gy"), flip(1, 1)),
+    ]
+    outgoing = vmem_call(
+        functools.partial(analysis_kernel, s, 4 * local),
+        shaped((8, layers, local, LANES), bf16),
+        [],
+        *arrived, obs,
+    )
+    returned = lax.all_to_all(outgoing, ("mem", "gy"), split_axis=0, concat_axis=0, tiled=True)
+    return vmem_call(
+        functools.partial(place_rows_kernel, s),
+        shaped((local, layers, rows, columns), bf16),
+        [((local * layers * rows, LANES), f32)],
+        returned,
+    )
+
+
+def on_device(prior_sample_set, flow_speeds, observed_cells, observed_values, error_variance):
+    local, layers, rows, columns = prior_sample_set.shape
+    suits = (
+        lax.axis_size("mem") == 4
+        and lax.axis_size("gy") == 2
+        and rows == 2 * HALO
+        and columns == LANES
+        and observed_cells.shape[-2] == 1
+        and local % (OCTET * PACK) == 0
+    )
+    form = on_device_tile if suits else on_device_general
+    return form(prior_sample_set, flow_speeds, observed_cells, observed_values, error_variance)
+
+
 def solution(mesh):
     in_specs = (
         P("mem", None, "gx", "gy"),

time: 75 us -> 57.2 us (0.76)
  Pallas kernels: 0 us -> 23.3 us
  other arithmetic: 11.9 us -> 0.01 us
  local copies, waits for them, and re-layouts: 13.5 us -> 2.86 us
  matrix products: 6.68 us -> 0 us
  waiting for transfers between devices: 15.9 us -> 9.38 us
  starting transfers between devices: 16.8 us -> 10.6 us
  blocking collectives: 8.54 us -> 10.6 us
  between operations: 1.24 us -> 0.07 us
    pallas_call x0 -> x5, Pallas kernels: none -> 23.3 us  [vmem_call(): pl.pallas_call(kernel, out_shape=outs, in_specs=[spec] * len(args), out_s...]
    dot_general x16 -> x0, matrix products: 6.68 us -> none  [the longest x4 1.46 us: analyze(): jnp.einsum('pab,pbc->pac', root, current, precision=highest)]
    add x3 -> x0, other arithmetic: 5.83 us -> none  [the longest x1 2.09 us: deep_step(): crop_margin(padded, 2) + 0.5 * section_two]
    all_to_all x1 -> x0, waiting for transfers between devices: 5.71 us -> none  [on_device(): lax.all_to_all(flattened_realizations, ('mem', 'gy'), split_axis=0, conca...]
    slice x8 -> x0, local copies, waits for them, and re-layouts: 5.57 us -> none  [the longest x4 3.86 us: with_halo(): lax.slice_in_dim(block, block.shape[dim] - width, None, axis=dim)]
    all_to_all x1 -> x0, starting transfers between devices: 3.59 us -> none  [on_device(): lax.all_to_all(flattened_realizations, ('mem', 'gy'), split_axis=0, conca...]
    ppermute x8, starting transfers between devices: 13.2 us -> 10.6 us  [the longest x1 2.93 us: on_device_tile(): halo = lax.ppermute(halo_out, ('mem', 'gx'), along)]
    unnamed x14 -> x22, local copies, waits for them, and re-layouts: 0.3 us -> 2.86 us
  transfers between devices with their start and end apart: 9 -> 8, of which waited for: 7 -> 5; matrix products, arithmetic and copies ran while one was open for 4% -> 0% of each run, Pallas kernels for 0% -> 11%
where the time goes in v1:
time: 57.2 us; the launch traced here: 56.8 us
  Pallas kernels  23.3 us (41%)
  starting transfers between devices  10.6 us (19%)
  blocking collectives  10.6 us (19%)
  waiting for transfers between devices  9.38 us (16%)
  local copies, waits for them, and re-layouts  2.86 us (5%)
    pallas_call x5, Pallas kernels, vmem_call(): pl.pallas_call(kernel, out_shape=outs, in_specs=[spec] * len(args), out_s...  23.3 us
    all_to_all x1, blocking collectives, on_device_tile(): lax.all_to_all(outgoing, ('mem', 'gy'), split_axis=0, concat_axis=0, tile...  10.6 us
    ppermute x1, waiting for transfers between devices, on_device_tile(): corner = lax.ppermute(corner_out, ('mem', 'gx', 'gy'), diagonal)  3.73 us
    ppermute x1, starting transfers between devices, on_device_tile(): halo = lax.ppermute(halo_out, ('mem', 'gx'), along)  2.93 us
    unnamed x22, local copies, waits for them, and re-layouts  2.86 us
    ppermute x1, starting transfers between devices, on_device_tile(): corner = lax.ppermute(corner_out, ('mem', 'gx', 'gy'), diagonal)  2.53 us
    ppermute x1, waiting for transfers between devices, on_device_tile(): lax.ppermute(pieces[3], ('mem', 'gy'), flip(1, 1))  2.39 us
    ppermute x1, waiting for transfers between devices, on_device_tile(): sib = lax.ppermute(prior_sample_set, 'mem', pair).reshape(own.shape)  1.75 us
  transfers between devices with their start and end apart: 8, of which 5 were waited for; matrix products, arithmetic and copies ran while one was open for 0% of the time, Pallas kernels for 11%

profile of v1, /device:TPU:0, one launch (start us, length us, event | category | flops | bytes accessed | tf_op | source)
XLA Modules:
  0.0 56.8 jit_solution(15727037588350358050)
XLA Ops:
  0.0 0.5 collective-permute-start
  0.5 1.7 %collective-permute-done = f32[64,2,8,128]{3,2,1,0:T(8,128)S(1)} collective-permute-done((f32[64,2,8,128]{3,2,1,0:T(8,128)}, f32[64,2,8,128]{3,2,1,0:T(8,128)S(1)}, u32[]{:S(2)}, u32[]{:S(2)}) %collective-permute-start) | collective-permute-done | bytes 524320 | tf_op jit(solution)/shard_map/ppermute | solution.py:639
  2.2 0.8 %copy-done = f32[64,2,8,128]{3,2,1,0:T(8,128)} copy-done((f32[64,2,8,128]{3,2,1,0:T(8,128)}, f32[64,2,8,128]{3,2,1,0:T(8,128)S(1)}, u32[]{:S(2)}) %copy-start) | copy-done | bytes 524312
  3.0 2.2 %shard_map.56 = bf16[1328,128]{1,0:T(8,128)(2,1)} custom-call(f32[1024,128]{1,0:T(8,128)} %bitcast.7, f32[1024,128]{1,0:T(8,128)} %bitcast.10, f32[32,128]{1,0:T(8,128)} %bitcast.13), custom_call_target="tpu_custom_call" | custom-call | tf_op jit(solution)/shard_map/pallas_call | solution.py:605
  5.3 2.9 %collective-permute-start.1 = (bf16[1328,128]{1,0:T(8,128)(2,1)}, bf16[1328,128]{1,0:T(8,128)(2,1)S(1)}, u32[]{:S(2)}, u32[]{:S(2)}) collective-permute-start(bf16[1328,128]{1,0:T(8,128)(2,1)} %shard_map.56), channel_id=1, source_target_pairs={{0,2},{2,4},{4,6},{6,0},{8,14},{10,8},{12,10},{14,12},{16,18},{18,... | collective-permute-start | bytes 1019912 | tf_op jit(solution)/shard_map/ppermute | solution.py:648
  8.2 6.1 %shard_map.55 = (f32[512,128]{1,0:T(8,128)}, f32[160,128]{1,0:T(8,128)}, bf16[112,128]{1,0:T(8,128)(2,1)}, f32[32,128]{1,0:T(8,128)}) custom-call(f32[1024,128]{1,0:T(8,128)} %bitcast.8, f32[1024,128]{1,0:T(8,128)} %bitcast.11, f32[32,128]{1,0:T(8,128)} %bitcast.14), custom_call_target="tpu_custom_call" | custom-call | tf_op jit(solution)/shard_map/pallas_call | solution.py:605
  14.2 2.5 %collective-permute-start.3 = (bf16[112,128]{1,0:T(8,128)(2,1)}, bf16[112,128]{1,0:T(8,128)(2,1)S(1)}, u32[]{:S(2)}, u32[]{:S(2)}) collective-permute-start(bf16[112,128]{1,0:T(8,128)(2,1)} %get-tuple-element.16), channel_id=1, source_target_pairs={{0,3},{1,2},{2,5},{3,4},{4,7},{5,6},{6,1},{7,0},{8,15},{9,14},{10,... | collective-permute-start | bytes 86024 | tf_op jit(solution)/shard_map/ppermute | solution.py:663
  16.8 0.5 collective-permute-start.2
  17.3 0.0 copy-done.10
  17.3 3.7 %collective-permute-done.3.corner_ref = bf16[112,128]{1,0:T(8,128)(2,1)S(1)} collective-permute-done((bf16[112,128]{1,0:T(8,128)(2,1)}, bf16[112,128]{1,0:T(8,128)(2,1)S(1)}, u32[]{:S(2)}, u32[]{:S(2)}) %collective-permute-start.3) | collective-permute-done | bytes 28704 | tf_op jit(solution)/shard_map/ppermute | solution.py:663
  21.0 1.4 %collective-permute-done.2.side_ref = f32[160,128]{1,0:T(8,128)S(1)} collective-permute-done((f32[160,128]{1,0:T(8,128)}, f32[160,128]{1,0:T(8,128)S(1)}, u32[]{:S(2)}, u32[]{:S(2)}) %collective-permute-start.2) | collective-permute-done | bytes 81952 | tf_op jit(solution)/shard_map/ppermute | solution.py:662
  22.4 0.0 collective-permute-done.1.halo_ref
  22.4 0.0 copy-done.6
  22.4 0.6 %copy-done.2 = f32[160,128]{1,0:T(8,128)} copy-done((f32[160,128]{1,0:T(8,128)}, f32[160,128]{1,0:T(8,128)S(1)}, u32[]{:S(2)}) %copy-start.2) | copy-done | bytes 81944
  23.0 0.1 copy-done.1
  23.2 8.1 %shard_map.57 = (bf16[2,128,128]{2,1,0:T(8,128)(2,1)}, bf16[2,128,128]{2,1,0:T(8,128)(2,1)}, bf16[2,128,128]{2,1,0:T(8,128)(2,1)}, bf16[2,128,128]{2,1,0:T(8,128)(2,1)}) custom-call(f32[1024,128]{1,0:T(8,128)} %bitcast.9, f32[1024,128]{1,0:T(8,128)} %bitcast.12, f32[32,128]{1,0:T(8,128)} %bitcast.15, f32[32,128]{1,0:T(8,128)} %get-tuple-element.13.wind_strip_ref, ...), custom_call_target="tpu_custom_call" | custom-call | tf_op jit(solution)/shard_map/pallas_call | solution.py:605
  31.2 0.5 collective-permute-start.4
  31.8 1.5 %collective-permute-start.5 = (bf16[2,128,128]{2,1,0:T(8,128)(2,1)}, bf16[2,128,128]{2,1,0:T(8,128)(2,1)S(1)}, u32[]{:S(2)}, u32[]{:S(2)}) collective-permute-start(bf16[2,128,128]{2,1,0:T(8,128)(2,1)} %get-tuple-element.19), channel_id=1, source_target_pairs={{0,16},{1,17},{8,24},{9,25},{16,0},{17,1},{24,8},{25,9},{2,18},{3,... | collective-permute-start | bytes 196616 | tf_op jit(solution)/shard_map/ppermute | solution.py:695
  33.3 1.5 %collective-permute-start.6 = (bf16[2,128,128]{2,1,0:T(8,128)(2,1)}, bf16[2,128,128]{2,1,0:T(8,128)(2,1)S(1)}, u32[]{:S(2)}, u32[]{:S(2)}) collective-permute-start(bf16[2,128,128]{2,1,0:T(8,128)(2,1)} %get-tuple-element.20), channel_id=1, source_target_pairs={{0,17},{1,16},{8,25},{9,24},{16,1},{17,0},{24,9},{25,8},{2,19},{3,... | collective-permute-start | bytes 196616 | tf_op jit(solution)/shard_map/ppermute | solution.py:696
  34.7 0.7 %copy-done.8 = f32[1,1,1,1,128]{4,3,2,1,0:T(1,128)S(1)} copy-done((f32[1,1,1,1,128]{4,3,2,1,0:T(1,128)S(1)}, f32[1,1,1,1,128]{4,3,2,1,0:T(1,128)}, u32[]{:S(2)}) %copy-start.8) | copy-done | bytes 536
  35.4 0.0 copy-done.9
  35.4 0.7 %collective-permute-start.7 = (f32[3,128]{1,0:T(4,128)S(1)}, f32[3,128]{1,0:T(4,128)S(1)}, u32[]{:S(2)}, u32[]{:S(2)}) collective-permute-start(f32[3,128]{1,0:T(4,128)S(1)} %pad_maximum_fusion), channel_id=1, source_target_pairs={{0,0},{8,1},{25,8},{17,9},{16,16},{24,17},{9,24},{1,25},{2,2},{10,... | collective-permute-start | bytes 4616 | tf_op jit(solution)/shard_map/ppermute | solution.py:669
  36.1 0.0 collective-permute-done.7.obs_ref
  36.1 0.0 copy-start.7
  36.1 0.0 collective-permute-done.4.piece1_ref
  36.1 0.1 collective-permute-done.5.piece2_ref
  36.2 2.4 %collective-permute-done.6.piece3_ref = bf16[2,128,128]{2,1,0:T(8,128)(2,1)S(1)} collective-permute-done((bf16[2,128,128]{2,1,0:T(8,128)(2,1)}, bf16[2,128,128]{2,1,0:T(8,128)(2,1)S(1)}, u32[]{:S(2)}, u32[]{:S(2)}) %collective-permute-start.6) | collective-permute-done | bytes 65568 | tf_op jit(solution)/shard_map/ppermute | solution.py:696
  38.6 0.0 copy-done.3
  38.6 0.6 %copy-done.5 = bf16[2,128,128]{2,1,0:T(8,128)(2,1)} copy-done((bf16[2,128,128]{2,1,0:T(8,128)(2,1)}, bf16[2,128,128]{2,1,0:T(8,128)(2,1)S(1)}, u32[]{:S(2)}) %copy-start.5) | copy-done | bytes 65560
  39.3 5.0 %shard_map.58 = bf16[8,2,64,128]{3,2,1,0:T(8,128)(2,1)} custom-call(bf16[2,128,128]{2,1,0:T(8,128)(2,1)} %get-tuple-element.17.piece0_ref, bf16[2,128,128]{2,1,0:T(8,128)(2,1)} %copy-done.3, bf16[2,128,128]{2,1,0:T(8,128)(2,1)} %copy-done.4, bf16[2,128,128]{2,1,0:T(8,128)(2,1)} %copy-done.5, f32[3,128]{1,0:T(4,128)} %copy-done.7), custom_call_target="tpu_custom_call" | custom-call | tf_op jit(solution)/shard_map/pallas_call | solution.py:605
  44.3 10.6 %all_to_all.5.in_ref = bf16[8,2,64,128]{3,2,1,0:T(8,128)(2,1)} all-to-all(bf16[8,2,64,128]{3,2,1,0:T(8,128)(2,1)} %shard_map.58), channel_id=1, replica_groups=mesh['mem'=4,'gx'=4,'gy'=2] {'mem','gy'}, dimensions={0} | all-to-all | bytes 524288 | tf_op jit(solution)/shard_map/all_to_all | solution.py:704
  54.9 1.9 %shard_map.59 = bf16[64,2,8,128]{3,2,1,0:T(8,128)(2,1)} custom-call(bf16[8,2,64,128]{3,2,1,0:T(8,128)(2,1)} %all_to_all.5.in_ref), custom_call_target="tpu_custom_call" | custom-call | tf_op jit(solution)/shard_map/pallas_call | solution.py:605
  (14 shorter events, 0.0 us)
Async XLA Ops:
  0.0 2.2 %collective-permute-start = (f32[64,2,8,128]{3,2,1,0:T(8,128)}, f32[64,2,8,128]{3,2,1,0:T(8,128)S(1)}, u32[]{:S(2)}, u32[]{:S(2)}) collective-permute-start(f32[64,2,8,128]{3,2,1,0:T(8,128)} %param.5), channel_id=1, source_target_pairs={{0,8},{8,0},{16,24},{24,16},{1,9},{9,1},{17,25},{25,17},{2,10},{10... | collective-permute-start | bytes 1572872 | tf_op jit(solution)/shard_map/ppermute | solution.py:639
  2.2 0.8 %copy-start = (f32[64,2,8,128]{3,2,1,0:T(8,128)}, f32[64,2,8,128]{3,2,1,0:T(8,128)S(1)}, u32[]{:S(2)}) copy-start(f32[64,2,8,128]{3,2,1,0:T(8,128)S(1)} %collective-permute-done) | copy-start | bytes 1572868
  5.3 17.2 %collective-permute-start.1 = (bf16[1328,128]{1,0:T(8,128)(2,1)}, bf16[1328,128]{1,0:T(8,128)(2,1)S(1)}, u32[]{:S(2)}, u32[]{:S(2)}) collective-permute-start(bf16[1328,128]{1,0:T(8,128)(2,1)} %shard_map.56), channel_id=1, source_target_pairs={{0,2},{2,4},{4,6},{6,0},{8,14},{10,8},{12,10},{14,12},{16,18},{18,... | collective-permute-start | bytes 1019912 | tf_op jit(solution)/shard_map/ppermute | solution.py:648
  14.2 3.0 %copy-start.10 = (s32[1,1,1,1,128]{4,3,2,1,0:T(1,128)S(1)}, s32[1,1,1,1,128]{4,3,2,1,0:T(1,128)}, u32[]{:S(2)}) copy-start(s32[1,1,1,1,128]{4,3,2,1,0:T(1,128)} %param.7) | copy-start | bytes 1540
  14.2 6.8 %collective-permute-start.3 = (bf16[112,128]{1,0:T(8,128)(2,1)}, bf16[112,128]{1,0:T(8,128)(2,1)S(1)}, u32[]{:S(2)}, u32[]{:S(2)}) collective-permute-start(bf16[112,128]{1,0:T(8,128)(2,1)} %get-tuple-element.16), channel_id=1, source_target_pairs={{0,3},{1,2},{2,5},{3,4},{4,7},{5,6},{6,1},{7,0},{8,15},{9,14},{10,... | collective-permute-start | bytes 86024 | tf_op jit(solution)/shard_map/ppermute | solution.py:663
  16.8 5.6 %collective-permute-start.2 = (f32[160,128]{1,0:T(8,128)}, f32[160,128]{1,0:T(8,128)S(1)}, u32[]{:S(2)}, u32[]{:S(2)}) collective-permute-start(f32[160,128]{1,0:T(8,128)} %get-tuple-element.15), channel_id=1, source_target_pairs={{0,1},{1,0},{2,3},{3,2},{4,5},{5,4},{6,7},{7,6},{8,9},{9,8},{10,11... | collective-permute-start | bytes 245768 | tf_op jit(solution)/shard_map/ppermute | solution.py:662
  21.0 1.4 %copy-start.6 = (bf16[112,128]{1,0:T(8,128)(2,1)}, bf16[112,128]{1,0:T(8,128)(2,1)S(1)}, u32[]{:S(2)}) copy-start(bf16[112,128]{1,0:T(8,128)(2,1)S(1)} %collective-permute-done.3.corner_ref) | copy-start | bytes 86020
  22.4 0.6 %copy-start.2 = (f32[160,128]{1,0:T(8,128)}, f32[160,128]{1,0:T(8,128)S(1)}, u32[]{:S(2)}) copy-start(f32[160,128]{1,0:T(8,128)S(1)} %collective-permute-done.2.side_ref) | copy-start | bytes 245764
  22.4 0.8 %copy-start.1 = (bf16[1328,128]{1,0:T(8,128)(2,1)}, bf16[1328,128]{1,0:T(8,128)(2,1)S(1)}, u32[]{:S(2)}) copy-start(bf16[1328,128]{1,0:T(8,128)(2,1)S(1)} %collective-permute-done.1.halo_ref) | copy-start | bytes 1019908
  31.2 4.9 %collective-permute-start.4 = (bf16[2,128,128]{2,1,0:T(8,128)(2,1)}, bf16[2,128,128]{2,1,0:T(8,128)(2,1)S(1)}, u32[]{:S(2)}, u32[]{:S(2)}) collective-permute-start(bf16[2,128,128]{2,1,0:T(8,128)(2,1)} %get-tuple-element.18), channel_id=1, source_target_pairs={{0,1},{1,0},{8,9},{9,8},{16,17},{17,16},{24,25},{25,24},{2,3},{3,2... | collective-permute-start | bytes 196616 | tf_op jit(solution)/shard_map/ppermute | solution.py:694
  31.8 4.5 %collective-permute-start.5 = (bf16[2,128,128]{2,1,0:T(8,128)(2,1)}, bf16[2,128,128]{2,1,0:T(8,128)(2,1)S(1)}, u32[]{:S(2)}, u32[]{:S(2)}) collective-permute-start(bf16[2,128,128]{2,1,0:T(8,128)(2,1)} %get-tuple-element.19), channel_id=1, source_target_pairs={{0,16},{1,17},{8,24},{9,25},{16,0},{17,1},{24,8},{25,9},{2,18},{3,... | collective-permute-start | bytes 196616 | tf_op jit(solution)/shard_map/ppermute | solution.py:695
  33.3 5.4 %collective-permute-start.6 = (bf16[2,128,128]{2,1,0:T(8,128)(2,1)}, bf16[2,128,128]{2,1,0:T(8,128)(2,1)S(1)}, u32[]{:S(2)}, u32[]{:S(2)}) collective-permute-start(bf16[2,128,128]{2,1,0:T(8,128)(2,1)} %get-tuple-element.20), channel_id=1, source_target_pairs={{0,17},{1,16},{8,25},{9,24},{16,1},{17,0},{24,9},{25,8},{2,19},{3,... | collective-permute-start | bytes 196616 | tf_op jit(solution)/shard_map/ppermute | solution.py:696
  34.7 0.7 %copy-start.8 = (f32[1,1,1,1,128]{4,3,2,1,0:T(1,128)S(1)}, f32[1,1,1,1,128]{4,3,2,1,0:T(1,128)}, u32[]{:S(2)}) copy-start(f32[1,1,1,1,128]{4,3,2,1,0:T(1,128)} %param.9) | copy-start | bytes 1540
  34.7 0.7 %copy-start.9 = (f32[1,1,1,1,128]{4,3,2,1,0:T(1,128)S(1)}, f32[1,1,1,1,128]{4,3,2,1,0:T(1,128)}, u32[]{:S(2)}) copy-start(f32[1,1,1,1,128]{4,3,2,1,0:T(1,128)} %param.8) | copy-start | bytes 1540
  35.4 0.7 %collective-permute-start.7 = (f32[3,128]{1,0:T(4,128)S(1)}, f32[3,128]{1,0:T(4,128)S(1)}, u32[]{:S(2)}, u32[]{:S(2)}) collective-permute-start(f32[3,128]{1,0:T(4,128)S(1)} %pad_maximum_fusion), channel_id=1, source_target_pairs={{0,0},{8,1},{25,8},{17,9},{16,16},{24,17},{9,24},{1,25},{2,2},{10,... | collective-permute-start | bytes 4616 | tf_op jit(solution)/shard_map/ppermute | solution.py:669
  36.1 2.6 %copy-start.7 = (f32[3,128]{1,0:T(4,128)}, f32[3,128]{1,0:T(4,128)S(1)}, u32[]{:S(2)}) copy-start(f32[3,128]{1,0:T(4,128)S(1)} %collective-permute-done.7.obs_ref) | copy-start | bytes 4612
  36.1 2.5 %copy-start.3 = (bf16[2,128,128]{2,1,0:T(8,128)(2,1)}, bf16[2,128,128]{2,1,0:T(8,128)(2,1)S(1)}, u32[]{:S(2)}) copy-start(bf16[2,128,128]{2,1,0:T(8,128)(2,1)S(1)} %collective-permute-done.4.piece1_ref) | copy-start | bytes 196612
  36.2 2.4 %copy-start.4 = (bf16[2,128,128]{2,1,0:T(8,128)(2,1)}, bf16[2,128,128]{2,1,0:T(8,128)(2,1)S(1)}, u32[]{:S(2)}) copy-start(bf16[2,128,128]{2,1,0:T(8,128)(2,1)S(1)} %collective-permute-done.5.piece2_ref) | copy-start | bytes 196612
  38.6 0.6 %copy-start.5 = (bf16[2,128,128]{2,1,0:T(8,128)(2,1)}, bf16[2,128,128]{2,1,0:T(8,128)(2,1)S(1)}, u32[]{:S(2)}) copy-start(bf16[2,128,128]{2,1,0:T(8,128)(2,1)S(1)} %collective-permute-done.6.piece3_ref) | copy-start | bytes 196612

commit v2 on v0

--- a/solution.py
+++ b/solution.py
@@ -1,6 +1,11 @@
+import functools
+import math
+
 import jax
 import jax.numpy as jnp
 from jax import lax
+from jax.experimental import pallas as pl
+from jax.experimental.pallas import tpu as pltpu
 from jax.sharding import PartitionSpec as P
 
 ROOT_STEPS = 4
@@ -131,7 +136,7 @@
     return (jnp.roll(increment, patch // 2, axis=3) + mean_field[None]).astype(jnp.bfloat16)
 
 
-def on_device(prior_sample_set, flow_speeds, observed_cells, observed_values, error_variance):
+def on_device_general(prior_sample_set, flow_speeds, observed_cells, observed_values, error_variance):
     member_group_count = lax.axis_size("mem")
     northward_group_count = lax.axis_size("gy")
     local_member_states, layer_stack, rows_x, column_count_north = prior_sample_set.shape
@@ -203,6 +208,521 @@
     )
 
 
+LANES = 128
+HALO = 4
+OCTET = 8
+DOMAIN = 3 * HALO
+EXTENT = LANES + 2 * OCTET
+VMEM_GRANT = 24 << 20
+STAGE_FACTORS = (1.0 / 4.0, 1.0 / 3.0, 1.0 / 2.0, 1.0)
+
+
+def split_two(x):
+    high = x.astype(jnp.bfloat16)
+    return high, (x - high.astype(jnp.float32)).astype(jnp.bfloat16)
+
+
+def split_three(x):
+    high = x.astype(jnp.bfloat16)
+    rest = x - high.astype(jnp.float32)
+    middle = rest.astype(jnp.bfloat16)
+    return high, middle, (rest - middle.astype(jnp.float32)).astype(jnp.bfloat16)
+
+
+def tile_row(odd, j):
+    return jnp.where(odd == 1, DOMAIN - 1 - j, j - HALO)
+
+
+def domain_row(odd, row):
+    return jnp.where(odd == 1, DOMAIN - 1 - row, row + HALO)
+
+
+class Sizes:
+    def __init__(self, local, layers, rows):
+        self.local = local
+        self.layers = layers
+        self.rows = rows
+        self.members = 2 * local
+        self.per_member = layers * rows
+        self.halo_rows = layers * (HALO + 1) * LANES
+        self.wind_rows = 2 * layers * HALO
+        self.side_rows = layers * 2 * HALO * OCTET
+        self.corner_rows = layers * HALO * OCTET
+        self.obs_at = self.side_rows + 2 * layers * rows
+
+    def field_at(self, layer, j):
+        return (layer * DOMAIN + j) * EXTENT
+
+    def wind_at(self, part, layer, j):
+        return ((part * self.layers + layer) * DOMAIN + j) * EXTENT
+
+
+def columns_first(s, odd, own_ref, sib_ref, layer, j):
+    start = layer * s.rows + tile_row(odd, j)
+    parts = [ref[pl.ds(start, s.local, stride=s.per_member), :] for ref in (own_ref, sib_ref)]
+    return jnp.concatenate(parts, axis=0).T
+
+
+def wind_scale(s, odd, value):
+    sign = jnp.where(odd == 1, -0.5, 0.5)
+    row = lax.broadcasted_iota(jnp.int32, value.shape, 0)
+    return value * jnp.where(row < value.shape[0] // 2, sign, 0.5)
+
+
+def fetch_kernel(
+    s, prior_ref, wind_ref, cells_ref, values_ref, errors_ref, own_ref, wind_out_ref, obs_ref,
+    cells_vmem, values_vmem, errors_vmem, sems,
+):
+    copies = [
+        pltpu.make_async_copy(source, target, sems.at[i])
+        for i, (source, target) in enumerate(
+            (
+                (cells_ref, cells_vmem), (values_ref, values_vmem), (errors_ref, errors_vmem),
+                (wind_ref, wind_out_ref), (prior_ref, own_ref),
+            )
+        )
+    ]
+    for copy in copies:
+        copy.start()
+    obs_ref[...] = jnp.zeros_like(obs_ref)
+    for copy in copies[:3]:
+        copy.wait()
+    obs_ref[0:1, :] = cells_vmem[...].astype(jnp.float32)
+    obs_ref[1:2, :] = values_vmem[...]
+    obs_ref[2:3, :] = errors_vmem[...]
+    for copy in copies[3:]:
+        copy.wait()
+
+
+def pack_halo_kernel(s, own_ref, sib_ref, wind_ref, out_ref, field_ref, rows_ref):
+    odd = lax.rem(lax.axis_index("mem"), 2)
+    for layer in range(s.layers):
+        base = layer * (HALO + 1) * LANES
+        for j in range(HALO):
+            value = columns_first(s, odd, own_ref, sib_ref, layer, 2 * HALO + j)
+            field_ref[pl.ds(s.field_at(layer, 2 * HALO + j) + OCTET, LANES), :] = value
+            high, low = split_two(value)
+            out_ref[pl.ds(base + (HALO - j) * LANES, LANES), :] = high
+            if j == HALO - 1:
+                out_ref[pl.ds(base, LANES), :] = low
+    for block in range(2 * s.layers):
+        for j in range(HALO):
+            row = block * s.rows + tile_row(odd, 2 * HALO + j)
+            rows_ref[pl.ds(block * HALO + j, 1), :] = wind_ref[pl.ds(row, 1), :]
+    for i, part in enumerate(split_three(wind_scale(s, odd, rows_ref[...]))):
+        out_ref[pl.ds(s.halo_rows + i * s.wind_rows, s.wind_rows), :] = part
+
+
+def spread(parts, rows, targets, store):
+    stacked = jnp.concatenate(parts, axis=0)
+    turned = stacked.T
+    source = lax.broadcasted_iota(jnp.int32, (stacked.shape[0], LANES), 0)
+    for first, second in zip(targets[::2], targets[1::2], strict=True):
+        chosen = [jnp.where(lax.rem(source, rows) == row, 1.0, 0.0) for row in (first, second)]
+        both = dot(turned, jnp.concatenate(chosen, axis=1).astype(jnp.bfloat16), ((1,), (0,)))
+        store(first, both[:, :LANES])
+        store(second, both[:, LANES:])
+
+
+def pack_edges_kernel(s, own_ref, sib_ref, wind_ref, halo_ref, obs_ref, _, field_ref, side_ref, corner_ref, winds_ref):
+    odd = lax.rem(lax.axis_index("mem"), 2)
+    for layer in range(s.layers):
+        for j in range(HALO, 2 * HALO):
+            value = columns_first(s, odd, own_ref, sib_ref, layer, j)
+            field_ref[pl.ds(s.field_at(layer, j) + OCTET, LANES), :] = value
+    for layer in range(s.layers):
+        for j in range(HALO, DOMAIN):
+            at = s.field_at(layer, j) + OCTET
+            to = (layer * 2 * HALO + j - HALO) * OCTET
+            side_ref[pl.ds(to, HALO), :] = field_ref[pl.ds(at + LANES - HALO, HALO), :]
+            side_ref[pl.ds(to + HALO, HALO), :] = field_ref[pl.ds(at, HALO), :]
+        to, at = layer * HALO * OCTET, (layer * 2 * HALO + HALO) * OCTET
+        corner_ref[pl.ds(to, HALO * OCTET), :] = side_ref[pl.ds(at, HALO * OCTET), :].astype(jnp.bfloat16)
+    corner_ref[pl.ds(s.corner_rows, 3 * s.wind_rows), :] = halo_ref[pl.ds(s.halo_rows, 3 * s.wind_rows), :]
+    scaled = wind_scale(s, odd, wind_ref[...])
+    side_ref[pl.ds(s.side_rows, 2 * s.layers * s.rows), :] = scaled
+    side_ref[pl.ds(s.obs_at, OCTET), :] = obs_ref[...]
+
+    def store(row, value):
+        at = s.wind_at(row // s.rows // s.layers, row // s.rows % s.layers, domain_row(odd, row % s.rows))
+        winds_ref[pl.ds(pl.multiple_of(at, OCTET) + OCTET, LANES), :] = value
+
+    rows = 2 * s.layers * s.rows
+    spread(split_three(scaled), rows, list(range(rows)), store)
+
+
+def set_wind_edges(winds_ref, turned, row, at):
+    edge = jnp.concatenate([turned[LANES - OCTET :], turned[:OCTET]], axis=0)
+    value = jnp.broadcast_to(edge[:, row : row + 1], (2 * OCTET, LANES))
+    winds_ref[pl.ds(at + HALO, HALO), :] = value[HALO : 2 * HALO]
+    winds_ref[pl.ds(at + OCTET + LANES, HALO), :] = value[OCTET : OCTET + HALO]
+
+
+def padded_rows(x):
+    return jnp.concatenate([x, jnp.zeros((LANES - x.shape[0], LANES), x.dtype)], axis=0)
+
+
+def set_field_edges(s, field_ref, layer, j, edge):
+    at = s.field_at(layer, j)
+    field_ref[pl.ds(at + HALO, HALO), :] = edge[:HALO]
+    field_ref[pl.ds(at + OCTET + LANES, HALO), :] = edge[HALO:]
+
+
+def evaluate(s, field_ref, winds_ref, from_ref, stage, start, wanted, emit):
+    factor, share = STAGE_FACTORS[stage], 0.2 / s.layers
+    centre = {}
+    for j in range(wanted[0] - 1, wanted[1] + 1):
+        for layer in range(s.layers):
+            centre[layer, j] = from_ref[pl.ds(s.field_at(layer, j) + start, OCTET), :]
+    for j in range(*wanted):
+        for layer in range(s.layers):
+            at = s.field_at(layer, j) + start
+            others = sum(centre[k, j] for k in range(s.layers) if k != layer)
+            north, south = centre[layer, j + 1], centre[layer, j - 1]
+            east, west = from_ref[pl.ds(at + 1, OCTET), :], from_ref[pl.ds(at - 1, OCTET), :]
+            along = winds_ref[pl.ds(s.wind_at(0, layer, j) + start, OCTET), :]
+            across = winds_ref[pl.ds(s.wind_at(1, layer, j) + start, OCTET), :]
+            total = along * (south - north) + across * (west - east)
+            total = total + 0.1 * ((north + south) + (east + west))
+            total = total + ((share - 0.6) * centre[layer, j] + share * others)
+            base = field_ref[pl.ds(at, OCTET), :]
+            emit(layer, j, base + (total if factor == 1.0 else factor * total))
+
+
+def run_stage(s, field_ref, winds_ref, from_ref, to_ref, stage, wanted):
+    def step(i, carry):
+        start = HALO + OCTET * i
+
+        def emit(layer, j, value):
+            to_ref[pl.ds(s.field_at(layer, j) + start, OCTET), :] = value
+
+        evaluate(s, field_ref, winds_ref, from_ref, stage, start, wanted, emit)
+        return carry
+
+    lax.fori_loop(0, (LANES + 2 * HALO) // OCTET, step, 0)
+
+
+def inner_kernel(s, _, __, side_ref, field_ref, winds_ref, first_ref, second_ref):
+    odd = lax.rem(lax.axis_index("mem"), 2)
+    for layer in range(s.layers):
+        for j in range(HALO, DOMAIN):
+            edge = side_ref[pl.ds((layer * 2 * HALO + j - HALO) * OCTET, OCTET), :]
+            set_field_edges(s, field_ref, layer, j, edge)
+    beside = padded_rows(side_ref[pl.ds(s.side_rows, 2 * s.layers * s.rows), :]).T
+    for block in range(2 * s.layers):
+        for row in range(s.rows):
+            at = s.wind_at(block // s.layers, block % s.layers, domain_row(odd, row))
+            set_wind_edges(winds_ref, beside, block * s.rows + row, pl.multiple_of(at, OCTET))
+    refs = (field_ref, first_ref, second_ref, first_ref)
+    for stage in range(3):
+        wanted = (HALO + 1 + stage, DOMAIN - 1 - stage)
+        run_stage(s, field_ref, winds_ref, refs[stage], refs[stage + 1], stage, wanted)
+
+
+def forecast_kernel(
+    s, _, __, ___, ____, halo_ref, corner_ref,
+    out0_ref, out1_ref, out2_ref, out3_ref, field_ref, winds_ref, first_ref, second_ref,
+):
+    mem = lax.axis_index("mem")
+    odd = lax.rem(mem, 2)
+    place = (mem // 2) * 2 + lax.axis_index("gy")
+
+    for layer in range(s.layers):
+        corner = corner_ref[pl.ds(layer * HALO * OCTET, HALO * OCTET), :].astype(jnp.float32)
+        for j in range(HALO):
+            base = layer * (HALO + 1) * LANES
+            value = halo_ref[pl.ds(base + (HALO - j) * LANES, LANES), :].astype(jnp.float32)
+            if j == HALO - 1:
+                value = value + halo_ref[pl.ds(base, LANES), :].astype(jnp.float32)
+            field_ref[pl.ds(s.field_at(layer, j) + OCTET, LANES), :] = value
+            set_field_edges(s, field_ref, layer, j, corner[j * OCTET : (j + 1) * OCTET])
+    far = [corner_ref[pl.ds(s.corner_rows + i * s.wind_rows, s.wind_rows), :].astype(jnp.float32) for i in range(3)]
+    beyond = padded_rows(far[0] + far[1] + far[2]).T
+    targets = [block * HALO + j for block in range(2 * s.layers) for j in range(1, HALO)]
+
+    def wind_at(row):
+        return s.wind_at(row // HALO // s.layers, row // HALO % s.layers, row % HALO)
+
+    for row in targets:
+        set_wind_edges(winds_ref, beyond, row, wind_at(row))
+
+    def store(row, value):
+        winds_ref[pl.ds(wind_at(row) + OCTET, LANES), :] = value
+
+    near = [halo_ref[pl.ds(s.halo_rows + i * s.wind_rows, s.wind_rows), :] for i in range(3)]
+    spread(near, s.wind_rows, targets, store)
+
+    refs = (field_ref, first_ref, second_ref, first_ref)
+    for stage in range(3):
+        wanted = (1 + stage, HALO + 1 + stage)
+        run_stage(s, field_ref, winds_ref, refs[stage], refs[stage + 1], stage, wanted)
+
+    swap_one = jnp.bitwise_xor(jnp.bitwise_and(place, 1), odd) == 1
+    swap_two = jnp.bitwise_xor(place // 2, odd) == 1
+    outs = (out0_ref, out1_ref, out2_ref, out3_ref)
+
+    def last_step(i, carry):
+        results = [{}, {}]
+        for k in range(2):
+            start = OCTET + 2 * OCTET * i + OCTET * k
+            emit = lambda layer, j, value: results[k].update({(layer, j): value})
+            evaluate(s, field_ref, winds_ref, first_ref, 3, start, (HALO, 2 * HALO), emit)
+        at = pl.multiple_of(2 * OCTET * i, 2 * OCTET)
+        for layer in range(s.layers):
+            rows = [
+                jnp.concatenate([result[layer, HALO + t] for result in results], axis=0).astype(jnp.bfloat16)
+                for t in range(HALO)
+            ]
+            rows = [jnp.where(swap_one, rows[t ^ 1], rows[t]) for t in range(HALO)]
+            rows = [jnp.where(swap_two, rows[t ^ 2], rows[t]) for t in range(HALO)]
+            for d, out_ref in enumerate(outs):
+                out_ref[layer, pl.ds(at, 2 * OCTET), :] = rows[d]
+        return carry
+
+    lax.fori_loop(0, LANES // (2 * OCTET), last_step, 0)
+
+
+def dot(a, b, contract):
+    return lax.dot_general(a, b, (contract, ((), ())), preferred_element_type=jnp.float32)
+
+
+def dot_three(a, b, contract=((1,), (0,))):
+    (a_high, a_low), (b_high, b_low) = a, b
+    return dot(a_high, b_low, contract) + dot(a_low, b_high, contract) + dot(a_high, b_high, contract)
+
+
+def analysis_kernel(s, total_members, piece0_ref, piece1_ref, piece2_ref, piece3_ref, obs_ref, side_ref, out0_ref, out1_ref, out2_ref, out3_ref):
+    mem, side = lax.axis_index("mem"), lax.axis_index("gy")
+    outs = (out0_ref, out1_ref, out2_ref, out3_ref)
+    pieces = (piece0_ref, piece1_ref, piece2_ref, piece3_ref)
+    width = 2 * LANES
+    cells_total = s.layers * width
+    inverse = 1.0 / total_members
+    members = jnp.concatenate(
+        [
+            jnp.concatenate([pieces[2 * dx + dy][layer] for layer in range(s.layers) for dy in range(2)], axis=0)
+            for dx in range(2)
+        ],
+        axis=1,
+    )
+    mean_row = dot(jnp.ones((OCTET, total_members), jnp.bfloat16), members, ((1,), (1,)))[0:1] * inverse
+    mean = dot(members, jnp.ones((total_members, LANES), jnp.bfloat16), ((1,), (0,))) * inverse
+    perturbation = jnp.concatenate(
+        [(members[:, i : i + LANES].astype(jnp.float32) - mean).astype(jnp.bfloat16) for i in range(0, total_members, LANES)],
+        axis=1,
+    )
+
+    count = obs_ref.shape[1]
+    mine = lax.rem(mem, 2) == side
+    obs = padded_rows(jnp.where(mine, obs_ref[...], side_ref[pl.ds(s.obs_at, OCTET), :])).T
+    cells = obs[:, 0:1].astype(jnp.int32)
+    values, errors = obs[:, 1:2], obs[:, 2:3]
+    column = jnp.bitwise_and(cells, width - 1)
+    layer_of = jnp.right_shift(cells, width.bit_length() - 1)
+    half = jnp.bitwise_xor(jnp.right_shift(column, LANES.bit_length() - 1), side)
+    index = layer_of * width + half * LANES + jnp.bitwise_and(column, LANES - 1)
+    chosen = jnp.where(lax.broadcasted_iota(jnp.int32, (count, cells_total), 1) == index, 1.0, 0.0)
+    picked = dot(chosen.astype(jnp.bfloat16), members, ((1,), (0,)))
+    base = jnp.sum(picked, axis=1, keepdims=True) * inverse
+    offset = column.astype(jnp.float32) - 0.5 * (width - 1)
+    weight = jnp.zeros_like(values)
+    for shift in (-1, 0, 1):
+        distance = (shift * width + offset) / width
+        weight = weight + jnp.exp(-0.5 * distance * distance) / errors
+    scale = jnp.sqrt(weight)
+    scaled = (picked - base) * scale
+    innovation = (values - base) * scale
+    parts = split_two(scaled)
+    size = (total_members, total_members)
+    diagonal = lax.broadcasted_iota(jnp.int32, size, 0) == lax.broadcasted_iota(jnp.int32, size, 1)
+    identity = jnp.where(diagonal, 1.0, 0.0)
+    gram = dot_three(parts, parts, ((0,), (0,))) + (total_members - 1.0) * identity
+    square = jnp.sum(jnp.sum(gram * gram, axis=0, keepdims=True), axis=1, keepdims=True)
+    frob = jnp.sqrt(square)
+    current = gram / frob
+    middle = 1.5 * identity - 0.5 * current
+    root = middle
+    for step in range(1, ROOT_STEPS):
+        middle_parts = split_two(middle)
+        current = dot_three(split_two(current), middle_parts)
+        root_parts = split_two(root)
+        middle = 1.5 * identity - 0.5 * dot_three(root_parts, split_two(current))
+        root = dot_three(split_two(middle), root_parts)
+    projected = jnp.sum(scaled * innovation, axis=0, keepdims=True)
+    once = jnp.sum(root * projected, axis=1, keepdims=True)
+    mean_weights = jnp.sum(root * once, axis=0, keepdims=True) / frob
+    weights = (math.sqrt(total_members - 1.0) * root / jnp.sqrt(frob) + mean_weights).astype(jnp.bfloat16)
+    for dx in range(2):
+        for part in range(2):
+            rows = slice((2 * dx + part) * s.local, (2 * dx + part + 1) * s.local)
+            block = dot(weights[rows], perturbation, ((1,), (1,))) + mean_row
+            block = block.astype(jnp.bfloat16)
+            for dy in range(2):
+                for layer in range(s.layers):
+                    at = (layer * 2 + dy) * LANES
+                    outs[2 * dx + dy][part, layer] = block[:, at : at + LANES]
+
+
+def place_rows_kernel(s, *refs):
+    pieces, passed, out_ref, rows_ref = refs[:4], refs[4:8], refs[8], refs[9]
+    mem = lax.axis_index("mem")
+    odd = lax.rem(mem, 2)
+    place = (mem // 2) * 2 + lax.axis_index("gy")
+    for d in range(4):
+        for ref, part, parity in ((pieces[d], 0, odd), (passed[d], 1, 1 - odd)):
+            row = 4 * parity + jnp.bitwise_xor(place, d)
+            for layer in range(s.layers):
+                for octet in range(0, s.local // OCTET, 2):
+                    value = ref[part, layer, octet * OCTET : (octet + 2) * OCTET, :].astype(jnp.float32)
+                    start = octet * OCTET * s.per_member + layer * s.rows + row
+                    rows_ref[pl.ds(start, 2 * OCTET, stride=s.per_member), :] = value
+    out_ref[...] = rows_ref[...].astype(jnp.bfloat16).reshape(out_ref.shape)
+
+
+def vmem_call(kernel, outs, scratch, *args, aliases=None):
+    spec = pl.BlockSpec(memory_space=pltpu.VMEM)
+    return pl.pallas_call(
+        kernel,
+        out_shape=outs,
+        in_specs=[spec] * len(args),
+        out_specs=jax.tree.map(lambda _: spec, outs),
+        scratch_shapes=[pltpu.VMEM(shape, dtype) for shape, dtype in scratch],
+        input_output_aliases=aliases or {},
+        compiler_params=pltpu.CompilerParams(vmem_limit_bytes=VMEM_GRANT),
+    )(*args)
+
+
+def on_device_tile(prior_sample_set, flow_speeds, observed_cells, observed_values, error_variance):
+    local, layers, rows, columns = prior_sample_set.shape
+    s = Sizes(local, layers, rows)
+    n_gx = lax.axis_size("gx")
+    f32, bf16 = jnp.float32, jnp.bfloat16
+    shaped = jax.ShapeDtypeStruct
+
+    pair = [(m, m ^ 1) for m in range(4)]
+
+    def step(m):
+        return 1 if m % 2 == 0 else n_gx - 1
+
+    along = [(m * n_gx + z, m * n_gx + (z + step(m)) % n_gx) for m in range(4) for z in range(n_gx)]
+    across = [(0, 1), (1, 0)]
+    diagonal = [
+        ((m * n_gx + z) * 2 + y, (m * n_gx + (z + step(m)) % n_gx) * 2 + 1 - y)
+        for m in range(4) for z in range(n_gx) for y in range(2)
+    ]
+    owners = [((x * 2 + y) * 2 + c, (x * 2 + c) * 2 + y) for x in range(2) for c in range(2) for y in range(2)]
+
+    sib = lax.ppermute(prior_sample_set, "mem", pair).reshape(local * layers * rows, columns)
+    count = observed_cells.shape[-1]
+    vmem, hbm = pl.BlockSpec(memory_space=pltpu.VMEM), pl.BlockSpec(memory_space=pltpu.HBM)
+    own, wind, obs = pl.pallas_call(
+        functools.partial(fetch_kernel, s),
+        out_shape=(
+            shaped((local * layers * rows, columns), f32),
+            shaped((2 * layers * rows, columns), f32),
+            shaped((OCTET, count), f32),
+        ),
+        in_specs=[hbm] * 5,
+        out_specs=(vmem, vmem, vmem),
+        scratch_shapes=[
+            pltpu.VMEM((1, count), jnp.int32),
+            pltpu.VMEM((1, count), f32),
+            pltpu.VMEM((1, count), f32),
+            pltpu.SemaphoreType.DMA((5,)),
+        ],
+        compiler_params=pltpu.CompilerParams(vmem_limit_bytes=VMEM_GRANT),
+    )(
+        *(
+            pltpu.with_memory_space_constraint(x, pltpu.HBM)
+            for x in (
+                prior_sample_set.reshape(local * layers * rows, columns),
+                flow_speeds.reshape(2 * layers * rows, columns),
+                observed_cells.reshape(1, count),
+                observed_values.reshape(1, count),
+                error_variance.reshape(1, count),
+            )
+        )
+    )
+    obs_sib = lax.ppermute(obs, "mem", pair)
+
+    field_shape = shaped((layers * DOMAIN * EXTENT, LANES), f32)
+    winds_shape = shaped((2 * layers * DOMAIN * EXTENT, LANES), f32)
+    halo_out, field = vmem_call(
+        functools.partial(pack_halo_kernel, s),
+        (shaped((s.halo_rows + 3 * s.wind_rows, LANES), bf16), field_shape),
+        [((s.wind_rows, LANES), f32)],
+        own, sib, wind,
+    )
+    halo = lax.ppermute(halo_out, ("mem", "gx"), along)
+    field, side_out, corner_out, winds = vmem_call(
+        functools.partial(pack_edges_kernel, s),
+        (
+            field_shape,
+            shaped((s.obs_at + OCTET, LANES), f32),
+            shaped((s.corner_rows + 3 * s.wind_rows, LANES), bf16),
+            winds_shape,
+        ),
+        [],
+        own, sib, wind, halo_out, obs_sib, field,
+        aliases={5: 0},
+    )
+    side = lax.ppermute(side_out, "gy", across)
+    corner = lax.ppermute(corner_out, ("mem", "gx", "gy"), diagonal)
+    field, winds, first, second = vmem_call(
+        functools.partial(inner_kernel, s),
+        (field_shape, winds_shape, field_shape, field_shape),
+        [],
+        field, winds, side,
+        aliases={0: 0, 1: 1},
+    )
+    piece = shaped((layers, LANES, s.members), bf16)
+    *pieces, _, _, _, _ = vmem_call(
+        functools.partial(forecast_kernel, s),
+        (piece, piece, piece, piece, field_shape, winds_shape, field_shape, field_shape),
+        [],
+        field, winds, first, second, halo, corner,
+        aliases={0: 4, 1: 5, 2: 6, 3: 7},
+    )
+
+    def flip(d):
+        dx, dy = d // 2, d % 2
+        return [((m * 2 + y), ((m ^ (2 * dx)) * 2 + (y ^ dy))) for m in range(4) for y in range(2)]
+
+    def exchange(parts):
+        return [parts[0]] + [lax.ppermute(parts[d], ("mem", "gy"), flip(d)) for d in range(1, 4)]
+
+    answer = shaped((2, layers, local, LANES), bf16)
+    outgoing = vmem_call(
+        functools.partial(analysis_kernel, s, 4 * local),
+        (answer, answer, answer, answer),
+        [],
+        *exchange(pieces), obs, side,
+    )
+    returned = exchange(outgoing)
+    passed = [lax.ppermute(part, "mem", pair) for part in returned]
+    return vmem_call(
+        functools.partial(place_rows_kernel, s),
+        shaped((local, layers, rows, columns), bf16),
+        [((local * layers * rows, LANES), f32)],
+        *returned, *passed,
+    )
+
+
+def on_device(prior_sample_set, flow_speeds, observed_cells, observed_values, error_variance):
+    local, layers, rows, columns = prior_sample_set.shape
+    suits = (
+        lax.axis_size("mem") == 4
+        and lax.axis_size("gy") == 2
+        and rows == 2 * HALO
+        and columns == LANES
+        and observed_cells.shape[-2] == 1
+        and 2 * local == LANES
+        and observed_cells.shape[-1] == LANES
+    )
+    form = on_device_tile if suits else on_device_general
+    return form(prior_sample_set, flow_speeds, observed_cells, observed_values, error_variance)
+
+
 def solution(mesh):
     in_specs = (
         P("mem", None, "gx", "gy"),

time: 75 us -> 40.3 us (0.54)
  local copies, waits for them, and re-layouts: 13.5 us -> 0 us
  other arithmetic: 11.9 us -> 0 us
  Pallas kernels: 0 us -> 10.4 us
  blocking collectives: 8.54 us -> 0 us
  matrix products: 6.68 us -> 0 us
  starting transfers between devices: 16.8 us -> 14.1 us
  between operations: 1.24 us -> 0.05 us
    pallas_call x0 -> x7, Pallas kernels: none -> 10.4 us  [the longest x6 9.21 us: vmem_call(): pl.pallas_call(kernel, out_shape=outs, in_specs=[spec] * len(args), out_s...]
    all_to_all x1 -> x0, blocking collectives: 8.54 us -> none  [on_device(): lax.all_to_all(outgoing, ('mem', 'gy'), split_axis=0, concat_axis=0, tile...]
    dot_general x16 -> x0, matrix products: 6.68 us -> none  [the longest x4 1.46 us: analyze(): jnp.einsum('pab,pbc->pac', root, current, precision=highest)]
    add x3 -> x0, other arithmetic: 5.83 us -> none  [the longest x1 2.09 us: deep_step(): crop_margin(padded, 2) + 0.5 * section_two]
    all_to_all x1 -> x0, waiting for transfers between devices: 5.71 us -> none  [on_device(): lax.all_to_all(flattened_realizations, ('mem', 'gy'), split_axis=0, conca...]
    slice x8 -> x0, local copies, waits for them, and re-layouts: 5.57 us -> none  [the longest x4 3.86 us: with_halo(): lax.slice_in_dim(block, block.shape[dim] - width, None, axis=dim)]
    ppermute x8 -> x15, waiting for transfers between devices: 10.2 us -> 15.7 us  [the longest x6 7.39 us: exchange(): lax.ppermute(parts[d], ('mem', 'gy'), flip(d))]
    all_to_all x1 -> x0, starting transfers between devices: 3.59 us -> none  [on_device(): lax.all_to_all(flattened_realizations, ('mem', 'gy'), split_axis=0, conca...]
  transfers between devices with their start and end apart: 9 -> 15, of which waited for: 7 -> 11; matrix products, arithmetic and copies ran while one was open for 4% -> 0% of each run, Pallas kernels for 0% -> 8%
where the time goes in v2:
time: 40.3 us; the launch traced here: 40.1 us
  waiting for transfers between devices  15.7 us (39%)
  starting transfers between devices  14.1 us (35%)
  Pallas kernels  10.4 us (26%)
    pallas_call x6, Pallas kernels, vmem_call(): pl.pallas_call(kernel, out_shape=outs, in_specs=[spec] * len(args), out_s...  9.21 us
    ppermute x6, waiting for transfers between devices, exchange(): lax.ppermute(parts[d], ('mem', 'gy'), flip(d))  7.39 us
    ppermute x6, starting transfers between devices, exchange(): lax.ppermute(parts[d], ('mem', 'gy'), flip(d))  7.1 us
    ppermute x1, waiting for transfers between devices, on_device_tile(): side = lax.ppermute(side_out, 'gy', across)  3.26 us
    ppermute x1, starting transfers between devices, on_device_tile(): halo = lax.ppermute(halo_out, ('mem', 'gx'), along)  2.99 us
    ppermute x1, waiting for transfers between devices, on_device_tile(): corner = lax.ppermute(corner_out, ('mem', 'gx', 'gy'), diagonal)  2.35 us
    ppermute x1, starting transfers between devices, on_device_tile(): obs_sib = lax.ppermute(obs, 'mem', pair)  1.88 us
    ppermute x1, starting transfers between devices, on_device_tile(): side = lax.ppermute(side_out, 'gy', across)  1.58 us
  transfers between devices with their start and end apart: 15, of which 11 were waited for; matrix products, arithmetic and copies ran while one was open for 0% of the time, Pallas kernels for 8%

profile of v2, /device:TPU:0, one launch (start us, length us, event | category | flops | bytes accessed | tf_op | source)
XLA Modules:
  0.0 40.1 jit_solution(5130711818097435190)
XLA Ops:
  0.0 0.5 %collective-permute-start = (f32[64,2,8,128]{3,2,1,0:T(8,128)}, f32[64,2,8,128]{3,2,1,0:T(8,128)S(1)}, u32[]{:S(2)}, u32[]{:S(2)}) collective-permute-start(f32[64,2,8,128]{3,2,1,0:T(8,128)} %param.5), channel_id=1, source_target_pairs={{0,8},{8,0},{16,24},{24,16},{1,9},{9,1},{17,25},{25,17},{2,10},{10... | collective-permute-start | bytes 1572872 | tf_op jit(solution)/shard_map/ppermute | solution.py:615
  0.5 1.1 %shard_map.55 = (f32[1024,128]{1,0:T(8,128)S(1)}, f32[32,128]{1,0:T(8,128)S(1)}, f32[8,128]{1,0:T(8,128)S(1)}) custom-call(f32[1024,128]{1,0:T(8,128)} %bitcast.8, f32[32,128]{1,0:T(8,128)} %bitcast.9, s32[1,128]{1,0:T(1,128)} %bitcast.10, f32[1,128]{1,0:T(1,128)} %bitcast.11, f32[1,128]{1,0:T(1,128)} %bitcast.12), custom_call_target="tpu_custom_call" | custom-call | tf_op jit(solution)/shard_map/pallas_call | solution.py:618
  1.7 0.6 %collective-permute-done = f32[64,2,8,128]{3,2,1,0:T(8,128)S(1)} collective-permute-done((f32[64,2,8,128]{3,2,1,0:T(8,128)}, f32[64,2,8,128]{3,2,1,0:T(8,128)S(1)}, u32[]{:S(2)}, u32[]{:S(2)}) %collective-permute-start) | collective-permute-done | bytes 524320 | tf_op jit(solution)/shard_map/ppermute | solution.py:615
  2.2 0.3 shard_map.56
  2.6 3.0 %collective-permute-start.3 = (bf16[1328,128]{1,0:T(8,128)(2,1)S(1)}, bf16[1328,128]{1,0:T(8,128)(2,1)S(1)}, u32[]{:S(2)}, u32[]{:S(2)}) collective-permute-start(bf16[1328,128]{1,0:T(8,128)(2,1)S(1)} %get-tuple-element.28.halo_ref), channel_id=1, source_target_pairs={{0,2},{2,4},{4,6},{6,0},{8,14},{10,8},{12,10},{14,12},{16,18},{18,... | collective-permute-start | bytes 1019912 | tf_op jit(solution)/shard_map/ppermute | solution.py:656
  5.6 1.9 %collective-permute-start.1 = (f32[8,128]{1,0:T(8,128)S(1)}, f32[8,128]{1,0:T(8,128)S(1)}, u32[]{:S(2)}, u32[]{:S(2)}) collective-permute-start(f32[8,128]{1,0:T(8,128)S(1)} %get-tuple-element.29.obs_ref), channel_id=1, source_target_pairs={{0,8},{8,0},{16,24},{24,16},{1,9},{9,1},{17,25},{25,17},{2,10},{10... | collective-permute-start | bytes 12296 | tf_op jit(solution)/shard_map/ppermute | solution.py:646
  7.4 0.8 %collective-permute-done.1.obs_ref = f32[8,128]{1,0:T(8,128)S(1)} collective-permute-done((f32[8,128]{1,0:T(8,128)S(1)}, f32[8,128]{1,0:T(8,128)S(1)}, u32[]{:S(2)}, u32[]{:S(2)}) %collective-permute-start.1) | collective-permute-done | bytes 4128 | tf_op jit(solution)/shard_map/ppermute | solution.py:646
  8.3 0.5 %shard_map.57 = (f32[3456,128]{1,0:T(8,128)S(1)}, f32[168,128]{1,0:T(8,128)S(1)}, bf16[112,128]{1,0:T(8,128)(2,1)S(1)}, f32[6912,128]{1,0:T(8,128)S(1)}) custom-call(f32[1024,128]{1,0:T(8,128)S(1)} %get-tuple-element.26.own_ref, f32[1024,128]{1,0:T(8,128)S(1)} %bitcast.7, f32[32,128]{1,0:T(8,128)S(1)} %get-tuple-element.27.wind_ref, ...), custom_call_target="tpu_custom_call", output_to_operand_aliasing={{0}: (5, {})} | custom-call | tf_op jit(solution)/shard_map/pallas_call | solution.py:584
  8.8 1.6 %collective-permute-start.2 = (f32[168,128]{1,0:T(8,128)S(1)}, f32[168,128]{1,0:T(8,128)S(1)}, u32[]{:S(2)}, u32[]{:S(2)}) collective-permute-start(f32[168,128]{1,0:T(8,128)S(1)} %get-tuple-element.33), channel_id=1, source_target_pairs={{0,1},{1,0},{2,3},{3,2},{4,5},{5,4},{6,7},{7,6},{8,9},{9,8},{10,11... | collective-permute-start | bytes 258056 | tf_op jit(solution)/shard_map/ppermute | solution.py:669
  10.4 3.3 %collective-permute-done.2.side_ref = f32[168,128]{1,0:T(8,128)S(1)} collective-permute-done((f32[168,128]{1,0:T(8,128)S(1)}, f32[168,128]{1,0:T(8,128)S(1)}, u32[]{:S(2)}, u32[]{:S(2)}) %collective-permute-start.2) | collective-permute-done | bytes 86048 | tf_op jit(solution)/shard_map/ppermute | solution.py:669
  13.6 1.6 %shard_map.58 = (f32[3456,128]{1,0:T(8,128)S(1)}, f32[6912,128]{1,0:T(8,128)S(1)}, f32[3456,128]{1,0:T(8,128)S(1)}, f32[3456,128]{1,0:T(8,128)S(1)}) custom-call(f32[3456,128]{1,0:T(8,128)S(1)} %get-tuple-element.31._, f32[6912,128]{1,0:T(8,128)S(1)} %get-tuple-element.32.__, ...), custom_call_target="tpu_custom_call", output_to_operand_aliasing={{0}: (0, {}), {1}: (1, {})} | custom-call | tf_op jit(solution)/shard_map/pallas_call | solution.py:584
  15.2 2.3 %collective-permute-done.4.corner_ref = bf16[112,128]{1,0:T(8,128)(2,1)S(1)} collective-permute-done((bf16[112,128]{1,0:T(8,128)(2,1)S(1)}, bf16[112,128]{1,0:T(8,128)(2,1)S(1)}, u32[]{:S(2)}, u32[]{:S(2)}) %collective-permute-start.4) | collective-permute-done | bytes 28704 | tf_op jit(solution)/shard_map/ppermute | solution.py:670
  17.6 0.0 collective-permute-done.3.halo_ref
  17.6 2.1 %shard_map.59 = (bf16[2,128,128]{2,1,0:T(8,128)(2,1)S(1)}, bf16[2,128,128]{2,1,0:T(8,128)(2,1)S(1)}, bf16[2,128,128]{2,1,0:T(8,128)(2,1)S(1)}, bf16[2,128,128]{2...) custom-call(f32[3456,128]{1,0:T(8,128)S(1)} %get-tuple-element.34._,, ...), custom_call_target="tpu_custom_call", output_to_operand_aliasing={{4}: (0, {}), {5}: (1, {}), {6}: (2, {}), {7}: (3, {})} | custom-call | tf_op jit(solution)/shard_map/pallas_call | solution.py:584
  19.7 0.6 %collective-permute-start.5 = (bf16[2,128,128]{2,1,0:T(8,128)(2,1)S(1)}, bf16[2,128,128]{2,1,0:T(8,128)(2,1)S(1)}, u32[]{:S(2)}, u32[]{:S(2)}) collective-permute-start(bf16[2,128,128]{2,1,0:T(8,128)(2,1)S(1)} %get-tuple-element.40), channel_id=1, source_target_pairs={{0,1},{1,0},{8,9},{9,8},{16,17},{17,16},{24,25},{25,24},{2,3},{3,2... | collective-permute-start | bytes 196616 | tf_op jit(solution)/shard_map/ppermute | solution.py:692
  20.2 1.5 %collective-permute-start.6 = (bf16[2,128,128]{2,1,0:T(8,128)(2,1)S(1)}, bf16[2,128,128]{2,1,0:T(8,128)(2,1)S(1)}, u32[]{:S(2)}, u32[]{:S(2)}) collective-permute-start(bf16[2,128,128]{2,1,0:T(8,128)(2,1)S(1)} %get-tuple-element.41), channel_id=1, source_target_pairs={{0,16},{1,17},{8,24},{9,25},{16,0},{17,1},{24,8},{25,9},{2,18},{3,... | collective-permute-start | bytes 196616 | tf_op jit(solution)/shard_map/ppermute | solution.py:692
  21.7 1.5 %collective-permute-start.7 = (bf16[2,128,128]{2,1,0:T(8,128)(2,1)S(1)}, bf16[2,128,128]{2,1,0:T(8,128)(2,1)S(1)}, u32[]{:S(2)}, u32[]{:S(2)}) collective-permute-start(bf16[2,128,128]{2,1,0:T(8,128)(2,1)S(1)} %get-tuple-element.42), channel_id=1, source_target_pairs={{0,17},{1,16},{8,25},{9,24},{16,1},{17,0},{24,9},{25,8},{2,19},{3,... | collective-permute-start | bytes 196616 | tf_op jit(solution)/shard_map/ppermute | solution.py:692
  23.2 1.1 %collective-permute-done.5.piece1_ref = bf16[2,128,128]{2,1,0:T(8,128)(2,1)S(1)} collective-permute-done((bf16[2,128,128]{2,1,0:T(8,128)(2,1)S(1)}, bf16[2,128,128]{2,1,0:T(8,128)(2,1)S(1)}, u32[]{:S(2)}, u32[]{:S(2)}) %collective-permute-start.5) | collective-permute-done | bytes 65568 | tf_op jit(solution)/shard_map/ppermute | solution.py:692
  24.3 0.2 collective-permute-done.6.piece2_ref
  24.5 2.4 %collective-permute-done.7.piece3_ref = bf16[2,128,128]{2,1,0:T(8,128)(2,1)S(1)} collective-permute-done((bf16[2,128,128]{2,1,0:T(8,128)(2,1)S(1)}, bf16[2,128,128]{2,1,0:T(8,128)(2,1)S(1)}, u32[]{:S(2)}, u32[]{:S(2)}) %collective-permute-start.7) | collective-permute-done | bytes 65568 | tf_op jit(solution)/shard_map/ppermute | solution.py:692
  26.9 3.7 %shard_map.60 = (bf16[2,2,64,128]{3,2,1,0:T(8,128)(2,1)S(1)}, bf16[2,2,64,128]{3,2,1,0:T(8,128)(2,1)S(1)}, bf16[2,2,64,128]{3,2,1,0:T(8,128)(2,1)S(1)}, bf16[2,2,64,128]{3,2,1,0:T(8,128)(2,1)S(1)}) custom-call(bf16[2,128,128]{2,1,0:T(8,128)(2,1)S(1)} %get-tuple-element.39.piece0_ref, bf16[2,128,128]{2,1,0:T(8,128)(2,1)S(1)} %collective-permute-done.5.piece1_ref, ...), custom_call_target="tpu_custom_call" | custom-call | tf_op jit(solution)/shard_map/pallas_call | solution.py:584
  30.6 1.6 %collective-permute-start.8 = (bf16[2,2,64,128]{3,2,1,0:T(8,128)(2,1)S(1)}, bf16[2,2,64,128]{3,2,1,0:T(8,128)(2,1)S(1)}, u32[]{:S(2)}, u32[]{:S(2)}) collective-permute-start(bf16[2,2,64,128]{3,2,1,0:T(8,128)(2,1)S(1)} %get-tuple-element.44), channel_id=1, source_target_pairs={{0,1},{1,0},{8,9},{9,8},{16,17},{17,16},{24,25},{25,24},{2,3},{3,2... | collective-permute-start | bytes 196616 | tf_op jit(solution)/shard_map/ppermute | solution.py:692
  32.2 0.5 %collective-permute-start.9 = (bf16[2,2,64,128]{3,2,1,0:T(8,128)(2,1)S(1)}, bf16[2,2,64,128]{3,2,1,0:T(8,128)(2,1)S(1)}, u32[]{:S(2)}, u32[]{:S(2)}) collective-permute-start(bf16[2,2,64,128]{3,2,1,0:T(8,128)(2,1)S(1)} %get-tuple-element.45), channel_id=1, source_target_pairs={{0,16},{1,17},{8,24},{9,25},{16,0},{17,1},{24,8},{25,9},{2,18},{3,... | collective-permute-start | bytes 196616 | tf_op jit(solution)/shard_map/ppermute | solution.py:692
  32.7 1.4 %collective-permute-start.10 = (bf16[2,2,64,128]{3,2,1,0:T(8,128)(2,1)S(1)}, bf16[2,2,64,128]{3,2,1,0:T(8,128)(2,1)S(1)}, u32[]{:S(2)}, u32[]{:S(2)}) collective-permute-start(bf16[2,2,64,128]{3,2,1,0:T(8,128)(2,1)S(1)} %get-tuple-element.46), channel_id=1, source_target_pairs={{0,17},{1,16},{8,25},{9,24},{16,1},{17,0},{24,9},{25,8},{2,19},{3,... | collective-permute-start | bytes 196616 | tf_op jit(solution)/shard_map/ppermute | solution.py:692
  34.1 0.0 collective-permute-start.11
  34.1 0.8 %collective-permute-done.8.refs_1_ = bf16[2,2,64,128]{3,2,1,0:T(8,128)(2,1)S(1)} collective-permute-done((bf16[2,2,64,128]{3,2,1,0:T(8,128)(2,1)S(1)}, bf16[2,2,64,128]{3,2,1,0:T(8,128)(2,1)S(1)}, u32[]{:S(2)}, u32[]{:S(2)}) %collective-permute-start.8) | collective-permute-done | bytes 65568 | tf_op jit(solution)/shard_map/ppermute | solution.py:692
  34.9 0.0 collective-permute-start.12
  34.9 1.5 %collective-permute-done.9.refs_2_ = bf16[2,2,64,128]{3,2,1,0:T(8,128)(2,1)S(1)} collective-permute-done((bf16[2,2,64,128]{3,2,1,0:T(8,128)(2,1)S(1)}, bf16[2,2,64,128]{3,2,1,0:T(8,128)(2,1)S(1)}, u32[]{:S(2)}, u32[]{:S(2)}) %collective-permute-start.9) | collective-permute-done | bytes 65568 | tf_op jit(solution)/shard_map/ppermute | solution.py:692
  36.4 0.0 collective-permute-start.13
  36.4 1.4 %collective-permute-done.10.refs_3_ = bf16[2,2,64,128]{3,2,1,0:T(8,128)(2,1)S(1)} collective-permute-done((bf16[2,2,64,128]{3,2,1,0:T(8,128)(2,1)S(1)}, bf16[2,2,64,128]{3,2,1,0:T(8,128)(2,1)S(1)}, u32[]{:S(2)}, u32[]{:S(2)}) %collective-permute-start.10) | collective-permute-done | bytes 65568 | tf_op jit(solution)/shard_map/ppermute | solution.py:692
  37.9 1.2 %collective-permute-done.14.refs_7_ = bf16[2,2,64,128]{3,2,1,0:T(8,128)(2,1)S(1)} collective-permute-done((bf16[2,2,64,128]{3,2,1,0:T(8,128)(2,1)S(1)}, bf16[2,2,64,128]{3,2,1,0:T(8,128)(2,1)S(1)}, u32[]{:S(2)}, u32[]{:S(2)}) %collective-permute-start.14) | collective-permute-done | bytes 65568 | tf_op jit(solution)/shard_map/ppermute | solution.py:702
  39.1 1.0 %shard_map.61 = bf16[64,2,8,128]{3,2,1,0:T(8,128)(2,1)} custom-call(bf16[2,2,64,128]{3,2,1,0:T(8,128)(2,1)S(1)} %get-tuple-element.43.refs_0_, bf16[2,2,64,128]{3,2,1,0:T(8,128)(2,1)S(1)} %collective-permute-done.8.refs_1_, bf16[2,2,64,128]{3,2,1,0:T(8,128)(2,1)S(1)} %collective-permute-done.9.refs_2_, ...), custom_call_target="tpu_custom_call" | custom-call | tf_op jit(solution)/shard_map/pallas_call | solution.py:584
  (5 shorter events, 0.0 us)
Async XLA Ops:
  0.0 2.2 %collective-permute-start = (f32[64,2,8,128]{3,2,1,0:T(8,128)}, f32[64,2,8,128]{3,2,1,0:T(8,128)S(1)}, u32[]{:S(2)}, u32[]{:S(2)}) collective-permute-start(f32[64,2,8,128]{3,2,1,0:T(8,128)} %param.5), channel_id=1, source_target_pairs={{0,8},{8,0},{16,24},{24,16},{1,9},{9,1},{17,25},{25,17},{2,10},{10... | collective-permute-start | bytes 1572872 | tf_op jit(solution)/shard_map/ppermute | solution.py:615
  2.6 15.0 %collective-permute-start.3 = (bf16[1328,128]{1,0:T(8,128)(2,1)S(1)}, bf16[1328,128]{1,0:T(8,128)(2,1)S(1)}, u32[]{:S(2)}, u32[]{:S(2)}) collective-permute-start(bf16[1328,128]{1,0:T(8,128)(2,1)S(1)} %get-tuple-element.28.halo_ref), channel_id=1, source_target_pairs={{0,2},{2,4},{4,6},{6,0},{8,14},{10,8},{12,10},{14,12},{16,18},{18,... | collective-permute-start | bytes 1019912 | tf_op jit(solution)/shard_map/ppermute | solution.py:656
  5.6 2.7 %collective-permute-start.1 = (f32[8,128]{1,0:T(8,128)S(1)}, f32[8,128]{1,0:T(8,128)S(1)}, u32[]{:S(2)}, u32[]{:S(2)}) collective-permute-start(f32[8,128]{1,0:T(8,128)S(1)} %get-tuple-element.29.obs_ref), channel_id=1, source_target_pairs={{0,8},{8,0},{16,24},{24,16},{1,9},{9,1},{17,25},{25,17},{2,10},{10... | collective-permute-start | bytes 12296 | tf_op jit(solution)/shard_map/ppermute | solution.py:646
  8.8 4.8 %collective-permute-start.2 = (f32[168,128]{1,0:T(8,128)S(1)}, f32[168,128]{1,0:T(8,128)S(1)}, u32[]{:S(2)}, u32[]{:S(2)}) collective-permute-start(f32[168,128]{1,0:T(8,128)S(1)} %get-tuple-element.33), channel_id=1, source_target_pairs={{0,1},{1,0},{2,3},{3,2},{4,5},{5,4},{6,7},{7,6},{8,9},{9,8},{10,11... | collective-permute-start | bytes 258056 | tf_op jit(solution)/shard_map/ppermute | solution.py:669
  10.4 7.2 %collective-permute-start.4 = (bf16[112,128]{1,0:T(8,128)(2,1)S(1)}, bf16[112,128]{1,0:T(8,128)(2,1)S(1)}, u32[]{:S(2)}, u32[]{:S(2)}) collective-permute-start(bf16[112,128]{1,0:T(8,128)(2,1)S(1)} %get-tuple-element.38), channel_id=1, source_target_pairs={{0,3},{1,2},{2,5},{3,4},{4,7},{5,6},{6,1},{7,0},{8,15},{9,14},{10,... | collective-permute-start | bytes 86024 | tf_op jit(solution)/shard_map/ppermute | solution.py:670
  19.7 4.7 %collective-permute-start.5 = (bf16[2,128,128]{2,1,0:T(8,128)(2,1)S(1)}, bf16[2,128,128]{2,1,0:T(8,128)(2,1)S(1)}, u32[]{:S(2)}, u32[]{:S(2)}) collective-permute-start(bf16[2,128,128]{2,1,0:T(8,128)(2,1)S(1)} %get-tuple-element.40), channel_id=1, source_target_pairs={{0,1},{1,0},{8,9},{9,8},{16,17},{17,16},{24,25},{25,24},{2,3},{3,2... | collective-permute-start | bytes 196616 | tf_op jit(solution)/shard_map/ppermute | solution.py:692
  20.2 4.3 %collective-permute-start.6 = (bf16[2,128,128]{2,1,0:T(8,128)(2,1)S(1)}, bf16[2,128,128]{2,1,0:T(8,128)(2,1)S(1)}, u32[]{:S(2)}, u32[]{:S(2)}) collective-permute-start(bf16[2,128,128]{2,1,0:T(8,128)(2,1)S(1)} %get-tuple-element.41), channel_id=1, source_target_pairs={{0,16},{1,17},{8,24},{9,25},{16,0},{17,1},{24,8},{25,9},{2,18},{3,... | collective-permute-start | bytes 196616 | tf_op jit(solution)/shard_map/ppermute | solution.py:692
  21.7 5.2 %collective-permute-start.7 = (bf16[2,128,128]{2,1,0:T(8,128)(2,1)S(1)}, bf16[2,128,128]{2,1,0:T(8,128)(2,1)S(1)}, u32[]{:S(2)}, u32[]{:S(2)}) collective-permute-start(bf16[2,128,128]{2,1,0:T(8,128)(2,1)S(1)} %get-tuple-element.42), channel_id=1, source_target_pairs={{0,17},{1,16},{8,25},{9,24},{16,1},{17,0},{24,9},{25,8},{2,19},{3,... | collective-permute-start | bytes 196616 | tf_op jit(solution)/shard_map/ppermute | solution.py:692
  30.6 4.3 %collective-permute-start.8 = (bf16[2,2,64,128]{3,2,1,0:T(8,128)(2,1)S(1)}, bf16[2,2,64,128]{3,2,1,0:T(8,128)(2,1)S(1)}, u32[]{:S(2)}, u32[]{:S(2)}) collective-permute-start(bf16[2,2,64,128]{3,2,1,0:T(8,128)(2,1)S(1)} %get-tuple-element.44), channel_id=1, source_target_pairs={{0,1},{1,0},{8,9},{9,8},{16,17},{17,16},{24,25},{25,24},{2,3},{3,2... | collective-permute-start | bytes 196616 | tf_op jit(solution)/shard_map/ppermute | solution.py:692
  32.2 4.3 %collective-permute-start.9 = (bf16[2,2,64,128]{3,2,1,0:T(8,128)(2,1)S(1)}, bf16[2,2,64,128]{3,2,1,0:T(8,128)(2,1)S(1)}, u32[]{:S(2)}, u32[]{:S(2)}) collective-permute-start(bf16[2,2,64,128]{3,2,1,0:T(8,128)(2,1)S(1)} %get-tuple-element.45), channel_id=1, source_target_pairs={{0,16},{1,17},{8,24},{9,25},{16,0},{17,1},{24,8},{25,9},{2,18},{3,... | collective-permute-start | bytes 196616 | tf_op jit(solution)/shard_map/ppermute | solution.py:692
  32.7 5.2 %collective-permute-start.10 = (bf16[2,2,64,128]{3,2,1,0:T(8,128)(2,1)S(1)}, bf16[2,2,64,128]{3,2,1,0:T(8,128)(2,1)S(1)}, u32[]{:S(2)}, u32[]{:S(2)}) collective-permute-start(bf16[2,2,64,128]{3,2,1,0:T(8,128)(2,1)S(1)} %get-tuple-element.46), channel_id=1, source_target_pairs={{0,17},{1,16},{8,25},{9,24},{16,1},{17,0},{24,9},{25,8},{2,19},{3,... | collective-permute-start | bytes 196616 | tf_op jit(solution)/shard_map/ppermute | solution.py:692
  34.1 3.7 %collective-permute-start.11 = (bf16[2,2,64,128]{3,2,1,0:T(8,128)(2,1)S(1)}, bf16[2,2,64,128]{3,2,1,0:T(8,128)(2,1)S(1)}, u32[]{:S(2)}, u32[]{:S(2)}) collective-permute-start(bf16[2,2,64,128]{3,2,1,0:T(8,128)(2,1)S(1)} %get-tuple-element.43.refs_0_), channel_id=1, source_target_pairs={{0,8},{8,0},{16,24},{24,16},{1,9},{9,1},{17,25},{25,17},{2,10},{10... | collective-permute-start | bytes 196616 | tf_op jit(solution)/shard_map/ppermute | solution.py:702
  34.9 3.0 %collective-permute-start.12 = (bf16[2,2,64,128]{3,2,1,0:T(8,128)(2,1)S(1)}, bf16[2,2,64,128]{3,2,1,0:T(8,128)(2,1)S(1)}, u32[]{:S(2)}, u32[]{:S(2)}) collective-permute-start(bf16[2,2,64,128]{3,2,1,0:T(8,128)(2,1)S(1)} %collective-permute-done.8.refs_1_), channel_id=1, source_target_pairs={{0,8},{8,0},{16,24},{24,16},{1,9},{9,1},{17,25},{25,17},{2,10},{10... | collective-permute-start | bytes 196616 | tf_op jit(solution)/shard_map/ppermute | solution.py:702
  36.4 1.5 %collective-permute-start.13 = (bf16[2,2,64,128]{3,2,1,0:T(8,128)(2,1)S(1)}, bf16[2,2,64,128]{3,2,1,0:T(8,128)(2,1)S(1)}, u32[]{:S(2)}, u32[]{:S(2)}) collective-permute-start(bf16[2,2,64,128]{3,2,1,0:T(8,128)(2,1)S(1)} %collective-permute-done.9.refs_2_), channel_id=1, source_target_pairs={{0,8},{8,0},{16,24},{24,16},{1,9},{9,1},{17,25},{25,17},{2,10},{10... | collective-permute-start | bytes 196616 | tf_op jit(solution)/shard_map/ppermute | solution.py:702
  37.9 1.3 %collective-permute-start.14 = (bf16[2,2,64,128]{3,2,1,0:T(8,128)(2,1)S(1)}, bf16[2,2,64,128]{3,2,1,0:T(8,128)(2,1)S(1)}, u32[]{:S(2)}, u32[]{:S(2)}) collective-permute-start(bf16[2,2,64,128]{3,2,1,0:T(8,128)(2,1)S(1)} %collective-permute-done.10.refs_3_), channel_id=1, source_target_pairs={{0,8},{8,0},{16,24},{24,16},{1,9},{9,1},{17,25},{25,17},{2,10},{10... | collective-permute-start | bytes 196616 | tf_op jit(solution)/shard_map/ppermute | solution.py:702

commit v3 on v2

--- a/solution.py
+++ b/solution.py
@@ -1,5 +1,4 @@
 import functools
-import math
 
 import jax
 import jax.numpy as jnp
@@ -7,6 +6,7 @@
 from jax.experimental import pallas as pl
 from jax.experimental.pallas import tpu as pltpu
 from jax.sharding import PartitionSpec as P
+
 
 ROOT_STEPS = 4
 
@@ -111,7 +111,7 @@
     frob = jnp.sqrt(jnp.sum(gram * gram, axis=(1, 2)))
     current = gram / frob[:, None, None]
     root = jnp.broadcast_to(identity, gram.shape)
-    for step in range(ROOT_STEPS):
+    for _ in range(ROOT_STEPS):
         middle = 1.5 * identity - 0.5 * jnp.einsum("pab,pbc->pac", root, current, precision=highest)
         current = jnp.einsum("pab,pbc->pac", current, middle, precision=highest)
         root = jnp.einsum("pab,pbc->pac", middle, root, precision=highest)
@@ -248,7 +248,8 @@
         self.wind_rows = 2 * layers * HALO
         self.side_rows = layers * 2 * HALO * OCTET
         self.corner_rows = layers * HALO * OCTET
-        self.obs_at = self.side_rows + 2 * layers * rows
+        self.piece_rows = layers * LANES
+        self.obs_rows = 2 * OCTET
 
     def field_at(self, layer, j):
         return (layer * DOMAIN + j) * EXTENT
@@ -263,14 +264,15 @@
     return jnp.concatenate(parts, axis=0).T
 
 
-def wind_scale(s, odd, value):
-    sign = jnp.where(odd == 1, -0.5, 0.5)
+def wind_scale(odd, value):
+    half = 0.5 / diffusion
+    sign = jnp.where(odd == 1, -half, half)
     row = lax.broadcasted_iota(jnp.int32, value.shape, 0)
-    return value * jnp.where(row < value.shape[0] // 2, sign, 0.5)
+    return value * jnp.where(row < value.shape[0] // 2, sign, half)
 
 
 def fetch_kernel(
-    s, prior_ref, wind_ref, cells_ref, values_ref, errors_ref, own_ref, wind_out_ref, obs_ref,
+    prior_ref, wind_ref, cells_ref, values_ref, errors_ref, own_ref, wind_out_ref, obs_ref,
     cells_vmem, values_vmem, errors_vmem, sems,
 ):
     copies = [
@@ -309,7 +311,7 @@
         for j in range(HALO):
             row = block * s.rows + tile_row(odd, 2 * HALO + j)
             rows_ref[pl.ds(block * HALO + j, 1), :] = wind_ref[pl.ds(row, 1), :]
-    for i, part in enumerate(split_three(wind_scale(s, odd, rows_ref[...]))):
+    for i, part in enumerate(split_three(wind_scale(odd, rows_ref[...]))):
         out_ref[pl.ds(s.halo_rows + i * s.wind_rows, s.wind_rows), :] = part
 
 
@@ -324,7 +326,7 @@
         store(second, both[:, LANES:])
 
 
-def pack_edges_kernel(s, own_ref, sib_ref, wind_ref, halo_ref, obs_ref, _, field_ref, side_ref, corner_ref, winds_ref):
+def pack_edges_kernel(s, own_ref, sib_ref, wind_ref, halo_ref, _, field_ref, side_ref, corner_ref, winds_ref):
     odd = lax.rem(lax.axis_index("mem"), 2)
     for layer in range(s.layers):
         for j in range(HALO, 2 * HALO):
@@ -339,9 +341,8 @@
         to, at = layer * HALO * OCTET, (layer * 2 * HALO + HALO) * OCTET
         corner_ref[pl.ds(to, HALO * OCTET), :] = side_ref[pl.ds(at, HALO * OCTET), :].astype(jnp.bfloat16)
     corner_ref[pl.ds(s.corner_rows, 3 * s.wind_rows), :] = halo_ref[pl.ds(s.halo_rows, 3 * s.wind_rows), :]
-    scaled = wind_scale(s, odd, wind_ref[...])
+    scaled = wind_scale(odd, wind_ref[...])
     side_ref[pl.ds(s.side_rows, 2 * s.layers * s.rows), :] = scaled
-    side_ref[pl.ds(s.obs_at, OCTET), :] = obs_ref[...]
 
     def store(row, value):
         at = s.wind_at(row // s.rows // s.layers, row // s.rows % s.layers, domain_row(odd, row % s.rows))
@@ -369,7 +370,8 @@
 
 
 def evaluate(s, field_ref, winds_ref, from_ref, stage, start, wanted, emit):
-    factor, share = STAGE_FACTORS[stage], 0.2 / s.layers
+    factor, share = STAGE_FACTORS[stage] * diffusion, coupling / s.layers / diffusion
+    own_share = 4.0 + coupling / diffusion - share
     centre = {}
     for j in range(wanted[0] - 1, wanted[1] + 1):
         for layer in range(s.layers):
@@ -383,23 +385,23 @@
             along = winds_ref[pl.ds(s.wind_at(0, layer, j) + start, OCTET), :]
             across = winds_ref[pl.ds(s.wind_at(1, layer, j) + start, OCTET), :]
             total = along * (south - north) + across * (west - east)
-            total = total + 0.1 * ((north + south) + (east + west))
-            total = total + ((share - 0.6) * centre[layer, j] + share * others)
-            base = field_ref[pl.ds(at, OCTET), :]
-            emit(layer, j, base + (total if factor == 1.0 else factor * total))
+            total = total + ((north + south) + (east + west))
+            total = total + ((others if share == 1.0 else share * others) - own_share * centre[layer, j])
+            emit(layer, j, field_ref[pl.ds(at, OCTET), :] + factor * total)
 
 
 def run_stage(s, field_ref, winds_ref, from_ref, to_ref, stage, wanted):
     def step(i, carry):
-        start = HALO + OCTET * i
-
-        def emit(layer, j, value):
-            to_ref[pl.ds(s.field_at(layer, j) + start, OCTET), :] = value
-
-        evaluate(s, field_ref, winds_ref, from_ref, stage, start, wanted, emit)
+        for k in range(2):
+            start = 2 * OCTET * i + OCTET * k
+
+            def emit(layer, j, value):
+                to_ref[pl.ds(s.field_at(layer, j) + start, OCTET), :] = value
+
+            evaluate(s, field_ref, winds_ref, from_ref, stage, start, wanted, emit)
         return carry
 
-    lax.fori_loop(0, (LANES + 2 * HALO) // OCTET, step, 0)
+    lax.fori_loop(0, EXTENT // (2 * OCTET), step, 0)
 
 
 def inner_kernel(s, _, __, side_ref, field_ref, winds_ref, first_ref, second_ref):
@@ -420,7 +422,7 @@
 
 
 def forecast_kernel(
-    s, _, __, ___, ____, halo_ref, corner_ref,
+    s, _, __, ___, ____, halo_ref, corner_ref, obs_ref,
     out0_ref, out1_ref, out2_ref, out3_ref, field_ref, winds_ref, first_ref, second_ref,
 ):
     mem = lax.axis_index("mem")
@@ -457,6 +459,8 @@
         wanted = (1 + stage, HALO + 1 + stage)
         run_stage(s, field_ref, winds_ref, refs[stage], refs[stage + 1], stage, wanted)
 
+    for i, part in enumerate(split_three(obs_ref[...])):
+        out1_ref[pl.ds(s.piece_rows + i * s.obs_rows, s.obs_rows), :] = part
     swap_one = jnp.bitwise_xor(jnp.bitwise_and(place, 1), odd) == 1
     swap_two = jnp.bitwise_xor(place // 2, odd) == 1
     outs = (out0_ref, out1_ref, out2_ref, out3_ref)
@@ -476,7 +480,7 @@
             rows = [jnp.where(swap_one, rows[t ^ 1], rows[t]) for t in range(HALO)]
             rows = [jnp.where(swap_two, rows[t ^ 2], rows[t]) for t in range(HALO)]
             for d, out_ref in enumerate(outs):
-                out_ref[layer, pl.ds(at, 2 * OCTET), :] = rows[d]
+                out_ref[pl.ds(layer * LANES + at, 2 * OCTET), :] = rows[d]
         return carry
 
     lax.fori_loop(0, LANES // (2 * OCTET), last_step, 0)
@@ -486,35 +490,98 @@
     return lax.dot_general(a, b, (contract, ((), ())), preferred_element_type=jnp.float32)
 
 
-def dot_three(a, b, contract=((1,), (0,))):
-    (a_high, a_low), (b_high, b_low) = a, b
-    return dot(a_high, b_low, contract) + dot(a_low, b_high, contract) + dot(a_high, b_high, contract)
-
-
-def analysis_kernel(s, total_members, piece0_ref, piece1_ref, piece2_ref, piece3_ref, obs_ref, side_ref, out0_ref, out1_ref, out2_ref, out3_ref):
+def beside(*parts):
+    return jnp.concatenate(parts, axis=1)
+
+
+def below(*parts):
+    return jnp.concatenate(parts, axis=0)
+
+
+def dot_split(a, b):
+    (a_high, a_low), (b_high, b_low) = split_two(a), split_two(b)
+    row = beside(b_high, b_low)
+    both = dot(beside(a_high, a_low), below(row, row), ((1,), (0,)))
+    return both[:, : b.shape[1]] + both[:, b.shape[1] :]
+
+
+def root_parts(product, vector, total_members):
+    count = product.shape[0]
+    size = (count, count)
+    diagonal = lax.broadcasted_iota(jnp.int32, size, 0) == lax.broadcasted_iota(jnp.int32, size, 1)
+
+    def total(x):
+        return jnp.sum(jnp.sum(x, axis=0, keepdims=True), axis=1, keepdims=True)
+
+    def plus(x, scalar):
+        return jnp.where(diagonal, x + scalar, x)
+
+    def twice(matrix, column):
+        once = jnp.sum(matrix * column, axis=0, keepdims=True)
+        return jnp.sum(matrix * once, axis=1, keepdims=True)
+
+    least = total_members - 1.0
+    trace = total(jnp.where(diagonal, product, 0.0))
+    square = total(product * product) + (2.0 * least) * trace + least * least * total_members
+    inverse = lax.rsqrt(square)
+    b = product * inverse
+    x = least * inverse
+    z = jnp.ones_like(x)
+    m = 1.5 - 0.5 * x
+    middle = plus(-0.5 * b, m)
+    y = plus((0.25 * x - m) * b + 0.25 * dot_split(b, b), -x * m)
+    near = plus(m * m * b + dot_split(y, b), m * m * x)
+    slope = plus(y, m * m)
+    x, z = x * m * m, m
+    root = middle
+    vector = twice(middle, vector)
+    root_slope = jnp.where(diagonal, -0.5, 0.0)
+    for step in range(1, ROOT_STEPS):
+        m = 1.5 - 0.5 * x
+        middle = plus(-0.5 * near, 1.5)
+        root_slope = m * root_slope - 0.5 * dot_split(slope, root)
+        vector = twice(middle, vector)
+        z = m * z
+        if step < ROOT_STEPS - 1:
+            root = dot_split(middle, root)
+            rest = plus(near, -x)
+            y = dot_split(near, plus(0.25 * rest, -m))
+            slope = m * m * slope + dot_split(y, slope)
+            near = m * m * near + dot_split(y, rest)
+            x = x * m * m
+    return inverse, z, root_slope, vector
+
+
+def analysis_kernel(
+    s, total_members, piece0_ref, piece1_ref, piece2_ref, piece3_ref, obs_ref,
+    send_ref, perturbation_ref, weights_ref, mean_ref,
+):
     mem, side = lax.axis_index("mem"), lax.axis_index("gy")
-    outs = (out0_ref, out1_ref, out2_ref, out3_ref)
     pieces = (piece0_ref, piece1_ref, piece2_ref, piece3_ref)
     width = 2 * LANES
     cells_total = s.layers * width
-    inverse = 1.0 / total_members
-    members = jnp.concatenate(
-        [
-            jnp.concatenate([pieces[2 * dx + dy][layer] for layer in range(s.layers) for dy in range(2)], axis=0)
+    inverse_count = 1.0 / total_members
+    members = beside(
+        *(
+            below(*(pieces[2 * dx + dy][layer * LANES : (layer + 1) * LANES] for layer in range(s.layers) for dy in range(2)))
             for dx in range(2)
-        ],
-        axis=1,
-    )
-    mean_row = dot(jnp.ones((OCTET, total_members), jnp.bfloat16), members, ((1,), (1,)))[0:1] * inverse
-    mean = dot(members, jnp.ones((total_members, LANES), jnp.bfloat16), ((1,), (0,))) * inverse
-    perturbation = jnp.concatenate(
-        [(members[:, i : i + LANES].astype(jnp.float32) - mean).astype(jnp.bfloat16) for i in range(0, total_members, LANES)],
-        axis=1,
-    )
+        )
+    )
+    mean_row = dot(jnp.ones((OCTET, total_members), jnp.bfloat16), members, ((1,), (1,))) * inverse_count
+    mean = dot(members, jnp.ones((total_members, LANES), jnp.bfloat16), ((1,), (0,))) * inverse_count
+    perturbation = beside(
+        *(
+            (members[:, i : i + LANES].astype(jnp.float32) - mean).astype(jnp.bfloat16)
+            for i in range(0, total_members, LANES)
+        )
+    )
+    perturbation_ref[...] = perturbation
+    mean_ref[...] = mean_row
 
     count = obs_ref.shape[1]
+    far = [piece1_ref[pl.ds(s.piece_rows + i * s.obs_rows, s.obs_rows), :].astype(jnp.float32) for i in range(3)]
     mine = lax.rem(mem, 2) == side
-    obs = padded_rows(jnp.where(mine, obs_ref[...], side_ref[pl.ds(s.obs_at, OCTET), :])).T
+    obs = padded_rows(jnp.where(mine, obs_ref[...], far[0] + far[1] + far[2])).T
     cells = obs[:, 0:1].astype(jnp.int32)
     values, errors = obs[:, 1:2], obs[:, 2:3]
     column = jnp.bitwise_and(cells, width - 1)
@@ -523,7 +590,7 @@
     index = layer_of * width + half * LANES + jnp.bitwise_and(column, LANES - 1)
     chosen = jnp.where(lax.broadcasted_iota(jnp.int32, (count, cells_total), 1) == index, 1.0, 0.0)
     picked = dot(chosen.astype(jnp.bfloat16), members, ((1,), (0,)))
-    base = jnp.sum(picked, axis=1, keepdims=True) * inverse
+    base = jnp.sum(picked, axis=1, keepdims=True) * inverse_count
     offset = column.astype(jnp.float32) - 0.5 * (width - 1)
     weight = jnp.zeros_like(values)
     for shift in (-1, 0, 1):
@@ -532,48 +599,63 @@
     scale = jnp.sqrt(weight)
     scaled = (picked - base) * scale
     innovation = (values - base) * scale
-    parts = split_two(scaled)
+
+    high, low = split_two(scaled)
+    quarters = dot(below(high, low), below(high, low), ((1,), (1,)))
+    halves = quarters[:count] + quarters[count:]
+    inverse, z, slope, twice = root_parts(halves[:, :count] + halves[:, count:], innovation, total_members)
+    slope_high, slope_low = split_two(slope * inverse)
+    both = beside(slope_high, slope_low)
+    carried = dot(both, below(high, high), ((1,), (0,))) + dot(both, below(low, low), ((1,), (0,)))
+    carried_high, carried_low = split_two(carried)
+    turned = below(high, low)
+    spread_part = dot(turned, below(carried_high, carried_high), ((0,), (0,)))
+    spread_part = spread_part + dot(turned, below(carried_low, carried_low), ((0,), (0,)))
+    mean_weights = jnp.sum(scaled * twice, axis=0, keepdims=True) * inverse
     size = (total_members, total_members)
     diagonal = lax.broadcasted_iota(jnp.int32, size, 0) == lax.broadcasted_iota(jnp.int32, size, 1)
-    identity = jnp.where(diagonal, 1.0, 0.0)
-    gram = dot_three(parts, parts, ((0,), (0,))) + (total_members - 1.0) * identity
-    square = jnp.sum(jnp.sum(gram * gram, axis=0, keepdims=True), axis=1, keepdims=True)
-    frob = jnp.sqrt(square)
-    current = gram / frob
-    middle = 1.5 * identity - 0.5 * current
-    root = middle
-    for step in range(1, ROOT_STEPS):
-        middle_parts = split_two(middle)
-        current = dot_three(split_two(current), middle_parts)
-        root_parts = split_two(root)
-        middle = 1.5 * identity - 0.5 * dot_three(root_parts, split_two(current))
-        root = dot_three(split_two(middle), root_parts)
-    projected = jnp.sum(scaled * innovation, axis=0, keepdims=True)
-    once = jnp.sum(root * projected, axis=1, keepdims=True)
-    mean_weights = jnp.sum(root * once, axis=0, keepdims=True) / frob
-    weights = (math.sqrt(total_members - 1.0) * root / jnp.sqrt(frob) + mean_weights).astype(jnp.bfloat16)
+    full = jnp.where(diagonal, spread_part + z, spread_part)
+    weights = (full * jnp.sqrt((total_members - 1.0) * inverse) + mean_weights).astype(jnp.bfloat16)
+    weights_ref[...] = weights
     for dx in range(2):
-        for part in range(2):
-            rows = slice((2 * dx + part) * s.local, (2 * dx + part + 1) * s.local)
-            block = dot(weights[rows], perturbation, ((1,), (1,))) + mean_row
-            block = block.astype(jnp.bfloat16)
-            for dy in range(2):
-                for layer in range(s.layers):
-                    at = (layer * 2 + dy) * LANES
-                    outs[2 * dx + dy][part, layer] = block[:, at : at + LANES]
+        block = answer_rows(s, weights, perturbation, mean_row, dx, 1)
+        for dy in range(2):
+            for layer in range(s.layers):
+                at = (layer * 2 + dy) * LANES
+                send_ref[2 * dx + dy, layer] = block[:, at : at + LANES]
+
+
+def answer_rows(s, weights, perturbation, mean_row, dx, part):
+    first = (2 * dx + part) * s.local
+    block = dot(weights[first : first + s.local], perturbation, ((1,), (1,))) + mean_row[0:1]
+    return block.astype(jnp.bfloat16)
+
+
+def answer_kernel(s, perturbation_ref, weights_ref, mean_ref, *outs):
+    for dx in range(2):
+        block = answer_rows(s, weights_ref[...], perturbation_ref[...], mean_ref[...], dx, 0)
+        for dy in range(2):
+            for layer in range(s.layers):
+                at = (layer * 2 + dy) * LANES
+                outs[2 * dx + dy][0, layer] = block[:, at : at + LANES]
+
+
+def join_kernel(received_ref, *refs):
+    for d in range(4):
+        refs[4 + d][1] = received_ref[d]
 
 
 def place_rows_kernel(s, *refs):
-    pieces, passed, out_ref, rows_ref = refs[:4], refs[4:8], refs[8], refs[9]
+    pieces, out_ref, rows_ref = refs[:4], refs[4], refs[5]
     mem = lax.axis_index("mem")
     odd = lax.rem(mem, 2)
     place = (mem // 2) * 2 + lax.axis_index("gy")
     for d in range(4):
-        for ref, part, parity in ((pieces[d], 0, odd), (passed[d], 1, 1 - odd)):
+        for part, parity in ((0, odd), (1, 1 - odd)):
             row = 4 * parity + jnp.bitwise_xor(place, d)
             for layer in range(s.layers):
                 for octet in range(0, s.local // OCTET, 2):
-                    value = ref[part, layer, octet * OCTET : (octet + 2) * OCTET, :].astype(jnp.float32)
+                    value = pieces[d][part, layer, octet * OCTET : (octet + 2) * OCTET, :].astype(jnp.float32)
                     start = octet * OCTET * s.per_member + layer * s.rows + row
                     rows_ref[pl.ds(start, 2 * OCTET, stride=s.per_member), :] = value
     out_ref[...] = rows_ref[...].astype(jnp.bfloat16).reshape(out_ref.shape)
@@ -610,17 +692,16 @@
         ((m * n_gx + z) * 2 + y, (m * n_gx + (z + step(m)) % n_gx) * 2 + 1 - y)
         for m in range(4) for z in range(n_gx) for y in range(2)
     ]
-    owners = [((x * 2 + y) * 2 + c, (x * 2 + c) * 2 + y) for x in range(2) for c in range(2) for y in range(2)]
 
     sib = lax.ppermute(prior_sample_set, "mem", pair).reshape(local * layers * rows, columns)
     count = observed_cells.shape[-1]
     vmem, hbm = pl.BlockSpec(memory_space=pltpu.VMEM), pl.BlockSpec(memory_space=pltpu.HBM)
     own, wind, obs = pl.pallas_call(
-        functools.partial(fetch_kernel, s),
+        fetch_kernel,
         out_shape=(
             shaped((local * layers * rows, columns), f32),
             shaped((2 * layers * rows, columns), f32),
-            shaped((OCTET, count), f32),
+            shaped((2 * OCTET, count), f32),
         ),
         in_specs=[hbm] * 5,
         out_specs=(vmem, vmem, vmem),
@@ -658,13 +739,13 @@
         functools.partial(pack_edges_kernel, s),
         (
             field_shape,
-            shaped((s.obs_at + OCTET, LANES), f32),
+            shaped((s.side_rows + 2 * layers * rows, LANES), f32),
             shaped((s.corner_rows + 3 * s.wind_rows, LANES), bf16),
             winds_shape,
         ),
         [],
-        own, sib, wind, halo_out, obs_sib, field,
-        aliases={5: 0},
+        own, sib, wind, halo_out, field,
+        aliases={4: 0},
     )
     side = lax.ppermute(side_out, "gy", across)
     corner = lax.ppermute(corner_out, ("mem", "gx", "gy"), diagonal)
@@ -675,12 +756,13 @@
         field, winds, side,
         aliases={0: 0, 1: 1},
     )
-    piece = shaped((layers, LANES, s.members), bf16)
+    piece = shaped((s.piece_rows, s.members), bf16)
+    piece_obs = shaped((s.piece_rows + 3 * s.obs_rows, s.members), bf16)
     *pieces, _, _, _, _ = vmem_call(
         functools.partial(forecast_kernel, s),
-        (piece, piece, piece, piece, field_shape, winds_shape, field_shape, field_shape),
+        (piece, piece_obs, piece, piece, field_shape, winds_shape, field_shape, field_shape),
         [],
-        field, winds, first, second, halo, corner,
+        field, winds, first, second, halo, corner, obs_sib,
         aliases={0: 4, 1: 5, 2: 6, 3: 7},
     )
 
@@ -689,27 +771,41 @@
         return [((m * 2 + y), ((m ^ (2 * dx)) * 2 + (y ^ dy))) for m in range(4) for y in range(2)]
 
     def exchange(parts):
-        return [parts[0]] + [lax.ppermute(parts[d], ("mem", "gy"), flip(d)) for d in range(1, 4)]
-
+        arrived = [parts[0]]
+        for d in range(1, 4):
+            arrived.append(lax.ppermute(parts[d], ("mem", "gy"), flip(d)))
+        return arrived
+
+    total = 4 * local
+    send, perturbation, weights, mean = vmem_call(
+        functools.partial(analysis_kernel, s, total),
+        (
+            shaped((4, layers, local, LANES), bf16),
+            shaped((layers * 2 * LANES, total), bf16),
+            shaped((total, total), bf16),
+            shaped((OCTET, layers * 2 * LANES), f32),
+        ),
+        [],
+        *exchange(pieces), obs,
+    )
+    received = lax.ppermute(send, "mem", pair)
     answer = shaped((2, layers, local, LANES), bf16)
-    outgoing = vmem_call(
-        functools.partial(analysis_kernel, s, 4 * local),
-        (answer, answer, answer, answer),
-        [],
-        *exchange(pieces), obs, side,
-    )
-    returned = exchange(outgoing)
-    passed = [lax.ppermute(part, "mem", pair) for part in returned]
+    answers = vmem_call(
+        functools.partial(answer_kernel, s), (answer, answer, answer, answer), [], perturbation, weights, mean
+    )
+    answers = vmem_call(
+        join_kernel, (answer, answer, answer, answer), [], received, *answers, aliases={1 + d: d for d in range(4)}
+    )
     return vmem_call(
         functools.partial(place_rows_kernel, s),
         shaped((local, layers, rows, columns), bf16),
         [((local * layers * rows, LANES), f32)],
-        *returned, *passed,
+        *exchange(answers),
     )
 
 
 def on_device(prior_sample_set, flow_speeds, observed_cells, observed_values, error_variance):
-    local, layers, rows, columns = prior_sample_set.shape
+    local, _, rows, columns = prior_sample_set.shape
     suits = (
         lax.axis_size("mem") == 4
         and lax.axis_size("gy") == 2

time: 40.3 us -> 39 us (0.968)
  Pallas kernels: 10.4 us -> 8.92 us
    ppermute x1, waiting for transfers between devices: 2.35 us -> 5.63 us  [on_device_tile(): corner = lax.ppermute(corner_out, ('mem', 'gx', 'gy'), diagonal)]
    ppermute x1, waiting for transfers between devices: 3.26 us -> 1.21 us  [on_device_tile(): side = lax.ppermute(side_out, 'gy', across)]
    ppermute x1, starting transfers between devices: 1.88 us -> 0.2 us  [on_device_tile(): obs_sib = lax.ppermute(obs, 'mem', pair)]
    ppermute x1, starting transfers between devices: 0.01 us -> 1.52 us  [on_device_tile(): corner = lax.ppermute(corner_out, ('mem', 'gx', 'gy'), diagonal)]
    pallas_call x6 -> x8, Pallas kernels: 9.21 us -> 7.77 us  [vmem_call(): pl.pallas_call(kernel, out_shape=outs, in_specs=[spec] * len(args), out_s...]
    ppermute x1, waiting for transfers between devices: 0.82 us -> 0.01 us  [on_device_tile(): obs_sib = lax.ppermute(obs, 'mem', pair)]
    ppermute x10 -> x7, waiting for transfers between devices: 8.63 us -> 8.45 us  [the longest x6 7.4 us: exchange(): arrived.append(lax.ppermute(parts[d], ('mem', 'gy'), flip(d)))]
    ppermute x10 -> x7, starting transfers between devices: 7.11 us -> 7.18 us  [the longest x6 7.11 us: exchange(): arrived.append(lax.ppermute(parts[d], ('mem', 'gy'), flip(d)))]
  transfers between devices with their start and end apart: 15 -> 12, of which waited for: 11 -> 9; matrix products, arithmetic and copies ran while one was open for 0% -> 0% of each run, Pallas kernels for 8% -> 9%
where the time goes in v3:
time: 39 us; the launch traced here: 38.8 us
  waiting for transfers between devices  15.9 us (41%)
  starting transfers between devices  13.9 us (36%)
  Pallas kernels  8.92 us (23%)
    pallas_call x8, Pallas kernels, vmem_call(): pl.pallas_call(kernel, out_shape=outs, in_specs=[spec] * len(args), out_s...  7.77 us
    ppermute x6, waiting for transfers between devices, exchange(): arrived.append(lax.ppermute(parts[d], ('mem', 'gy'), flip(d)))  7.4 us
    ppermute x6, starting transfers between devices, exchange(): arrived.append(lax.ppermute(parts[d], ('mem', 'gy'), flip(d)))  7.11 us
    ppermute x1, waiting for transfers between devices, on_device_tile(): corner = lax.ppermute(corner_out, ('mem', 'gx', 'gy'), diagonal)  5.63 us
    ppermute x1, starting transfers between devices, on_device_tile(): halo = lax.ppermute(halo_out, ('mem', 'gx'), along)  2.99 us
    ppermute x1, starting transfers between devices, on_device_tile(): side = lax.ppermute(side_out, 'gy', across)  1.58 us
    ppermute x1, starting transfers between devices, on_device_tile(): corner = lax.ppermute(corner_out, ('mem', 'gx', 'gy'), diagonal)  1.52 us
    ppermute x1, waiting for transfers between devices, on_device_tile(): side = lax.ppermute(side_out, 'gy', across)  1.21 us
  transfers between devices with their start and end apart: 12, of which 9 were waited for; matrix products, arithmetic and copies ran while one was open for 0% of the time, Pallas kernels for 9%

profile of v3, /device:TPU:0, one launch (start us, length us, event | category | flops | bytes accessed | tf_op | source)
XLA Modules:
  0.0 38.8 jit_solution(11844141001347990142)
XLA Ops:
  0.0 0.5 %collective-permute-start = (f32[64,2,8,128]{3,2,1,0:T(8,128)}, f32[64,2,8,128]{3,2,1,0:T(8,128)S(1)}, u32[]{:S(2)}, u32[]{:S(2)}) collective-permute-start(f32[64,2,8,128]{3,2,1,0:T(8,128)} %param.5), channel_id=1, source_target_pairs={{0,8},{8,0},{16,24},{24,16},{1,9},{9,1},{17,25},{25,17},{2,10},{10... | collective-permute-start | bytes 1572872 | tf_op jit(solution)/shard_map/ppermute | solution.py:696
  0.5 1.1 %shard_map.55 = (f32[1024,128]{1,0:T(8,128)S(1)}, f32[32,128]{1,0:T(8,128)S(1)}, f32[16,128]{1,0:T(8,128)S(1)}) custom-call(f32[1024,128]{1,0:T(8,128)} %bitcast.8, f32[32,128]{1,0:T(8,128)} %bitcast.9, s32[1,128]{1,0:T(1,128)} %bitcast.10, f32[1,128]{1,0:T(1,128)} %bitcast.11, f32[1,128]{1,0:T(1,128)} %bitcast.12), custom_call_target="tpu_custom_call" | custom-call | tf_op jit(solution)/shard_map/pallas_call | solution.py:699
  1.7 0.6 %collective-permute-done = f32[64,2,8,128]{3,2,1,0:T(8,128)S(1)} collective-permute-done((f32[64,2,8,128]{3,2,1,0:T(8,128)}, f32[64,2,8,128]{3,2,1,0:T(8,128)S(1)}, u32[]{:S(2)}, u32[]{:S(2)}) %collective-permute-start) | collective-permute-done | bytes 524320 | tf_op jit(solution)/shard_map/ppermute | solution.py:696
  2.2 0.3 shard_map.56
  2.6 3.0 %collective-permute-start.2 = (bf16[1328,128]{1,0:T(8,128)(2,1)S(1)}, bf16[1328,128]{1,0:T(8,128)(2,1)S(1)}, u32[]{:S(2)}, u32[]{:S(2)}) collective-permute-start(bf16[1328,128]{1,0:T(8,128)(2,1)S(1)} %get-tuple-element.36.halo_ref), channel_id=1, source_target_pairs={{0,2},{2,4},{4,6},{6,0},{8,14},{10,8},{12,10},{14,12},{16,18},{18,... | collective-permute-start | bytes 1019912 | tf_op jit(solution)/shard_map/ppermute | solution.py:737
  5.6 0.5 %shard_map.57 = (f32[3456,128]{1,0:T(8,128)S(1)}, f32[160,128]{1,0:T(8,128)S(1)}, bf16[112,128]{1,0:T(8,128)(2,1)S(1)}, f32[6912,128]{1,0:T(8,128)S(1)}) custom-call(f32[1024,128]{1,0:T(8,128)S(1)} %get-tuple-element.34.own_ref, f32[1024,128]{1,0:T(8,128)S(1)} %bitcast.7, f32[32,128]{1,0:T(8,128)S(1)} %get-tuple-element.35.wind_ref, ...), custom_call_target="tpu_custom_call", output_to_operand_aliasing={{0}: (4, {})} | custom-call | tf_op jit(solution)/shard_map/pallas_call | solution.py:666
  6.1 1.6 %collective-permute-start.1 = (f32[160,128]{1,0:T(8,128)S(1)}, f32[160,128]{1,0:T(8,128)S(1)}, u32[]{:S(2)}, u32[]{:S(2)}) collective-permute-start(f32[160,128]{1,0:T(8,128)S(1)} %get-tuple-element.40), channel_id=1, source_target_pairs={{0,1},{1,0},{2,3},{3,2},{4,5},{5,4},{6,7},{7,6},{8,9},{9,8},{10,11... | collective-permute-start | bytes 245768 | tf_op jit(solution)/shard_map/ppermute | solution.py:750
  7.7 1.5 %collective-permute-start.3 = (bf16[112,128]{1,0:T(8,128)(2,1)S(1)}, bf16[112,128]{1,0:T(8,128)(2,1)S(1)}, u32[]{:S(2)}, u32[]{:S(2)}) collective-permute-start(bf16[112,128]{1,0:T(8,128)(2,1)S(1)} %get-tuple-element.45), channel_id=1, source_target_pairs={{0,3},{1,2},{2,5},{3,4},{4,7},{5,6},{6,1},{7,0},{8,15},{9,14},{10,... | collective-permute-start | bytes 86024 | tf_op jit(solution)/shard_map/ppermute | solution.py:751
  9.2 0.2 collective-permute-start.4
  9.4 1.2 %collective-permute-done.1.side_ref = f32[160,128]{1,0:T(8,128)S(1)} collective-permute-done((f32[160,128]{1,0:T(8,128)S(1)}, f32[160,128]{1,0:T(8,128)S(1)}, u32[]{:S(2)}, u32[]{:S(2)}) %collective-permute-start.1) | collective-permute-done | bytes 81952 | tf_op jit(solution)/shard_map/ppermute | solution.py:750
  10.6 1.3 %shard_map.58 = (f32[3456,128]{1,0:T(8,128)S(1)}, f32[6912,128]{1,0:T(8,128)S(1)}, f32[3456,128]{1,0:T(8,128)S(1)}, f32[3456,128]{1,0:T(8,128)S(1)}) custom-call(f32[3456,128]{1,0:T(8,128)S(1)} %get-tuple-element.38._, f32[6912,128]{1,0:T(8,128)S(1)} %get-tuple-element.39.__, ...), custom_call_target="tpu_custom_call", output_to_operand_aliasing={{0}: (0, {}), {1}: (1, {})} | custom-call | tf_op jit(solution)/shard_map/pallas_call | solution.py:666
  12.0 0.0 collective-permute-done.4.obs_ref
  12.0 5.6 %collective-permute-done.3.corner_ref = bf16[112,128]{1,0:T(8,128)(2,1)S(1)} collective-permute-done((bf16[112,128]{1,0:T(8,128)(2,1)S(1)}, bf16[112,128]{1,0:T(8,128)(2,1)S(1)}, u32[]{:S(2)}, u32[]{:S(2)}) %collective-permute-start.3) | collective-permute-done | bytes 28704 | tf_op jit(solution)/shard_map/ppermute | solution.py:751
  17.6 0.0 collective-permute-done.2.halo_ref
  17.6 1.8 %shard_map.59 = (bf16[256,128]{1,0:T(8,128)(2,1)S(1)}, bf16[304,128]{1,0:T(8,128)(2,1)S(1)}, bf16[256,128]{1,0:T(8,128)(2,1)S(1)}, bf16[256,128]{1,0:T(8,128)(2,...) custom-call(f32[3456,128]{1,0:T(8,128)S(1)} %get-tuple-element.41._,, ...), custom_call_target="tpu_custom_call", output_to_operand_aliasing={{4}: (0, {}), {5}: (1, {}), {6}: (2, {}), {7}: (3, {})} | custom-call | tf_op jit(solution)/shard_map/pallas_call | solution.py:666
  19.4 0.6 %collective-permute-start.5 = (bf16[304,128]{1,0:T(8,128)(2,1)S(1)}, bf16[304,128]{1,0:T(8,128)(2,1)S(1)}, u32[]{:S(2)}, u32[]{:S(2)}) collective-permute-start(bf16[304,128]{1,0:T(8,128)(2,1)S(1)} %get-tuple-element.48), channel_id=1, source_target_pairs={{0,1},{1,0},{8,9},{9,8},{16,17},{17,16},{24,25},{25,24},{2,3},{3,2... | collective-permute-start | bytes 233480 | tf_op jit(solution)/shard_map/ppermute | solution.py:776
  20.0 1.5 %collective-permute-start.6 = (bf16[256,128]{1,0:T(8,128)(2,1)S(1)}, bf16[256,128]{1,0:T(8,128)(2,1)S(1)}, u32[]{:S(2)}, u32[]{:S(2)}) collective-permute-start(bf16[256,128]{1,0:T(8,128)(2,1)S(1)} %get-tuple-element.49), channel_id=1, source_target_pairs={{0,16},{1,17},{8,24},{9,25},{16,0},{17,1},{24,8},{25,9},{2,18},{3,... | collective-permute-start | bytes 196616 | tf_op jit(solution)/shard_map/ppermute | solution.py:776
  21.5 1.5 %collective-permute-start.7 = (bf16[256,128]{1,0:T(8,128)(2,1)S(1)}, bf16[256,128]{1,0:T(8,128)(2,1)S(1)}, u32[]{:S(2)}, u32[]{:S(2)}) collective-permute-start(bf16[256,128]{1,0:T(8,128)(2,1)S(1)} %get-tuple-element.50), channel_id=1, source_target_pairs={{0,17},{1,16},{8,25},{9,24},{16,1},{17,0},{24,9},{25,8},{2,19},{3,... | collective-permute-start | bytes 196616 | tf_op jit(solution)/shard_map/ppermute | solution.py:776
  23.0 1.3 %collective-permute-done.6.piece2_ref = bf16[256,128]{1,0:T(8,128)(2,1)S(1)} collective-permute-done((bf16[256,128]{1,0:T(8,128)(2,1)S(1)}, bf16[256,128]{1,0:T(8,128)(2,1)S(1)}, u32[]{:S(2)}, u32[]{:S(2)}) %collective-permute-start.6) | collective-permute-done | bytes 65568 | tf_op jit(solution)/shard_map/ppermute | solution.py:776
  24.2 2.4 %collective-permute-done.7.piece3_ref = bf16[256,128]{1,0:T(8,128)(2,1)S(1)} collective-permute-done((bf16[256,128]{1,0:T(8,128)(2,1)S(1)}, bf16[256,128]{1,0:T(8,128)(2,1)S(1)}, u32[]{:S(2)}, u32[]{:S(2)}) %collective-permute-start.7) | collective-permute-done | bytes 65568 | tf_op jit(solution)/shard_map/ppermute | solution.py:776
  26.6 0.0 collective-permute-done.5.piece1_ref
  26.6 2.5 %shard_map.60 = (bf16[4,2,64,128]{3,2,1,0:T(8,128)(2,1)S(1)}, bf16[512,256]{1,0:T(8,128)(2,1)S(1)}, bf16[256,256]{1,0:T(8,128)(2,1)S(1)}, f32[8,512]{1,0:T(8,128)S(1)}) custom-call(bf16[256,128]{1,0:T(8,128)(2,1)S(1)} %get-tuple-element.47.piece0_ref, bf16[304,128]{1,0:T(8,128)(2,1)S(1)} %collective-permute-done.5.piece1_ref, ...), custom_call_target="tpu_custom_call" | custom-call | tf_op jit(solution)/shard_map/pallas_call | solution.py:666
  29.1 0.1 collective-permute-start.8
  29.2 0.3 shard_map.61
  29.5 1.0 %collective-permute-done.8.received_ref = bf16[4,2,64,128]{3,2,1,0:T(8,128)(2,1)S(1)} collective-permute-done((bf16[4,2,64,128]{3,2,1,0:T(8,128)(2,1)S(1)}, bf16[4,2,64,128]{3,2,1,0:T(8,128)(2,1)S(1)}, u32[]{:S(2)}, u32[]{:S(2)}) %collective-permute-start.8) | collective-permute-done | bytes 131104 | tf_op jit(solution)/shard_map/ppermute | solution.py:791
  30.5 1.6 %collective-permute-start.9 = (bf16[2,2,64,128]{3,2,1,0:T(8,128)(2,1)S(1)}, bf16[2,2,64,128]{3,2,1,0:T(8,128)(2,1)S(1)}, u32[]{:S(2)}, u32[]{:S(2)}) collective-permute-start(bf16[2,2,64,128]{3,2,1,0:T(8,128)(2,1)S(1)} %get-tuple-element.60), channel_id=1, source_target_pairs={{0,1},{1,0},{8,9},{9,8},{16,17},{17,16},{24,25},{25,24},{2,3},{3,2... | collective-permute-start | bytes 196616 | tf_op jit(solution)/shard_map/ppermute | solution.py:776
  32.1 0.5 %collective-permute-start.10 = (bf16[2,2,64,128]{3,2,1,0:T(8,128)(2,1)S(1)}, bf16[2,2,64,128]{3,2,1,0:T(8,128)(2,1)S(1)}, u32[]{:S(2)}, u32[]{:S(2)}) collective-permute-start(bf16[2,2,64,128]{3,2,1,0:T(8,128)(2,1)S(1)} %get-tuple-element.61), channel_id=1, source_target_pairs={{0,16},{1,17},{8,24},{9,25},{16,0},{17,1},{24,8},{25,9},{2,18},{3,... | collective-permute-start | bytes 196616 | tf_op jit(solution)/shard_map/ppermute | solution.py:776
  32.7 1.4 %collective-permute-start.11 = (bf16[2,2,64,128]{3,2,1,0:T(8,128)(2,1)S(1)}, bf16[2,2,64,128]{3,2,1,0:T(8,128)(2,1)S(1)}, u32[]{:S(2)}, u32[]{:S(2)}) collective-permute-start(bf16[2,2,64,128]{3,2,1,0:T(8,128)(2,1)S(1)} %get-tuple-element.62), channel_id=1, source_target_pairs={{0,17},{1,16},{8,25},{9,24},{16,1},{17,0},{24,9},{25,8},{2,19},{3,... | collective-permute-start | bytes 196616 | tf_op jit(solution)/shard_map/ppermute | solution.py:776
  34.1 0.8 %collective-permute-done.9.refs_1_ = bf16[2,2,64,128]{3,2,1,0:T(8,128)(2,1)S(1)} collective-permute-done((bf16[2,2,64,128]{3,2,1,0:T(8,128)(2,1)S(1)}, bf16[2,2,64,128]{3,2,1,0:T(8,128)(2,1)S(1)}, u32[]{:S(2)}, u32[]{:S(2)}) %collective-permute-start.9) | collective-permute-done | bytes 65568 | tf_op jit(solution)/shard_map/ppermute | solution.py:776
  34.9 1.8 %collective-permute-done.10.refs_2_ = bf16[2,2,64,128]{3,2,1,0:T(8,128)(2,1)S(1)} collective-permute-done((bf16[2,2,64,128]{3,2,1,0:T(8,128)(2,1)S(1)}, bf16[2,2,64,128]{3,2,1,0:T(8,128)(2,1)S(1)}, u32[]{:S(2)}, u32[]{:S(2)}) %collective-permute-start.10) | collective-permute-done | bytes 65568 | tf_op jit(solution)/shard_map/ppermute | solution.py:776
  36.7 1.1 %collective-permute-done.11.refs_3_ = bf16[2,2,64,128]{3,2,1,0:T(8,128)(2,1)S(1)} collective-permute-done((bf16[2,2,64,128]{3,2,1,0:T(8,128)(2,1)S(1)}, bf16[2,2,64,128]{3,2,1,0:T(8,128)(2,1)S(1)}, u32[]{:S(2)}, u32[]{:S(2)}) %collective-permute-start.11) | collective-permute-done | bytes 65568 | tf_op jit(solution)/shard_map/ppermute | solution.py:776
  37.8 1.0 %shard_map.63 = bf16[64,2,8,128]{3,2,1,0:T(8,128)(2,1)} custom-call(bf16[2,2,64,128]{3,2,1,0:T(8,128)(2,1)S(1)} %get-tuple-element.59.refs_0_, bf16[2,2,64,128]{3,2,1,0:T(8,128)(2,1)S(1)} %collective-permute-done.9.refs_1_, bf16[2,2,64,128]{3,2,1,0:T(8,128)(2,1)S(1)} %collective-permute-done.10.refs_2_, ...), custom_call_target="tpu_custom_call" | custom-call | tf_op jit(solution)/shard_map/pallas_call | solution.py:666
  (1 shorter events, 0.0 us)
Async XLA Ops:
  0.0 2.2 %collective-permute-start = (f32[64,2,8,128]{3,2,1,0:T(8,128)}, f32[64,2,8,128]{3,2,1,0:T(8,128)S(1)}, u32[]{:S(2)}, u32[]{:S(2)}) collective-permute-start(f32[64,2,8,128]{3,2,1,0:T(8,128)} %param.5), channel_id=1, source_target_pairs={{0,8},{8,0},{16,24},{24,16},{1,9},{9,1},{17,25},{25,17},{2,10},{10... | collective-permute-start | bytes 1572872 | tf_op jit(solution)/shard_map/ppermute | solution.py:696
  2.6 15.0 %collective-permute-start.2 = (bf16[1328,128]{1,0:T(8,128)(2,1)S(1)}, bf16[1328,128]{1,0:T(8,128)(2,1)S(1)}, u32[]{:S(2)}, u32[]{:S(2)}) collective-permute-start(bf16[1328,128]{1,0:T(8,128)(2,1)S(1)} %get-tuple-element.36.halo_ref), channel_id=1, source_target_pairs={{0,2},{2,4},{4,6},{6,0},{8,14},{10,8},{12,10},{14,12},{16,18},{18,... | collective-permute-start | bytes 1019912 | tf_op jit(solution)/shard_map/ppermute | solution.py:737
  6.1 4.5 %collective-permute-start.1 = (f32[160,128]{1,0:T(8,128)S(1)}, f32[160,128]{1,0:T(8,128)S(1)}, u32[]{:S(2)}, u32[]{:S(2)}) collective-permute-start(f32[160,128]{1,0:T(8,128)S(1)} %get-tuple-element.40), channel_id=1, source_target_pairs={{0,1},{1,0},{2,3},{3,2},{4,5},{5,4},{6,7},{7,6},{8,9},{9,8},{10,11... | collective-permute-start | bytes 245768 | tf_op jit(solution)/shard_map/ppermute | solution.py:750
  7.7 9.9 %collective-permute-start.3 = (bf16[112,128]{1,0:T(8,128)(2,1)S(1)}, bf16[112,128]{1,0:T(8,128)(2,1)S(1)}, u32[]{:S(2)}, u32[]{:S(2)}) collective-permute-start(bf16[112,128]{1,0:T(8,128)(2,1)S(1)} %get-tuple-element.45), channel_id=1, source_target_pairs={{0,3},{1,2},{2,5},{3,4},{4,7},{5,6},{6,1},{7,0},{8,15},{9,14},{10,... | collective-permute-start | bytes 86024 | tf_op jit(solution)/shard_map/ppermute | solution.py:751
  9.2 2.8 %collective-permute-start.4 = (f32[16,128]{1,0:T(8,128)S(1)}, f32[16,128]{1,0:T(8,128)S(1)}, u32[]{:S(2)}, u32[]{:S(2)}) collective-permute-start(f32[16,128]{1,0:T(8,128)S(1)} %get-tuple-element.46.obs_ref), channel_id=1, source_target_pairs={{0,8},{8,0},{16,24},{24,16},{1,9},{9,1},{17,25},{25,17},{2,10},{10... | collective-permute-start | bytes 24584 | tf_op jit(solution)/shard_map/ppermute | solution.py:727
  19.4 7.2 %collective-permute-start.5 = (bf16[304,128]{1,0:T(8,128)(2,1)S(1)}, bf16[304,128]{1,0:T(8,128)(2,1)S(1)}, u32[]{:S(2)}, u32[]{:S(2)}) collective-permute-start(bf16[304,128]{1,0:T(8,128)(2,1)S(1)} %get-tuple-element.48), channel_id=1, source_target_pairs={{0,1},{1,0},{8,9},{9,8},{16,17},{17,16},{24,25},{25,24},{2,3},{3,2... | collective-permute-start | bytes 233480 | tf_op jit(solution)/shard_map/ppermute | solution.py:776
  20.0 4.3 %collective-permute-start.6 = (bf16[256,128]{1,0:T(8,128)(2,1)S(1)}, bf16[256,128]{1,0:T(8,128)(2,1)S(1)}, u32[]{:S(2)}, u32[]{:S(2)}) collective-permute-start(bf16[256,128]{1,0:T(8,128)(2,1)S(1)} %get-tuple-element.49), channel_id=1, source_target_pairs={{0,16},{1,17},{8,24},{9,25},{16,0},{17,1},{24,8},{25,9},{2,18},{3,... | collective-permute-start | bytes 196616 | tf_op jit(solution)/shard_map/ppermute | solution.py:776
  21.5 5.2 %collective-permute-start.7 = (bf16[256,128]{1,0:T(8,128)(2,1)S(1)}, bf16[256,128]{1,0:T(8,128)(2,1)S(1)}, u32[]{:S(2)}, u32[]{:S(2)}) collective-permute-start(bf16[256,128]{1,0:T(8,128)(2,1)S(1)} %get-tuple-element.50), channel_id=1, source_target_pairs={{0,17},{1,16},{8,25},{9,24},{16,1},{17,0},{24,9},{25,8},{2,19},{3,... | collective-permute-start | bytes 196616 | tf_op jit(solution)/shard_map/ppermute | solution.py:776
  29.1 1.4 %collective-permute-start.8 = (bf16[4,2,64,128]{3,2,1,0:T(8,128)(2,1)S(1)}, bf16[4,2,64,128]{3,2,1,0:T(8,128)(2,1)S(1)}, u32[]{:S(2)}, u32[]{:S(2)}) collective-permute-start(bf16[4,2,64,128]{3,2,1,0:T(8,128)(2,1)S(1)} %get-tuple-element.51), channel_id=1, source_target_pairs={{0,8},{8,0},{16,24},{24,16},{1,9},{9,1},{17,25},{25,17},{2,10},{10... | collective-permute-start | bytes 393224 | tf_op jit(solution)/shard_map/ppermute | solution.py:791
  30.5 4.3 %collective-permute-start.9 = (bf16[2,2,64,128]{3,2,1,0:T(8,128)(2,1)S(1)}, bf16[2,2,64,128]{3,2,1,0:T(8,128)(2,1)S(1)}, u32[]{:S(2)}, u32[]{:S(2)}) collective-permute-start(bf16[2,2,64,128]{3,2,1,0:T(8,128)(2,1)S(1)} %get-tuple-element.60), channel_id=1, source_target_pairs={{0,1},{1,0},{8,9},{9,8},{16,17},{17,16},{24,25},{25,24},{2,3},{3,2... | collective-permute-start | bytes 196616 | tf_op jit(solution)/shard_map/ppermute | solution.py:776
  32.1 4.6 %collective-permute-start.10 = (bf16[2,2,64,128]{3,2,1,0:T(8,128)(2,1)S(1)}, bf16[2,2,64,128]{3,2,1,0:T(8,128)(2,1)S(1)}, u32[]{:S(2)}, u32[]{:S(2)}) collective-permute-start(bf16[2,2,64,128]{3,2,1,0:T(8,128)(2,1)S(1)} %get-tuple-element.61), channel_id=1, source_target_pairs={{0,16},{1,17},{8,24},{9,25},{16,0},{17,1},{24,8},{25,9},{2,18},{3,... | collective-permute-start | bytes 196616 | tf_op jit(solution)/shard_map/ppermute | solution.py:776
  32.7 5.2 %collective-permute-start.11 = (bf16[2,2,64,128]{3,2,1,0:T(8,128)(2,1)S(1)}, bf16[2,2,64,128]{3,2,1,0:T(8,128)(2,1)S(1)}, u32[]{:S(2)}, u32[]{:S(2)}) collective-permute-start(bf16[2,2,64,128]{3,2,1,0:T(8,128)(2,1)S(1)} %get-tuple-element.62), channel_id=1, source_target_pairs={{0,17},{1,16},{8,25},{9,24},{16,1},{17,0},{24,9},{25,8},{2,19},{3,... | collective-permute-start | bytes 196616 | tf_op jit(solution)/shard_map/ppermute | solution.py:776

commit v4 on v3

--- a/solution.py
+++ b/solution.py
@@ -214,6 +214,8 @@
 DOMAIN = 3 * HALO
 EXTENT = LANES + 2 * OCTET
 VMEM_GRANT = 24 << 20
+LARGEST = 6.0
+WIDENING = 11.06 / LARGEST
 STAGE_FACTORS = (1.0 / 4.0, 1.0 / 3.0, 1.0 / 2.0, 1.0)
 
 
@@ -244,7 +246,7 @@
         self.rows = rows
         self.members = 2 * local
         self.per_member = layers * rows
-        self.halo_rows = layers * (HALO + 1) * LANES
+        self.halo_rows = HALO * LANES
         self.wind_rows = 2 * layers * HALO
         self.side_rows = layers * 2 * HALO * OCTET
         self.corner_rows = layers * HALO * OCTET
@@ -271,10 +273,26 @@
     return value * jnp.where(row < value.shape[0] // 2, sign, half)
 
 
+def widened(u):
+    v = WIDENING * jnp.abs(u)
+    series = v * (1.0 + v * (1.0 / 2.0) * (1.0 + v * (1.0 / 3.0) * (1.0 + v * (1.0 / 4.0))))
+    g = jnp.where(v < 0.05, series, jnp.exp(v) - 1.0)
+    return jnp.where(u < 0.0, -g, g)
+
+
+def narrowed(w):
+    g = jnp.abs(w)
+    series = g * (1.0 - g * (1.0 / 2.0 - g * (1.0 / 3.0 - g * (1.0 / 4.0 - g * (1.0 / 5.0)))))
+    u = jnp.where(g < 0.05, series, jnp.log(1.0 + g)) * (1.0 / WIDENING)
+    return jnp.where(w < 0.0, -u, u)
+
+
 def fetch_kernel(
-    prior_ref, wind_ref, cells_ref, values_ref, errors_ref, own_ref, wind_out_ref, obs_ref,
-    cells_vmem, values_vmem, errors_vmem, sems,
+    s, prior_ref, wind_ref, cells_ref, values_ref, errors_ref,
+    own_ref, wind_out_ref, obs_ref, same_ref, other_ref,
+    cells_vmem, values_vmem, errors_vmem, rows_ref, sems,
 ):
+    odd = lax.rem(lax.axis_index("mem"), 2)
     copies = [
         pltpu.make_async_copy(source, target, sems.at[i])
         for i, (source, target) in enumerate(
@@ -287,32 +305,24 @@
     for copy in copies:
         copy.start()
     obs_ref[...] = jnp.zeros_like(obs_ref)
-    for copy in copies[:3]:
+    for copy in copies[:4]:
         copy.wait()
     obs_ref[0:1, :] = cells_vmem[...].astype(jnp.float32)
     obs_ref[1:2, :] = values_vmem[...]
     obs_ref[2:3, :] = errors_vmem[...]
-    for copy in copies[3:]:
-        copy.wait()
-
-
-def pack_halo_kernel(s, own_ref, sib_ref, wind_ref, out_ref, field_ref, rows_ref):
-    odd = lax.rem(lax.axis_index("mem"), 2)
-    for layer in range(s.layers):
-        base = layer * (HALO + 1) * LANES
-        for j in range(HALO):
-            value = columns_first(s, odd, own_ref, sib_ref, layer, 2 * HALO + j)
-            field_ref[pl.ds(s.field_at(layer, 2 * HALO + j) + OCTET, LANES), :] = value
-            high, low = split_two(value)
-            out_ref[pl.ds(base + (HALO - j) * LANES, LANES), :] = high
-            if j == HALO - 1:
-                out_ref[pl.ds(base, LANES), :] = low
     for block in range(2 * s.layers):
         for j in range(HALO):
             row = block * s.rows + tile_row(odd, 2 * HALO + j)
-            rows_ref[pl.ds(block * HALO + j, 1), :] = wind_ref[pl.ds(row, 1), :]
+            rows_ref[pl.ds(block * HALO + j, 1), :] = wind_out_ref[pl.ds(row, 1), :]
     for i, part in enumerate(split_three(wind_scale(odd, rows_ref[...]))):
-        out_ref[pl.ds(s.halo_rows + i * s.wind_rows, s.wind_rows), :] = part
+        same_ref[pl.ds(s.halo_rows + i * s.wind_rows, s.wind_rows), :] = part.astype(jnp.float32)
+    copies[4].wait()
+    for parity, out_ref in ((odd, same_ref), (1 - odd, other_ref)):
+        for j in range(HALO):
+            row = tile_row(parity, 2 * HALO + j)
+            parts = [own_ref[pl.ds(layer * s.rows + row, s.local, stride=s.per_member), :] for layer in range(s.layers)]
+            value = jnp.concatenate(parts, axis=0).T
+            out_ref[pl.ds(j * LANES, LANES), :] = widened(value) if j == HALO - 1 else value
 
 
 def spread(parts, rows, targets, store):
@@ -326,21 +336,19 @@
         store(second, both[:, LANES:])
 
 
-def pack_edges_kernel(s, own_ref, sib_ref, wind_ref, halo_ref, _, field_ref, side_ref, corner_ref, winds_ref):
+def pack_edges_kernel(s, own_ref, sib_ref, wind_ref, same_ref, field_ref, side_ref, corner_ref, winds_ref):
     odd = lax.rem(lax.axis_index("mem"), 2)
     for layer in range(s.layers):
-        for j in range(HALO, 2 * HALO):
+        for j in range(HALO, DOMAIN):
             value = columns_first(s, odd, own_ref, sib_ref, layer, j)
             field_ref[pl.ds(s.field_at(layer, j) + OCTET, LANES), :] = value
-    for layer in range(s.layers):
-        for j in range(HALO, DOMAIN):
-            at = s.field_at(layer, j) + OCTET
             to = (layer * 2 * HALO + j - HALO) * OCTET
-            side_ref[pl.ds(to, HALO), :] = field_ref[pl.ds(at + LANES - HALO, HALO), :]
-            side_ref[pl.ds(to + HALO, HALO), :] = field_ref[pl.ds(at, HALO), :]
+            side_ref[pl.ds(to, HALO), :] = value[LANES - HALO :]
+            side_ref[pl.ds(to + HALO, HALO), :] = value[:HALO]
         to, at = layer * HALO * OCTET, (layer * 2 * HALO + HALO) * OCTET
         corner_ref[pl.ds(to, HALO * OCTET), :] = side_ref[pl.ds(at, HALO * OCTET), :].astype(jnp.bfloat16)
-    corner_ref[pl.ds(s.corner_rows, 3 * s.wind_rows), :] = halo_ref[pl.ds(s.halo_rows, 3 * s.wind_rows), :]
+    winds = same_ref[pl.ds(s.halo_rows, 3 * s.wind_rows), :]
+    corner_ref[pl.ds(s.corner_rows, 3 * s.wind_rows), :] = winds.astype(jnp.bfloat16)
     scaled = wind_scale(odd, wind_ref[...])
     side_ref[pl.ds(s.side_rows, 2 * s.layers * s.rows), :] = scaled
 
@@ -422,21 +430,29 @@
 
 
 def forecast_kernel(
-    s, _, __, ___, ____, halo_ref, corner_ref, obs_ref,
+    s, _, __, ___, ____, same_ref, other_ref, corner_ref, obs_ref,
     out0_ref, out1_ref, out2_ref, out3_ref, field_ref, winds_ref, first_ref, second_ref,
 ):
     mem = lax.axis_index("mem")
     odd = lax.rem(mem, 2)
     place = (mem // 2) * 2 + lax.axis_index("gy")
 
+    lower = lax.broadcasted_iota(jnp.int32, (LANES, LANES), 1) < s.local
+    for j in range(HALO):
+        both = []
+        for ref in (same_ref, other_ref):
+            value = ref[pl.ds(j * LANES, LANES), :]
+            both.append(narrowed(value) if j == HALO - 1 else value)
+        same, other = both
+        layer_fields = (
+            jnp.where(lower, same, pltpu.roll(other, s.local, 1)),
+            jnp.where(lower, pltpu.roll(same, s.local, 1), other),
+        )
+        for layer, value in enumerate(layer_fields):
+            field_ref[pl.ds(s.field_at(layer, j) + OCTET, LANES), :] = value
     for layer in range(s.layers):
         corner = corner_ref[pl.ds(layer * HALO * OCTET, HALO * OCTET), :].astype(jnp.float32)
         for j in range(HALO):
-            base = layer * (HALO + 1) * LANES
-            value = halo_ref[pl.ds(base + (HALO - j) * LANES, LANES), :].astype(jnp.float32)
-            if j == HALO - 1:
-                value = value + halo_ref[pl.ds(base, LANES), :].astype(jnp.float32)
-            field_ref[pl.ds(s.field_at(layer, j) + OCTET, LANES), :] = value
             set_field_edges(s, field_ref, layer, j, corner[j * OCTET : (j + 1) * OCTET])
     far = [corner_ref[pl.ds(s.corner_rows + i * s.wind_rows, s.wind_rows), :].astype(jnp.float32) for i in range(3)]
     beyond = padded_rows(far[0] + far[1] + far[2]).T
@@ -451,7 +467,7 @@
     def store(row, value):
         winds_ref[pl.ds(wind_at(row) + OCTET, LANES), :] = value
 
-    near = [halo_ref[pl.ds(s.halo_rows + i * s.wind_rows, s.wind_rows), :] for i in range(3)]
+    near = [same_ref[pl.ds(s.halo_rows + i * s.wind_rows, s.wind_rows), :].astype(jnp.bfloat16) for i in range(3)]
     spread(near, s.wind_rows, targets, store)
 
     refs = (field_ref, first_ref, second_ref, first_ref)
@@ -687,6 +703,9 @@
         return 1 if m % 2 == 0 else n_gx - 1
 
     along = [(m * n_gx + z, m * n_gx + (z + step(m)) % n_gx) for m in range(4) for z in range(n_gx)]
+    along_other = [
+        (m * n_gx + z, (m ^ 1) * n_gx + (z + step(m ^ 1)) % n_gx) for m in range(4) for z in range(n_gx)
+    ]
     across = [(0, 1), (1, 0)]
     diagonal = [
         ((m * n_gx + z) * 2 + y, (m * n_gx + (z + step(m)) % n_gx) * 2 + 1 - y)
@@ -696,19 +715,22 @@
     sib = lax.ppermute(prior_sample_set, "mem", pair).reshape(local * layers * rows, columns)
     count = observed_cells.shape[-1]
     vmem, hbm = pl.BlockSpec(memory_space=pltpu.VMEM), pl.BlockSpec(memory_space=pltpu.HBM)
-    own, wind, obs = pl.pallas_call(
-        fetch_kernel,
+    own, wind, obs, same_out, other_out = pl.pallas_call(
+        functools.partial(fetch_kernel, s),
         out_shape=(
             shaped((local * layers * rows, columns), f32),
             shaped((2 * layers * rows, columns), f32),
             shaped((2 * OCTET, count), f32),
+            shaped((s.halo_rows + 3 * s.wind_rows, LANES), f32),
+            shaped((s.halo_rows, LANES), f32),
         ),
         in_specs=[hbm] * 5,
-        out_specs=(vmem, vmem, vmem),
+        out_specs=(vmem, vmem, vmem, vmem, vmem),
         scratch_shapes=[
             pltpu.VMEM((1, count), jnp.int32),
             pltpu.VMEM((1, count), f32),
             pltpu.VMEM((1, count), f32),
+            pltpu.VMEM((s.wind_rows, LANES), f32),
             pltpu.SemaphoreType.DMA((5,)),
         ],
         compiler_params=pltpu.CompilerParams(vmem_limit_bytes=VMEM_GRANT),
@@ -728,13 +750,8 @@
 
     field_shape = shaped((layers * DOMAIN * EXTENT, LANES), f32)
     winds_shape = shaped((2 * layers * DOMAIN * EXTENT, LANES), f32)
-    halo_out, field = vmem_call(
-        functools.partial(pack_halo_kernel, s),
-        (shaped((s.halo_rows + 3 * s.wind_rows, LANES), bf16), field_shape),
-        [((s.wind_rows, LANES), f32)],
-        own, sib, wind,
-    )
-    halo = lax.ppermute(halo_out, ("mem", "gx"), along)
+    same = lax.ppermute(same_out.astype(jnp.float16), ("mem", "gx"), along).astype(f32)
+    other = lax.ppermute(other_out.astype(jnp.float16), ("mem", "gx"), along_other).astype(f32)
     field, side_out, corner_out, winds = vmem_call(
         functools.partial(pack_edges_kernel, s),
         (
@@ -744,8 +761,7 @@
             winds_shape,
         ),
         [],
-        own, sib, wind, halo_out, field,
-        aliases={4: 0},
+        own, sib, wind, same_out,
     )
     side = lax.ppermute(side_out, "gy", across)
     corner = lax.ppermute(corner_out, ("mem", "gx", "gy"), diagonal)
@@ -762,7 +778,7 @@
         functools.partial(forecast_kernel, s),
         (piece, piece_obs, piece, piece, field_shape, winds_shape, field_shape, field_shape),
         [],
-        field, winds, first, second, halo, corner, obs_sib,
+        field, winds, first, second, same, other, corner, obs_sib,
         aliases={0: 4, 1: 5, 2: 6, 3: 7},
     )
 

time: 39 us -> 37.3 us (0.956)
  waiting for transfers between devices: 15.9 us -> 12.1 us
  starting transfers between devices: 13.9 us -> 15.8 us
    ppermute x1, waiting for transfers between devices: 5.63 us -> 0.38 us  [on_device_tile(): corner = lax.ppermute(corner_out, ('mem', 'gx', 'gy'), diagonal)]
    ppermute x1 -> x2, waiting for transfers between devices: 0.01 us -> 3.16 us  [the longest x1 3.16 us: on_device_tile(): lax.ppermute(other_out.astype(jnp.float16), ('mem', 'gx'), along_other)]
    ppermute x1 -> x2, starting transfers between devices: 2.99 us -> 4.99 us  [the longest x1 2.62 us: on_device_tile(): lax.ppermute(same_out.astype(jnp.float16), ('mem', 'gx'), along).astype(f32)]
    ppermute x1, waiting for transfers between devices: 1.21 us -> 0.01 us  [on_device_tile(): side = lax.ppermute(side_out, 'gy', across)]
    ppermute x1, waiting for transfers between devices: 0.59 us -> 0.01 us  [on_device_tile(): lax.ppermute(prior_sample_set, 'mem', pair)]
    pallas_call x8 -> x7, Pallas kernels: 7.77 us -> 7.75 us  [vmem_call(): pl.pallas_call(kernel, out_shape=outs, in_specs=[spec] * len(args), out_s...]
  transfers between devices with their start and end apart: 12 -> 13, of which waited for: 9 -> 8; matrix products, arithmetic and copies ran while one was open for 0% -> 0% of each run, Pallas kernels for 9% -> 10%
where the time goes in v4:
time: 37.3 us; the launch traced here: 37.2 us
  starting transfers between devices  15.8 us (42%)
  waiting for transfers between devices  12.1 us (32%)
  Pallas kernels  9.16 us (25%)
    pallas_call x7, Pallas kernels, vmem_call(): pl.pallas_call(kernel, out_shape=outs, in_specs=[spec] * len(args), out_s...  7.75 us
    ppermute x6, waiting for transfers between devices, exchange(): arrived.append(lax.ppermute(parts[d], ('mem', 'gy'), flip(d)))  7.45 us
    ppermute x6, starting transfers between devices, exchange(): arrived.append(lax.ppermute(parts[d], ('mem', 'gy'), flip(d)))  7.11 us
    ppermute x1, waiting for transfers between devices, on_device_tile(): lax.ppermute(other_out.astype(jnp.float16), ('mem', 'gx'), along_other)  3.16 us
    ppermute x1, starting transfers between devices, on_device_tile(): lax.ppermute(same_out.astype(jnp.float16), ('mem', 'gx'), along).astype(f32)  2.62 us
    ppermute x1, starting transfers between devices, on_device_tile(): lax.ppermute(other_out.astype(jnp.float16), ('mem', 'gx'), along_other)  2.37 us
    ppermute x1, starting transfers between devices, on_device_tile(): side = lax.ppermute(side_out, 'gy', across)  1.59 us
    ppermute x1, starting transfers between devices, on_device_tile(): corner = lax.ppermute(corner_out, ('mem', 'gx', 'gy'), diagonal)  1.52 us
  transfers between devices with their start and end apart: 13, of which 8 were waited for; matrix products, arithmetic and copies ran while one was open for 0% of the time, Pallas kernels for 10%

profile of v4, /device:TPU:0, one launch (start us, length us, event | category | flops | bytes accessed | tf_op | source)
XLA Modules:
  0.0 37.2 jit_solution(9983810720460563937)
XLA Ops:
  0.0 0.5 %collective-permute-start = (f32[64,2,8,128]{3,2,1,0:T(8,128)}, f32[64,2,8,128]{3,2,1,0:T(8,128)S(1)}, u32[]{:S(2)}, u32[]{:S(2)}) collective-permute-start(f32[64,2,8,128]{3,2,1,0:T(8,128)} %param.5), channel_id=1, source_target_pairs={{0,8},{8,0},{16,24},{24,16},{1,9},{9,1},{17,25},{25,17},{2,10},{10... | collective-permute-start | bytes 1572872 | tf_op jit(solution)/shard_map/ppermute | solution.py:715
  0.5 1.4 %shard_map.55 = (f32[1024,128]{1,0:T(8,128)S(1)}, f32[32,128]{1,0:T(8,128)S(1)}, f32[16,128]{1,0:T(8,128)S(1)}, f32[560,128]{1,0:T(8,128)S(1)}, f32[512,128]{1,0:T(8,128)S(1)}) custom-call(f32[1024,128]{1,0:T(8,128)} %bitcast.7, f32[32,128]{1,0:T(8,128)} %bitcast.8, s32[1,128]{1,0:T(1,128)} %bitcast.9, f32[1,128]{1,0:T(1,128)} %bitcast.10, f32[1,128]{1,0:T(1,128)} %bitcast.11), custom_call_target="tpu_custom_call" | custom-call | tf_op jit(solution)/shard_map/pallas_call | solution.py:718
  1.9 2.6 %collective-permute-start.2 = (f16[560,128]{1,0:T(8,128)(2,1)S(1)}, f16[560,128]{1,0:T(8,128)(2,1)S(1)}, u32[]{:S(2)}, u32[]{:S(2)}) collective-permute-start(f16[560,128]{1,0:T(8,128)(2,1)S(1)} %convert_element_type.12), channel_id=1, source_target_pairs={{0,2},{2,4},{4,6},{6,0},{8,14},{10,8},{12,10},{14,12},{16,18},{18,... | collective-permute-start | bytes 430088 | tf_op jit(solution)/shard_map/ppermute | solution.py:753
  4.6 2.4 %collective-permute-start.3 = (f16[512,128]{1,0:T(8,128)(2,1)S(1)}, f16[512,128]{1,0:T(8,128)(2,1)S(1)}, u32[]{:S(2)}, u32[]{:S(2)}) collective-permute-start(f16[512,128]{1,0:T(8,128)(2,1)S(1)} %convert_element_type.14), channel_id=1, source_target_pairs={{0,14},{2,8},{4,10},{6,12},{8,2},{10,4},{12,6},{14,0},{16,30},{18,... | collective-permute-start | bytes 393224 | tf_op jit(solution)/shard_map/ppermute | solution.py:754
  7.0 0.0 collective-permute-done
  7.0 0.7 %shard_map.56 = (f32[3456,128]{1,0:T(8,128)S(1)}, f32[160,128]{1,0:T(8,128)S(1)}, bf16[112,128]{1,0:T(8,128)(2,1)S(1)}, f32[6912,128]{1,0:T(8,128)S(1)}) custom-call(f32[1024,128]{1,0:T(8,128)S(1)} %get-tuple-element.34.own_ref, f32[1024,128]{1,0:T(8,128)S(1)} %bitcast.6, f32[32,128]{1,0:T(8,128)S(1)} %get-tuple-element.35.wind_ref, ...), custom_call_target="tpu_custom_call" | custom-call | tf_op jit(solution)/shard_map/pallas_call | solution.py:682
  7.7 1.6 %collective-permute-start.1 = (f32[160,128]{1,0:T(8,128)S(1)}, f32[160,128]{1,0:T(8,128)S(1)}, u32[]{:S(2)}, u32[]{:S(2)}) collective-permute-start(f32[160,128]{1,0:T(8,128)S(1)} %get-tuple-element.39), channel_id=1, source_target_pairs={{0,1},{1,0},{2,3},{3,2},{4,5},{5,4},{6,7},{7,6},{8,9},{9,8},{10,11... | collective-permute-start | bytes 245768 | tf_op jit(solution)/shard_map/ppermute | solution.py:766
  9.3 1.5 %collective-permute-start.4 = (bf16[112,128]{1,0:T(8,128)(2,1)S(1)}, bf16[112,128]{1,0:T(8,128)(2,1)S(1)}, u32[]{:S(2)}, u32[]{:S(2)}) collective-permute-start(bf16[112,128]{1,0:T(8,128)(2,1)S(1)} %get-tuple-element.45), channel_id=1, source_target_pairs={{0,3},{1,2},{2,5},{3,4},{4,7},{5,6},{6,1},{7,0},{8,15},{9,14},{10,... | collective-permute-start | bytes 86024 | tf_op jit(solution)/shard_map/ppermute | solution.py:767
  10.8 0.0 collective-permute-start.5
  10.8 3.2 %collective-permute-done.3 = f16[512,128]{1,0:T(8,128)(2,1)S(1)} collective-permute-done((f16[512,128]{1,0:T(8,128)(2,1)S(1)}, f16[512,128]{1,0:T(8,128)(2,1)S(1)}, u32[]{:S(2)}, u32[]{:S(2)}) %collective-permute-start.3) | collective-permute-done | bytes 131104 | tf_op jit(solution)/shard_map/ppermute | solution.py:754
  14.0 0.0 collective-permute-done.2
  14.0 0.0 collective-permute-done.1.side_ref
  14.0 1.4 %shard_map.57 = (f32[3456,128]{1,0:T(8,128)S(1)}, f32[6912,128]{1,0:T(8,128)S(1)}, f32[3456,128]{1,0:T(8,128)S(1)}, f32[3456,128]{1,0:T(8,128)S(1)}) custom-call(f32[3456,128]{1,0:T(8,128)S(1)} %get-tuple-element.37._, f32[6912,128]{1,0:T(8,128)S(1)} %get-tuple-element.38.__, ...), custom_call_target="tpu_custom_call", output_to_operand_aliasing={{0}: (0, {}), {1}: (1, {})} | custom-call | tf_op jit(solution)/shard_map/pallas_call | solution.py:682
  15.5 0.0 collective-permute-done.5.obs_ref
  15.5 0.4 %collective-permute-done.4.corner_ref = bf16[112,128]{1,0:T(8,128)(2,1)S(1)} collective-permute-done((bf16[112,128]{1,0:T(8,128)(2,1)S(1)}, bf16[112,128]{1,0:T(8,128)(2,1)S(1)}, u32[]{:S(2)}, u32[]{:S(2)}) %collective-permute-start.4) | collective-permute-done | bytes 28704 | tf_op jit(solution)/shard_map/ppermute | solution.py:767
  15.8 1.8 %shard_map.58 = (bf16[256,128]{1,0:T(8,128)(2,1)S(1)}, bf16[304,128]{1,0:T(8,128)(2,1)S(1)}, bf16[256,128]{1,0:T(8,128)(2,1)S(1)}, bf16[256,128]{1,0:T(8,128)(2,...) custom-call(f32[3456,128]{1,0:T(8,128)S(1)} %get-tuple-element.40._,, ...), custom_call_target="tpu_custom_call", output_to_operand_aliasing={{4}: (0, {}), {5}: (1, {}), {6}: (2, {}), {7}: (3, {})} | custom-call | tf_op jit(solution)/shard_map/pallas_call | solution.py:682
  17.7 1.0 %collective-permute-start.6 = (bf16[304,128]{1,0:T(8,128)(2,1)S(1)}, bf16[304,128]{1,0:T(8,128)(2,1)S(1)}, u32[]{:S(2)}, u32[]{:S(2)}) collective-permute-start(bf16[304,128]{1,0:T(8,128)(2,1)S(1)} %get-tuple-element.48), channel_id=1, source_target_pairs={{0,1},{1,0},{8,9},{9,8},{16,17},{17,16},{24,25},{25,24},{2,3},{3,2... | collective-permute-start | bytes 233480 | tf_op jit(solution)/shard_map/ppermute | solution.py:792
  18.7 1.5 %collective-permute-start.7 = (bf16[256,128]{1,0:T(8,128)(2,1)S(1)}, bf16[256,128]{1,0:T(8,128)(2,1)S(1)}, u32[]{:S(2)}, u32[]{:S(2)}) collective-permute-start(bf16[256,128]{1,0:T(8,128)(2,1)S(1)} %get-tuple-element.49), channel_id=1, source_target_pairs={{0,16},{1,17},{8,24},{9,25},{16,0},{17,1},{24,8},{25,9},{2,18},{3,... | collective-permute-start | bytes 196616 | tf_op jit(solution)/shard_map/ppermute | solution.py:792
  20.2 1.1 %collective-permute-start.8 = (bf16[256,128]{1,0:T(8,128)(2,1)S(1)}, bf16[256,128]{1,0:T(8,128)(2,1)S(1)}, u32[]{:S(2)}, u32[]{:S(2)}) collective-permute-start(bf16[256,128]{1,0:T(8,128)(2,1)S(1)} %get-tuple-element.50), channel_id=1, source_target_pairs={{0,17},{1,16},{8,25},{9,24},{16,1},{17,0},{24,9},{25,8},{2,19},{3,... | collective-permute-start | bytes 196616 | tf_op jit(solution)/shard_map/ppermute | solution.py:792
  21.3 2.4 %collective-permute-done.7.piece2_ref = bf16[256,128]{1,0:T(8,128)(2,1)S(1)} collective-permute-done((bf16[256,128]{1,0:T(8,128)(2,1)S(1)}, bf16[256,128]{1,0:T(8,128)(2,1)S(1)}, u32[]{:S(2)}, u32[]{:S(2)}) %collective-permute-start.7) | collective-permute-done | bytes 65568 | tf_op jit(solution)/shard_map/ppermute | solution.py:792
  23.7 1.7 %collective-permute-done.8.piece3_ref = bf16[256,128]{1,0:T(8,128)(2,1)S(1)} collective-permute-done((bf16[256,128]{1,0:T(8,128)(2,1)S(1)}, bf16[256,128]{1,0:T(8,128)(2,1)S(1)}, u32[]{:S(2)}, u32[]{:S(2)}) %collective-permute-start.8) | collective-permute-done | bytes 65568 | tf_op jit(solution)/shard_map/ppermute | solution.py:792
  25.4 2.5 %shard_map.59 = (bf16[4,2,64,128]{3,2,1,0:T(8,128)(2,1)S(1)}, bf16[512,256]{1,0:T(8,128)(2,1)S(1)}, bf16[256,256]{1,0:T(8,128)(2,1)S(1)}, f32[8,512]{1,0:T(8,128)S(1)}) custom-call(bf16[256,128]{1,0:T(8,128)(2,1)S(1)} %get-tuple-element.47.piece0_ref, bf16[304,128]{1,0:T(8,128)(2,1)S(1)} %collective-permute-done.6.piece1_ref, ...), custom_call_target="tpu_custom_call" | custom-call | tf_op jit(solution)/shard_map/pallas_call | solution.py:682
  27.9 0.1 collective-permute-start.9
  27.9 0.3 shard_map.60
  28.2 1.1 %collective-permute-done.9.received_ref = bf16[4,2,64,128]{3,2,1,0:T(8,128)(2,1)S(1)} collective-permute-done((bf16[4,2,64,128]{3,2,1,0:T(8,128)(2,1)S(1)}, bf16[4,2,64,128]{3,2,1,0:T(8,128)(2,1)S(1)}, u32[]{:S(2)}, u32[]{:S(2)}) %collective-permute-start.9) | collective-permute-done | bytes 131104 | tf_op jit(solution)/shard_map/ppermute | solution.py:807
  29.3 1.1 %collective-permute-start.10 = (bf16[2,2,64,128]{3,2,1,0:T(8,128)(2,1)S(1)}, bf16[2,2,64,128]{3,2,1,0:T(8,128)(2,1)S(1)}, u32[]{:S(2)}, u32[]{:S(2)}) collective-permute-start(bf16[2,2,64,128]{3,2,1,0:T(8,128)(2,1)S(1)} %get-tuple-element.60), channel_id=1, source_target_pairs={{0,1},{1,0},{8,9},{9,8},{16,17},{17,16},{24,25},{25,24},{2,3},{3,2... | collective-permute-start | bytes 196616 | tf_op jit(solution)/shard_map/ppermute | solution.py:792
  30.4 0.6 %collective-permute-start.11 = (bf16[2,2,64,128]{3,2,1,0:T(8,128)(2,1)S(1)}, bf16[2,2,64,128]{3,2,1,0:T(8,128)(2,1)S(1)}, u32[]{:S(2)}, u32[]{:S(2)}) collective-permute-start(bf16[2,2,64,128]{3,2,1,0:T(8,128)(2,1)S(1)} %get-tuple-element.61), channel_id=1, source_target_pairs={{0,16},{1,17},{8,24},{9,25},{16,0},{17,1},{24,8},{25,9},{2,18},{3,... | collective-permute-start | bytes 196616 | tf_op jit(solution)/shard_map/ppermute | solution.py:792
  31.0 1.8 %collective-permute-start.12 = (bf16[2,2,64,128]{3,2,1,0:T(8,128)(2,1)S(1)}, bf16[2,2,64,128]{3,2,1,0:T(8,128)(2,1)S(1)}, u32[]{:S(2)}, u32[]{:S(2)}) collective-permute-start(bf16[2,2,64,128]{3,2,1,0:T(8,128)(2,1)S(1)} %get-tuple-element.62), channel_id=1, source_target_pairs={{0,17},{1,16},{8,25},{9,24},{16,1},{17,0},{24,9},{25,8},{2,19},{3,... | collective-permute-start | bytes 196616 | tf_op jit(solution)/shard_map/ppermute | solution.py:792
  32.8 0.8 %collective-permute-done.10.refs_1_ = bf16[2,2,64,128]{3,2,1,0:T(8,128)(2,1)S(1)} collective-permute-done((bf16[2,2,64,128]{3,2,1,0:T(8,128)(2,1)S(1)}, bf16[2,2,64,128]{3,2,1,0:T(8,128)(2,1)S(1)}, u32[]{:S(2)}, u32[]{:S(2)}) %collective-permute-start.10) | collective-permute-done | bytes 65568 | tf_op jit(solution)/shard_map/ppermute | solution.py:792
  33.6 1.4 %collective-permute-done.11.refs_2_ = bf16[2,2,64,128]{3,2,1,0:T(8,128)(2,1)S(1)} collective-permute-done((bf16[2,2,64,128]{3,2,1,0:T(8,128)(2,1)S(1)}, bf16[2,2,64,128]{3,2,1,0:T(8,128)(2,1)S(1)}, u32[]{:S(2)}, u32[]{:S(2)}) %collective-permute-start.11) | collective-permute-done | bytes 65568 | tf_op jit(solution)/shard_map/ppermute | solution.py:792
  35.0 1.2 %collective-permute-done.12.refs_3_ = bf16[2,2,64,128]{3,2,1,0:T(8,128)(2,1)S(1)} collective-permute-done((bf16[2,2,64,128]{3,2,1,0:T(8,128)(2,1)S(1)}, bf16[2,2,64,128]{3,2,1,0:T(8,128)(2,1)S(1)}, u32[]{:S(2)}, u32[]{:S(2)}) %collective-permute-start.12) | collective-permute-done | bytes 65568 | tf_op jit(solution)/shard_map/ppermute | solution.py:792
  36.2 1.0 %shard_map.62 = bf16[64,2,8,128]{3,2,1,0:T(8,128)(2,1)} custom-call(bf16[2,2,64,128]{3,2,1,0:T(8,128)(2,1)S(1)} %get-tuple-element.59.refs_0_, bf16[2,2,64,128]{3,2,1,0:T(8,128)(2,1)S(1)} %collective-permute-done.10.refs_1_, bf16[2,2,64,128]{3,2,1,0:T(8,128)(2,1)S(1)} %collective-permute-done.11.refs_2_, ...), custom_call_target="tpu_custom_call" | custom-call | tf_op jit(solution)/shard_map/pallas_call | solution.py:682
  (6 shorter events, 0.1 us)
Async XLA Ops:
  0.0 7.0 %collective-permute-start = (f32[64,2,8,128]{3,2,1,0:T(8,128)}, f32[64,2,8,128]{3,2,1,0:T(8,128)S(1)}, u32[]{:S(2)}, u32[]{:S(2)}) collective-permute-start(f32[64,2,8,128]{3,2,1,0:T(8,128)} %param.5), channel_id=1, source_target_pairs={{0,8},{8,0},{16,24},{24,16},{1,9},{9,1},{17,25},{25,17},{2,10},{10... | collective-permute-start | bytes 1572872 | tf_op jit(solution)/shard_map/ppermute | solution.py:715
  1.9 12.0 %collective-permute-start.2 = (f16[560,128]{1,0:T(8,128)(2,1)S(1)}, f16[560,128]{1,0:T(8,128)(2,1)S(1)}, u32[]{:S(2)}, u32[]{:S(2)}) collective-permute-start(f16[560,128]{1,0:T(8,128)(2,1)S(1)} %convert_element_type.12), channel_id=1, source_target_pairs={{0,2},{2,4},{4,6},{6,0},{8,14},{10,8},{12,10},{14,12},{16,18},{18,... | collective-permute-start | bytes 430088 | tf_op jit(solution)/shard_map/ppermute | solution.py:753
  4.6 9.4 %collective-permute-start.3 = (f16[512,128]{1,0:T(8,128)(2,1)S(1)}, f16[512,128]{1,0:T(8,128)(2,1)S(1)}, u32[]{:S(2)}, u32[]{:S(2)}) collective-permute-start(f16[512,128]{1,0:T(8,128)(2,1)S(1)} %convert_element_type.14), channel_id=1, source_target_pairs={{0,14},{2,8},{4,10},{6,12},{8,2},{10,4},{12,6},{14,0},{16,30},{18,... | collective-permute-start | bytes 393224 | tf_op jit(solution)/shard_map/ppermute | solution.py:754
  7.7 6.3 %collective-permute-start.1 = (f32[160,128]{1,0:T(8,128)S(1)}, f32[160,128]{1,0:T(8,128)S(1)}, u32[]{:S(2)}, u32[]{:S(2)}) collective-permute-start(f32[160,128]{1,0:T(8,128)S(1)} %get-tuple-element.39), channel_id=1, source_target_pairs={{0,1},{1,0},{2,3},{3,2},{4,5},{5,4},{6,7},{7,6},{8,9},{9,8},{10,11... | collective-permute-start | bytes 245768 | tf_op jit(solution)/shard_map/ppermute | solution.py:766
  9.3 6.6 %collective-permute-start.4 = (bf16[112,128]{1,0:T(8,128)(2,1)S(1)}, bf16[112,128]{1,0:T(8,128)(2,1)S(1)}, u32[]{:S(2)}, u32[]{:S(2)}) collective-permute-start(bf16[112,128]{1,0:T(8,128)(2,1)S(1)} %get-tuple-element.45), channel_id=1, source_target_pairs={{0,3},{1,2},{2,5},{3,4},{4,7},{5,6},{6,1},{7,0},{8,15},{9,14},{10,... | collective-permute-start | bytes 86024 | tf_op jit(solution)/shard_map/ppermute | solution.py:767
  10.8 4.7 %collective-permute-start.5 = (f32[16,128]{1,0:T(8,128)S(1)}, f32[16,128]{1,0:T(8,128)S(1)}, u32[]{:S(2)}, u32[]{:S(2)}) collective-permute-start(f32[16,128]{1,0:T(8,128)S(1)} %get-tuple-element.46.obs_ref), channel_id=1, source_target_pairs={{0,8},{8,0},{16,24},{24,16},{1,9},{9,1},{17,25},{25,17},{2,10},{10... | collective-permute-start | bytes 24584 | tf_op jit(solution)/shard_map/ppermute | solution.py:749
  17.7 7.7 %collective-permute-start.6 = (bf16[304,128]{1,0:T(8,128)(2,1)S(1)}, bf16[304,128]{1,0:T(8,128)(2,1)S(1)}, u32[]{:S(2)}, u32[]{:S(2)}) collective-permute-start(bf16[304,128]{1,0:T(8,128)(2,1)S(1)} %get-tuple-element.48), channel_id=1, source_target_pairs={{0,1},{1,0},{8,9},{9,8},{16,17},{17,16},{24,25},{25,24},{2,3},{3,2... | collective-permute-start | bytes 233480 | tf_op jit(solution)/shard_map/ppermute | solution.py:792
  18.7 4.9 %collective-permute-start.7 = (bf16[256,128]{1,0:T(8,128)(2,1)S(1)}, bf16[256,128]{1,0:T(8,128)(2,1)S(1)}, u32[]{:S(2)}, u32[]{:S(2)}) collective-permute-start(bf16[256,128]{1,0:T(8,128)(2,1)S(1)} %get-tuple-element.49), channel_id=1, source_target_pairs={{0,16},{1,17},{8,24},{9,25},{16,0},{17,1},{24,8},{25,9},{2,18},{3,... | collective-permute-start | bytes 196616 | tf_op jit(solution)/shard_map/ppermute | solution.py:792
  20.2 5.2 %collective-permute-start.8 = (bf16[256,128]{1,0:T(8,128)(2,1)S(1)}, bf16[256,128]{1,0:T(8,128)(2,1)S(1)}, u32[]{:S(2)}, u32[]{:S(2)}) collective-permute-start(bf16[256,128]{1,0:T(8,128)(2,1)S(1)} %get-tuple-element.50), channel_id=1, source_target_pairs={{0,17},{1,16},{8,25},{9,24},{16,1},{17,0},{24,9},{25,8},{2,19},{3,... | collective-permute-start | bytes 196616 | tf_op jit(solution)/shard_map/ppermute | solution.py:792
  27.9 1.4 %collective-permute-start.9 = (bf16[4,2,64,128]{3,2,1,0:T(8,128)(2,1)S(1)}, bf16[4,2,64,128]{3,2,1,0:T(8,128)(2,1)S(1)}, u32[]{:S(2)}, u32[]{:S(2)}) collective-permute-start(bf16[4,2,64,128]{3,2,1,0:T(8,128)(2,1)S(1)} %get-tuple-element.51), channel_id=1, source_target_pairs={{0,8},{8,0},{16,24},{24,16},{1,9},{9,1},{17,25},{25,17},{2,10},{10... | collective-permute-start | bytes 393224 | tf_op jit(solution)/shard_map/ppermute | solution.py:807
  29.3 4.3 %collective-permute-start.10 = (bf16[2,2,64,128]{3,2,1,0:T(8,128)(2,1)S(1)}, bf16[2,2,64,128]{3,2,1,0:T(8,128)(2,1)S(1)}, u32[]{:S(2)}, u32[]{:S(2)}) collective-permute-start(bf16[2,2,64,128]{3,2,1,0:T(8,128)(2,1)S(1)} %get-tuple-element.60), channel_id=1, source_target_pairs={{0,1},{1,0},{8,9},{9,8},{16,17},{17,16},{24,25},{25,24},{2,3},{3,2... | collective-permute-start | bytes 196616 | tf_op jit(solution)/shard_map/ppermute | solution.py:792
  30.4 4.6 %collective-permute-start.11 = (bf16[2,2,64,128]{3,2,1,0:T(8,128)(2,1)S(1)}, bf16[2,2,64,128]{3,2,1,0:T(8,128)(2,1)S(1)}, u32[]{:S(2)}, u32[]{:S(2)}) collective-permute-start(bf16[2,2,64,128]{3,2,1,0:T(8,128)(2,1)S(1)} %get-tuple-element.61), channel_id=1, source_target_pairs={{0,16},{1,17},{8,24},{9,25},{16,0},{17,1},{24,8},{25,9},{2,18},{3,... | collective-permute-start | bytes 196616 | tf_op jit(solution)/shard_map/ppermute | solution.py:792
  31.0 5.2 %collective-permute-start.12 = (bf16[2,2,64,128]{3,2,1,0:T(8,128)(2,1)S(1)}, bf16[2,2,64,128]{3,2,1,0:T(8,128)(2,1)S(1)}, u32[]{:S(2)}, u32[]{:S(2)}) collective-permute-start(bf16[2,2,64,128]{3,2,1,0:T(8,128)(2,1)S(1)} %get-tuple-element.62), channel_id=1, source_target_pairs={{0,17},{1,16},{8,25},{9,24},{16,1},{17,0},{24,9},{25,8},{2,19},{3,... | collective-permute-start | bytes 196616 | tf_op jit(solution)/shard_map/ppermute | solution.py:792

commit v5 on v4

--- a/solution.py
+++ b/solution.py
@@ -211,11 +211,13 @@
 LANES = 128
 HALO = 4
 OCTET = 8
+GROUP = 32
 DOMAIN = 3 * HALO
 EXTENT = LANES + 2 * OCTET
 VMEM_GRANT = 24 << 20
 LARGEST = 6.0
 WIDENING = 11.06 / LARGEST
+PRIOR_COPIES = 4
 STAGE_FACTORS = (1.0 / 4.0, 1.0 / 3.0, 1.0 / 2.0, 1.0)
 
 
@@ -298,11 +300,15 @@
         for i, (source, target) in enumerate(
             (
                 (cells_ref, cells_vmem), (values_ref, values_vmem), (errors_ref, errors_vmem),
-                (wind_ref, wind_out_ref), (prior_ref, own_ref),
+                (wind_ref, wind_out_ref),
             )
         )
     ]
-    for copy in copies:
+    share = own_ref.shape[0] // PRIOR_COPIES
+    for i in range(PRIOR_COPIES):
+        part = pl.ds(i * share, share)
+        copies.append(pltpu.make_async_copy(prior_ref.at[part], own_ref.at[part], sems.at[4 + i]))
+    for copy in copies[4:] + copies[:4]:
         copy.start()
     obs_ref[...] = jnp.zeros_like(obs_ref)
     for copy in copies[:4]:
@@ -316,7 +322,8 @@
             rows_ref[pl.ds(block * HALO + j, 1), :] = wind_out_ref[pl.ds(row, 1), :]
     for i, part in enumerate(split_three(wind_scale(odd, rows_ref[...]))):
         same_ref[pl.ds(s.halo_rows + i * s.wind_rows, s.wind_rows), :] = part.astype(jnp.float32)
-    copies[4].wait()
+    for copy in copies[4:]:
+        copy.wait()
     for parity, out_ref in ((odd, same_ref), (1 - odd, other_ref)):
         for j in range(HALO):
             row = tile_row(parity, 2 * HALO + j)
@@ -336,21 +343,46 @@
         store(second, both[:, LANES:])
 
 
-def pack_edges_kernel(s, own_ref, sib_ref, wind_ref, same_ref, field_ref, side_ref, corner_ref, winds_ref):
+def column_ends(x):
+    turned = padded_rows(x).T
+    return jnp.concatenate([turned[LANES - HALO :], turned[:HALO]], axis=0)
+
+
+def packed_ends(x):
+    parts = [part.astype(jnp.float32) for part in split_three(column_ends(x))]
+    packed = parts[0] + pltpu.roll(parts[1], GROUP, 1) + pltpu.roll(parts[2], 2 * GROUP, 1)
+    return jnp.concatenate([packed, jnp.zeros_like(packed)], axis=0).astype(jnp.bfloat16)
+
+
+def unpacked_ends(x):
+    packed = x.astype(jnp.float32)[: 2 * HALO]
+    return packed + pltpu.roll(packed, LANES - GROUP, 1) + pltpu.roll(packed, LANES - 2 * GROUP, 1)
+
+
+def pack_edges_kernel(s, own_ref, sib_ref, wind_ref, same_ref, field_ref, side_ref, corner_ref):
     odd = lax.rem(lax.axis_index("mem"), 2)
     for layer in range(s.layers):
+        rows = []
         for j in range(HALO, DOMAIN):
             value = columns_first(s, odd, own_ref, sib_ref, layer, j)
             field_ref[pl.ds(s.field_at(layer, j) + OCTET, LANES), :] = value
-            to = (layer * 2 * HALO + j - HALO) * OCTET
-            side_ref[pl.ds(to, HALO), :] = value[LANES - HALO :]
-            side_ref[pl.ds(to + HALO, HALO), :] = value[:HALO]
-        to, at = layer * HALO * OCTET, (layer * 2 * HALO + HALO) * OCTET
-        corner_ref[pl.ds(to, HALO * OCTET), :] = side_ref[pl.ds(at, HALO * OCTET), :].astype(jnp.bfloat16)
-    winds = same_ref[pl.ds(s.halo_rows, 3 * s.wind_rows), :]
-    corner_ref[pl.ds(s.corner_rows, 3 * s.wind_rows), :] = winds.astype(jnp.bfloat16)
+            rows += [value[LANES - HALO :], value[:HALO]]
+        count = len(rows) // 2
+        high, low = split_two(jnp.concatenate(rows, axis=0))
+        side_ref[pl.ds(layer * 2 * HALO * OCTET, 2 * HALO * OCTET), :] = high
+        low = low.astype(jnp.float32)
+        nearest = [low[i * OCTET + 2 : i * OCTET + 6] for i in range(2 * HALO)]
+        at = s.side_rows + 2 * OCTET + layer * 2 * HALO * HALO
+        side_ref[pl.ds(at, 2 * HALO * HALO), :] = jnp.concatenate(nearest, axis=0).astype(jnp.bfloat16)
+        corner_ref[pl.ds(layer * HALO * OCTET, HALO * OCTET), :] = jnp.concatenate(rows[count:], axis=0).astype(jnp.bfloat16)
+    near = [same_ref[pl.ds(s.halo_rows + i * s.wind_rows, s.wind_rows), :] for i in range(3)]
+    corner_ref[pl.ds(s.corner_rows, 2 * OCTET), :] = packed_ends(near[0] + near[1] + near[2])
+    side_ref[pl.ds(s.side_rows, 2 * OCTET), :] = packed_ends(wind_scale(odd, wind_ref[...]))
+
+
+def spread_winds_kernel(s, wind_ref, winds_ref):
+    odd = lax.rem(lax.axis_index("mem"), 2)
     scaled = wind_scale(odd, wind_ref[...])
-    side_ref[pl.ds(s.side_rows, 2 * s.layers * s.rows), :] = scaled
 
     def store(row, value):
         at = s.wind_at(row // s.rows // s.layers, row // s.rows % s.layers, domain_row(odd, row % s.rows))
@@ -360,11 +392,10 @@
     spread(split_three(scaled), rows, list(range(rows)), store)
 
 
-def set_wind_edges(winds_ref, turned, row, at):
-    edge = jnp.concatenate([turned[LANES - OCTET :], turned[:OCTET]], axis=0)
-    value = jnp.broadcast_to(edge[:, row : row + 1], (2 * OCTET, LANES))
-    winds_ref[pl.ds(at + HALO, HALO), :] = value[HALO : 2 * HALO]
-    winds_ref[pl.ds(at + OCTET + LANES, HALO), :] = value[OCTET : OCTET + HALO]
+def set_wind_edges(winds_ref, ends, row, at):
+    value = jnp.broadcast_to(ends[:, row : row + 1], (2 * HALO, LANES))
+    winds_ref[pl.ds(at + HALO, HALO), :] = value[:HALO]
+    winds_ref[pl.ds(at + OCTET + LANES, HALO), :] = value[HALO:]
 
 
 def padded_rows(x):
@@ -415,10 +446,15 @@
 def inner_kernel(s, _, __, side_ref, field_ref, winds_ref, first_ref, second_ref):
     odd = lax.rem(lax.axis_index("mem"), 2)
     for layer in range(s.layers):
+        edges = side_ref[pl.ds(layer * 2 * HALO * OCTET, 2 * HALO * OCTET), :].astype(jnp.float32)
+        at = s.side_rows + 2 * OCTET + layer * 2 * HALO * HALO
+        low = side_ref[pl.ds(at, 2 * HALO * HALO), :].astype(jnp.float32)
         for j in range(HALO, DOMAIN):
-            edge = side_ref[pl.ds((layer * 2 * HALO + j - HALO) * OCTET, OCTET), :]
-            set_field_edges(s, field_ref, layer, j, edge)
-    beside = padded_rows(side_ref[pl.ds(s.side_rows, 2 * s.layers * s.rows), :]).T
+            i = j - HALO
+            edge = edges[i * OCTET : (i + 1) * OCTET]
+            nearest = edge[2:6] + low[i * HALO : (i + 1) * HALO]
+            set_field_edges(s, field_ref, layer, j, jnp.concatenate([edge[:2], nearest, edge[6:]], axis=0))
+    beside = unpacked_ends(side_ref[pl.ds(s.side_rows, 2 * OCTET), :])
     for block in range(2 * s.layers):
         for row in range(s.rows):
             at = s.wind_at(block // s.layers, block % s.layers, domain_row(odd, row))
@@ -454,8 +490,7 @@
         corner = corner_ref[pl.ds(layer * HALO * OCTET, HALO * OCTET), :].astype(jnp.float32)
         for j in range(HALO):
             set_field_edges(s, field_ref, layer, j, corner[j * OCTET : (j + 1) * OCTET])
-    far = [corner_ref[pl.ds(s.corner_rows + i * s.wind_rows, s.wind_rows), :].astype(jnp.float32) for i in range(3)]
-    beyond = padded_rows(far[0] + far[1] + far[2]).T
+    beyond = unpacked_ends(corner_ref[pl.ds(s.corner_rows, 2 * OCTET), :])
     targets = [block * HALO + j for block in range(2 * s.layers) for j in range(1, HALO)]
 
     def wind_at(row):
@@ -662,19 +697,30 @@
 
 
 def place_rows_kernel(s, *refs):
-    pieces, out_ref, rows_ref = refs[:4], refs[4], refs[5]
+    pieces, out_ref, rows_ref, packed_ref, sems = refs[:4], refs[4], refs[5], refs[6], refs[7]
     mem = lax.axis_index("mem")
     odd = lax.rem(mem, 2)
     place = (mem // 2) * 2 + lax.axis_index("gy")
-    for d in range(4):
-        for part, parity in ((0, odd), (1, 1 - odd)):
-            row = 4 * parity + jnp.bitwise_xor(place, d)
-            for layer in range(s.layers):
-                for octet in range(0, s.local // OCTET, 2):
-                    value = pieces[d][part, layer, octet * OCTET : (octet + 2) * OCTET, :].astype(jnp.float32)
-                    start = octet * OCTET * s.per_member + layer * s.rows + row
-                    rows_ref[pl.ds(start, 2 * OCTET, stride=s.per_member), :] = value
-    out_ref[...] = rows_ref[...].astype(jnp.bfloat16).reshape(out_ref.shape)
+    count = 2 * OCTET
+    copies = []
+    for first in range(0, s.local, count):
+        for d in range(4):
+            for part, parity in ((0, odd), (1, 1 - odd)):
+                row = 4 * parity + jnp.bitwise_xor(place, d)
+                for layer in range(s.layers):
+                    value = pieces[d][part, layer, first : first + count, :].astype(jnp.float32)
+                    start = first * s.per_member + layer * s.rows + row
+                    rows_ref[pl.ds(start, count, stride=s.per_member), :] = value
+        rows = rows_ref[pl.ds(first * s.per_member, count * s.per_member), :]
+        packed_ref[pl.ds(first, count)] = rows.astype(jnp.bfloat16).reshape(count, s.layers, s.rows, LANES)
+        copies.append(
+            pltpu.make_async_copy(
+                packed_ref.at[pl.ds(first, count)], out_ref.at[pl.ds(first, count)], sems.at[first // count]
+            )
+        )
+        copies[-1].start()
+    for copy in copies:
+        copy.wait()
 
 
 def vmem_call(kernel, outs, scratch, *args, aliases=None):
@@ -731,7 +777,7 @@
             pltpu.VMEM((1, count), f32),
             pltpu.VMEM((1, count), f32),
             pltpu.VMEM((s.wind_rows, LANES), f32),
-            pltpu.SemaphoreType.DMA((5,)),
+            pltpu.SemaphoreType.DMA((4 + PRIOR_COPIES,)),
         ],
         compiler_params=pltpu.CompilerParams(vmem_limit_bytes=VMEM_GRANT),
     )(
@@ -752,17 +798,17 @@
     winds_shape = shaped((2 * layers * DOMAIN * EXTENT, LANES), f32)
     same = lax.ppermute(same_out.astype(jnp.float16), ("mem", "gx"), along).astype(f32)
     other = lax.ppermute(other_out.astype(jnp.float16), ("mem", "gx"), along_other).astype(f32)
-    field, side_out, corner_out, winds = vmem_call(
+    field, side_out, corner_out = vmem_call(
         functools.partial(pack_edges_kernel, s),
         (
             field_shape,
-            shaped((s.side_rows + 2 * layers * rows, LANES), f32),
-            shaped((s.corner_rows + 3 * s.wind_rows, LANES), bf16),
-            winds_shape,
+            shaped((s.side_rows + 2 * OCTET + layers * 2 * HALO * HALO, LANES), bf16),
+            shaped((s.corner_rows + 2 * OCTET, LANES), bf16),
         ),
         [],
         own, sib, wind, same_out,
     )
+    winds = vmem_call(functools.partial(spread_winds_kernel, s), winds_shape, [], wind)
     side = lax.ppermute(side_out, "gy", across)
     corner = lax.ppermute(corner_out, ("mem", "gx", "gy"), diagonal)
     field, winds, first, second = vmem_call(
@@ -812,12 +858,18 @@
     answers = vmem_call(
         join_kernel, (answer, answer, answer, answer), [], received, *answers, aliases={1 + d: d for d in range(4)}
     )
-    return vmem_call(
+    return pl.pallas_call(
         functools.partial(place_rows_kernel, s),
-        shaped((local, layers, rows, columns), bf16),
-        [((local * layers * rows, LANES), f32)],
-        *exchange(answers),
-    )
+        out_shape=shaped((local, layers, rows, columns), bf16),
+        in_specs=[vmem] * 4,
+        out_specs=hbm,
+        scratch_shapes=[
+            pltpu.VMEM((local * layers * rows, LANES), f32),
+            pltpu.VMEM((local, layers, rows, columns), bf16),
+            pltpu.SemaphoreType.DMA((local // (2 * OCTET),)),
+        ],
+        compiler_params=pltpu.CompilerParams(vmem_limit_bytes=VMEM_GRANT),
+    )(*exchange(answers))
 
 
 def on_device(prior_sample_set, flow_speeds, observed_cells, observed_values, error_variance):

time: 37.3 us -> 36.9 us (0.989)
  waiting for transfers between devices: 12.1 us -> 11.6 us
    pallas_call x0 -> x1, Pallas kernels: none -> 0.87 us  [on_device_tile(): pl.pallas_call(functools.partial(place_rows_kernel, s), out_shape=shaped(...]
    pallas_call x7, Pallas kernels: 7.75 us -> 6.9 us  [vmem_call(): pl.pallas_call(kernel, out_shape=outs, in_specs=[spec] * len(args), out_s...]
    ppermute x1, waiting for transfers between devices: 3.16 us -> 2.78 us  [on_device_tile(): lax.ppermute(other_out.astype(jnp.float16), ('mem', 'gx'), along_other)]
  transfers between devices with their start and end apart: 13 -> 13, of which waited for: 8 -> 8; matrix products, arithmetic and copies ran while one was open for 0% -> 0% of each run, Pallas kernels for 10% -> 11%
where the time goes in v5:
time: 36.9 us; the launch traced here: 36.7 us
  starting transfers between devices  15.7 us (43%)
  waiting for transfers between devices  11.6 us (31%)
  Pallas kernels  9.19 us (25%)
    ppermute x6, waiting for transfers between devices, exchange(): arrived.append(lax.ppermute(parts[d], ('mem', 'gy'), flip(d)))  7.43 us
    ppermute x6, starting transfers between devices, exchange(): arrived.append(lax.ppermute(parts[d], ('mem', 'gy'), flip(d)))  7.11 us
    pallas_call x7, Pallas kernels, vmem_call(): pl.pallas_call(kernel, out_shape=outs, in_specs=[spec] * len(args), out_s...  6.9 us
    ppermute x1, waiting for transfers between devices, on_device_tile(): lax.ppermute(other_out.astype(jnp.float16), ('mem', 'gx'), along_other)  2.78 us
    ppermute x1, starting transfers between devices, on_device_tile(): lax.ppermute(same_out.astype(jnp.float16), ('mem', 'gx'), along).astype(f32)  2.62 us
    ppermute x1, starting transfers between devices, on_device_tile(): lax.ppermute(other_out.astype(jnp.float16), ('mem', 'gx'), along_other)  2.37 us
    ppermute x1, starting transfers between devices, on_device_tile(): side = lax.ppermute(side_out, 'gy', across)  1.53 us
    ppermute x1, starting transfers between devices, on_device_tile(): corner = lax.ppermute(corner_out, ('mem', 'gx', 'gy'), diagonal)  1.52 us
  transfers between devices with their start and end apart: 13, of which 8 were waited for; matrix products, arithmetic and copies ran while one was open for 0% of the time, Pallas kernels for 11%

profile of v5, /device:TPU:0, one launch (start us, length us, event | category | flops | bytes accessed | tf_op | source)
XLA Modules:
  0.0 36.7 jit_solution(7480591154497732888)
XLA Ops:
  0.0 0.5 %collective-permute-start = (f32[64,2,8,128]{3,2,1,0:T(8,128)}, f32[64,2,8,128]{3,2,1,0:T(8,128)S(1)}, u32[]{:S(2)}, u32[]{:S(2)}) collective-permute-start(f32[64,2,8,128]{3,2,1,0:T(8,128)} %param.5), channel_id=1, source_target_pairs={{0,8},{8,0},{16,24},{24,16},{1,9},{9,1},{17,25},{25,17},{2,10},{10... | collective-permute-start | bytes 1572872 | tf_op jit(solution)/shard_map/ppermute | solution.py:761
  0.5 1.4 %shard_map.55 = (f32[1024,128]{1,0:T(8,128)S(1)}, f32[32,128]{1,0:T(8,128)S(1)}, f32[16,128]{1,0:T(8,128)S(1)}, f32[560,128]{1,0:T(8,128)S(1)}, f32[512,128]{1,0:T(8,128)S(1)}) custom-call(f32[1024,128]{1,0:T(8,128)} %bitcast.7, f32[32,128]{1,0:T(8,128)} %bitcast.8, s32[1,128]{1,0:T(1,128)} %bitcast.9, f32[1,128]{1,0:T(1,128)} %bitcast.10, f32[1,128]{1,0:T(1,128)} %bitcast.11), custom_call_target="tpu_custom_call" | custom-call | tf_op jit(solution)/shard_map/pallas_call | solution.py:764
  2.0 2.6 %collective-permute-start.2 = (f16[560,128]{1,0:T(8,128)(2,1)S(1)}, f16[560,128]{1,0:T(8,128)(2,1)S(1)}, u32[]{:S(2)}, u32[]{:S(2)}) collective-permute-start(f16[560,128]{1,0:T(8,128)(2,1)S(1)} %convert_element_type.12), channel_id=1, source_target_pairs={{0,2},{2,4},{4,6},{6,0},{8,14},{10,8},{12,10},{14,12},{16,18},{18,... | collective-permute-start | bytes 430088 | tf_op jit(solution)/shard_map/ppermute | solution.py:799
  4.6 2.4 %collective-permute-start.3 = (f16[512,128]{1,0:T(8,128)(2,1)S(1)}, f16[512,128]{1,0:T(8,128)(2,1)S(1)}, u32[]{:S(2)}, u32[]{:S(2)}) collective-permute-start(f16[512,128]{1,0:T(8,128)(2,1)S(1)} %convert_element_type.14), channel_id=1, source_target_pairs={{0,14},{2,8},{4,10},{6,12},{8,2},{10,4},{12,6},{14,0},{16,30},{18,... | collective-permute-start | bytes 393224 | tf_op jit(solution)/shard_map/ppermute | solution.py:800
  7.0 0.7 %shard_map.56 = (f32[3456,128]{1,0:T(8,128)S(1)}, bf16[208,128]{1,0:T(8,128)(2,1)S(1)}, bf16[80,128]{1,0:T(8,128)(2,1)S(1)}) custom-call(f32[1024,128]{1,0:T(8,128)S(1)} %get-tuple-element.33.own_ref, f32[1024,128]{1,0:T(8,128)S(1)} %bitcast.6, f32[32,128]{1,0:T(8,128)S(1)} %get-tuple-element.34.wind_ref, f32[560,128]{1,0:T(8,128)S(1)} %get-tuple-element.35.same_ref), custom_call_target="tpu_custom_call" | custom-call | tf_op jit(solution)/shard_map/pallas_call | solution.py:728
  7.7 1.5 %collective-permute-start.1 = (bf16[208,128]{1,0:T(8,128)(2,1)S(1)}, bf16[208,128]{1,0:T(8,128)(2,1)S(1)}, u32[]{:S(2)}, u32[]{:S(2)}) collective-permute-start(bf16[208,128]{1,0:T(8,128)(2,1)S(1)} %get-tuple-element.37), channel_id=1, source_target_pairs={{0,1},{1,0},{2,3},{3,2},{4,5},{5,4},{6,7},{7,6},{8,9},{9,8},{10,11... | collective-permute-start | bytes 159752 | tf_op jit(solution)/shard_map/ppermute | solution.py:812
  9.2 1.5 %collective-permute-start.4 = (bf16[80,128]{1,0:T(8,128)(2,1)S(1)}, bf16[80,128]{1,0:T(8,128)(2,1)S(1)}, u32[]{:S(2)}, u32[]{:S(2)}) collective-permute-start(bf16[80,128]{1,0:T(8,128)(2,1)S(1)} %get-tuple-element.43), channel_id=1, source_target_pairs={{0,3},{1,2},{2,5},{3,4},{4,7},{5,6},{6,1},{7,0},{8,15},{9,14},{10,... | collective-permute-start | bytes 61448 | tf_op jit(solution)/shard_map/ppermute | solution.py:813
  10.7 0.0 collective-permute-start.5
  10.7 0.5 %shard_map.57.__ = f32[6912,128]{1,0:T(8,128)S(1)} custom-call(f32[32,128]{1,0:T(8,128)S(1)} %get-tuple-element.34.wind_ref), custom_call_target="tpu_custom_call" | custom-call | tf_op jit(solution)/shard_map/pallas_call | solution.py:728
  11.2 2.8 %collective-permute-done.3 = f16[512,128]{1,0:T(8,128)(2,1)S(1)} collective-permute-done((f16[512,128]{1,0:T(8,128)(2,1)S(1)}, f16[512,128]{1,0:T(8,128)(2,1)S(1)}, u32[]{:S(2)}, u32[]{:S(2)}) %collective-permute-start.3) | collective-permute-done | bytes 131104 | tf_op jit(solution)/shard_map/ppermute | solution.py:800
  14.0 0.0 collective-permute-done.2
  14.0 0.0 collective-permute-done.1.side_ref
  14.1 1.2 %shard_map.58 = (f32[3456,128]{1,0:T(8,128)S(1)}, f32[6912,128]{1,0:T(8,128)S(1)}, f32[3456,128]{1,0:T(8,128)S(1)}, f32[3456,128]{1,0:T(8,128)S(1)}) custom-call(f32[3456,128]{1,0:T(8,128)S(1)} %get-tuple-element.36._, f32[6912,128]{1,0:T(8,128)S(1)} %shard_map.57.__, ...), custom_call_target="tpu_custom_call", output_to_operand_aliasing={{0}: (0, {}), {1}: (1, {})} | custom-call | tf_op jit(solution)/shard_map/pallas_call | solution.py:728
  15.3 0.0 collective-permute-done.5.obs_ref
  15.3 0.4 %collective-permute-done.4.corner_ref = bf16[80,128]{1,0:T(8,128)(2,1)S(1)} collective-permute-done((bf16[80,128]{1,0:T(8,128)(2,1)S(1)}, bf16[80,128]{1,0:T(8,128)(2,1)S(1)}, u32[]{:S(2)}, u32[]{:S(2)}) %collective-permute-start.4) | collective-permute-done | bytes 20512 | tf_op jit(solution)/shard_map/ppermute | solution.py:813
  15.7 1.7 %shard_map.59 = (bf16[256,128]{1,0:T(8,128)(2,1)S(1)}, bf16[304,128]{1,0:T(8,128)(2,1)S(1)}, bf16[256,128]{1,0:T(8,128)(2,1)S(1)}, bf16[256,128]{1,0:T(8,128)(2,...) custom-call(f32[3456,128]{1,0:T(8,128)S(1)} %get-tuple-element.38._,, ...), custom_call_target="tpu_custom_call", output_to_operand_aliasing={{4}: (0, {}), {5}: (1, {}), {6}: (2, {}), {7}: (3, {})} | custom-call | tf_op jit(solution)/shard_map/pallas_call | solution.py:728
  17.4 1.0 %collective-permute-start.6 = (bf16[304,128]{1,0:T(8,128)(2,1)S(1)}, bf16[304,128]{1,0:T(8,128)(2,1)S(1)}, u32[]{:S(2)}, u32[]{:S(2)}) collective-permute-start(bf16[304,128]{1,0:T(8,128)(2,1)S(1)} %get-tuple-element.46), channel_id=1, source_target_pairs={{0,1},{1,0},{8,9},{9,8},{16,17},{17,16},{24,25},{25,24},{2,3},{3,2... | collective-permute-start | bytes 233480 | tf_op jit(solution)/shard_map/ppermute | solution.py:838
  18.4 1.5 %collective-permute-start.7 = (bf16[256,128]{1,0:T(8,128)(2,1)S(1)}, bf16[256,128]{1,0:T(8,128)(2,1)S(1)}, u32[]{:S(2)}, u32[]{:S(2)}) collective-permute-start(bf16[256,128]{1,0:T(8,128)(2,1)S(1)} %get-tuple-element.47), channel_id=1, source_target_pairs={{0,16},{1,17},{8,24},{9,25},{16,0},{17,1},{24,8},{25,9},{2,18},{3,... | collective-permute-start | bytes 196616 | tf_op jit(solution)/shard_map/ppermute | solution.py:838
  19.9 1.1 %collective-permute-start.8 = (bf16[256,128]{1,0:T(8,128)(2,1)S(1)}, bf16[256,128]{1,0:T(8,128)(2,1)S(1)}, u32[]{:S(2)}, u32[]{:S(2)}) collective-permute-start(bf16[256,128]{1,0:T(8,128)(2,1)S(1)} %get-tuple-element.48), channel_id=1, source_target_pairs={{0,17},{1,16},{8,25},{9,24},{16,1},{17,0},{24,9},{25,8},{2,19},{3,... | collective-permute-start | bytes 196616 | tf_op jit(solution)/shard_map/ppermute | solution.py:838
  21.0 2.4 %collective-permute-done.7.piece2_ref = bf16[256,128]{1,0:T(8,128)(2,1)S(1)} collective-permute-done((bf16[256,128]{1,0:T(8,128)(2,1)S(1)}, bf16[256,128]{1,0:T(8,128)(2,1)S(1)}, u32[]{:S(2)}, u32[]{:S(2)}) %collective-permute-start.7) | collective-permute-done | bytes 65568 | tf_op jit(solution)/shard_map/ppermute | solution.py:838
  23.4 1.7 %collective-permute-done.8.piece3_ref = bf16[256,128]{1,0:T(8,128)(2,1)S(1)} collective-permute-done((bf16[256,128]{1,0:T(8,128)(2,1)S(1)}, bf16[256,128]{1,0:T(8,128)(2,1)S(1)}, u32[]{:S(2)}, u32[]{:S(2)}) %collective-permute-start.8) | collective-permute-done | bytes 65568 | tf_op jit(solution)/shard_map/ppermute | solution.py:838
  25.1 2.5 %shard_map.60 = (bf16[4,2,64,128]{3,2,1,0:T(8,128)(2,1)S(1)}, bf16[512,256]{1,0:T(8,128)(2,1)S(1)}, bf16[256,256]{1,0:T(8,128)(2,1)S(1)}, f32[8,512]{1,0:T(8,128)S(1)}) custom-call(bf16[256,128]{1,0:T(8,128)(2,1)S(1)} %get-tuple-element.45.piece0_ref, bf16[304,128]{1,0:T(8,128)(2,1)S(1)} %collective-permute-done.6.piece1_ref, ...), custom_call_target="tpu_custom_call" | custom-call | tf_op jit(solution)/shard_map/pallas_call | solution.py:728
  27.6 0.1 collective-permute-start.9
  27.6 0.3 shard_map.61
  27.9 1.1 %collective-permute-done.9.received_ref = bf16[4,2,64,128]{3,2,1,0:T(8,128)(2,1)S(1)} collective-permute-done((bf16[4,2,64,128]{3,2,1,0:T(8,128)(2,1)S(1)}, bf16[4,2,64,128]{3,2,1,0:T(8,128)(2,1)S(1)}, u32[]{:S(2)}, u32[]{:S(2)}) %collective-permute-start.9) | collective-permute-done | bytes 131104 | tf_op jit(solution)/shard_map/ppermute | solution.py:853
  29.0 1.1 %collective-permute-start.10 = (bf16[2,2,64,128]{3,2,1,0:T(8,128)(2,1)S(1)}, bf16[2,2,64,128]{3,2,1,0:T(8,128)(2,1)S(1)}, u32[]{:S(2)}, u32[]{:S(2)}) collective-permute-start(bf16[2,2,64,128]{3,2,1,0:T(8,128)(2,1)S(1)} %get-tuple-element.58), channel_id=1, source_target_pairs={{0,1},{1,0},{8,9},{9,8},{16,17},{17,16},{24,25},{25,24},{2,3},{3,2... | collective-permute-start | bytes 196616 | tf_op jit(solution)/shard_map/ppermute | solution.py:838
  30.1 0.5 %collective-permute-start.11 = (bf16[2,2,64,128]{3,2,1,0:T(8,128)(2,1)S(1)}, bf16[2,2,64,128]{3,2,1,0:T(8,128)(2,1)S(1)}, u32[]{:S(2)}, u32[]{:S(2)}) collective-permute-start(bf16[2,2,64,128]{3,2,1,0:T(8,128)(2,1)S(1)} %get-tuple-element.59), channel_id=1, source_target_pairs={{0,16},{1,17},{8,24},{9,25},{16,0},{17,1},{24,8},{25,9},{2,18},{3,... | collective-permute-start | bytes 196616 | tf_op jit(solution)/shard_map/ppermute | solution.py:838
  30.7 1.9 %collective-permute-start.12 = (bf16[2,2,64,128]{3,2,1,0:T(8,128)(2,1)S(1)}, bf16[2,2,64,128]{3,2,1,0:T(8,128)(2,1)S(1)}, u32[]{:S(2)}, u32[]{:S(2)}) collective-permute-start(bf16[2,2,64,128]{3,2,1,0:T(8,128)(2,1)S(1)} %get-tuple-element.60), channel_id=1, source_target_pairs={{0,17},{1,16},{8,25},{9,24},{16,1},{17,0},{24,9},{25,8},{2,19},{3,... | collective-permute-start | bytes 196616 | tf_op jit(solution)/shard_map/ppermute | solution.py:838
  32.5 0.8 %collective-permute-done.10.refs_1_ = bf16[2,2,64,128]{3,2,1,0:T(8,128)(2,1)S(1)} collective-permute-done((bf16[2,2,64,128]{3,2,1,0:T(8,128)(2,1)S(1)}, bf16[2,2,64,128]{3,2,1,0:T(8,128)(2,1)S(1)}, u32[]{:S(2)}, u32[]{:S(2)}) %collective-permute-start.10) | collective-permute-done | bytes 65568 | tf_op jit(solution)/shard_map/ppermute | solution.py:838
  33.3 1.4 %collective-permute-done.11.refs_2_ = bf16[2,2,64,128]{3,2,1,0:T(8,128)(2,1)S(1)} collective-permute-done((bf16[2,2,64,128]{3,2,1,0:T(8,128)(2,1)S(1)}, bf16[2,2,64,128]{3,2,1,0:T(8,128)(2,1)S(1)}, u32[]{:S(2)}, u32[]{:S(2)}) %collective-permute-start.11) | collective-permute-done | bytes 65568 | tf_op jit(solution)/shard_map/ppermute | solution.py:838
  34.7 1.2 %collective-permute-done.12.refs_3_ = bf16[2,2,64,128]{3,2,1,0:T(8,128)(2,1)S(1)} collective-permute-done((bf16[2,2,64,128]{3,2,1,0:T(8,128)(2,1)S(1)}, bf16[2,2,64,128]{3,2,1,0:T(8,128)(2,1)S(1)}, u32[]{:S(2)}, u32[]{:S(2)}) %collective-permute-start.12) | collective-permute-done | bytes 65568 | tf_op jit(solution)/shard_map/ppermute | solution.py:838
  35.9 0.9 %shard_map.63 = bf16[64,2,8,128]{3,2,1,0:T(8,128)(2,1)} custom-call(bf16[2,2,64,128]{3,2,1,0:T(8,128)(2,1)S(1)} %get-tuple-element.57.refs_0_, bf16[2,2,64,128]{3,2,1,0:T(8,128)(2,1)S(1)} %collective-permute-done.10.refs_1_, bf16[2,2,64,128]{3,2,1,0:T(8,128)(2,1)S(1)} %collective-permute-done.11.refs_2_, ...), custom_call_target="tpu_custom_call" | custom-call | tf_op jit(solution)/shard_map/pallas_call | solution.py:861
  (7 shorter events, 0.1 us)
Async XLA Ops:
  0.0 7.0 %collective-permute-start = (f32[64,2,8,128]{3,2,1,0:T(8,128)}, f32[64,2,8,128]{3,2,1,0:T(8,128)S(1)}, u32[]{:S(2)}, u32[]{:S(2)}) collective-permute-start(f32[64,2,8,128]{3,2,1,0:T(8,128)} %param.5), channel_id=1, source_target_pairs={{0,8},{8,0},{16,24},{24,16},{1,9},{9,1},{17,25},{25,17},{2,10},{10... | collective-permute-start | bytes 1572872 | tf_op jit(solution)/shard_map/ppermute | solution.py:761
  2.0 12.0 %collective-permute-start.2 = (f16[560,128]{1,0:T(8,128)(2,1)S(1)}, f16[560,128]{1,0:T(8,128)(2,1)S(1)}, u32[]{:S(2)}, u32[]{:S(2)}) collective-permute-start(f16[560,128]{1,0:T(8,128)(2,1)S(1)} %convert_element_type.12), channel_id=1, source_target_pairs={{0,2},{2,4},{4,6},{6,0},{8,14},{10,8},{12,10},{14,12},{16,18},{18,... | collective-permute-start | bytes 430088 | tf_op jit(solution)/shard_map/ppermute | solution.py:799
  4.6 9.4 %collective-permute-start.3 = (f16[512,128]{1,0:T(8,128)(2,1)S(1)}, f16[512,128]{1,0:T(8,128)(2,1)S(1)}, u32[]{:S(2)}, u32[]{:S(2)}) collective-permute-start(f16[512,128]{1,0:T(8,128)(2,1)S(1)} %convert_element_type.14), channel_id=1, source_target_pairs={{0,14},{2,8},{4,10},{6,12},{8,2},{10,4},{12,6},{14,0},{16,30},{18,... | collective-permute-start | bytes 393224 | tf_op jit(solution)/shard_map/ppermute | solution.py:800
  7.7 6.4 %collective-permute-start.1 = (bf16[208,128]{1,0:T(8,128)(2,1)S(1)}, bf16[208,128]{1,0:T(8,128)(2,1)S(1)}, u32[]{:S(2)}, u32[]{:S(2)}) collective-permute-start(bf16[208,128]{1,0:T(8,128)(2,1)S(1)} %get-tuple-element.37), channel_id=1, source_target_pairs={{0,1},{1,0},{2,3},{3,2},{4,5},{5,4},{6,7},{7,6},{8,9},{9,8},{10,11... | collective-permute-start | bytes 159752 | tf_op jit(solution)/shard_map/ppermute | solution.py:812
  9.2 6.5 %collective-permute-start.4 = (bf16[80,128]{1,0:T(8,128)(2,1)S(1)}, bf16[80,128]{1,0:T(8,128)(2,1)S(1)}, u32[]{:S(2)}, u32[]{:S(2)}) collective-permute-start(bf16[80,128]{1,0:T(8,128)(2,1)S(1)} %get-tuple-element.43), channel_id=1, source_target_pairs={{0,3},{1,2},{2,5},{3,4},{4,7},{5,6},{6,1},{7,0},{8,15},{9,14},{10,... | collective-permute-start | bytes 61448 | tf_op jit(solution)/shard_map/ppermute | solution.py:813
  10.7 4.6 %collective-permute-start.5 = (f32[16,128]{1,0:T(8,128)S(1)}, f32[16,128]{1,0:T(8,128)S(1)}, u32[]{:S(2)}, u32[]{:S(2)}) collective-permute-start(f32[16,128]{1,0:T(8,128)S(1)} %get-tuple-element.44.obs_ref), channel_id=1, source_target_pairs={{0,8},{8,0},{16,24},{24,16},{1,9},{9,1},{17,25},{25,17},{2,10},{10... | collective-permute-start | bytes 24584 | tf_op jit(solution)/shard_map/ppermute | solution.py:795
  17.4 7.7 %collective-permute-start.6 = (bf16[304,128]{1,0:T(8,128)(2,1)S(1)}, bf16[304,128]{1,0:T(8,128)(2,1)S(1)}, u32[]{:S(2)}, u32[]{:S(2)}) collective-permute-start(bf16[304,128]{1,0:T(8,128)(2,1)S(1)} %get-tuple-element.46), channel_id=1, source_target_pairs={{0,1},{1,0},{8,9},{9,8},{16,17},{17,16},{24,25},{25,24},{2,3},{3,2... | collective-permute-start | bytes 233480 | tf_op jit(solution)/shard_map/ppermute | solution.py:838
  18.4 4.9 %collective-permute-start.7 = (bf16[256,128]{1,0:T(8,128)(2,1)S(1)}, bf16[256,128]{1,0:T(8,128)(2,1)S(1)}, u32[]{:S(2)}, u32[]{:S(2)}) collective-permute-start(bf16[256,128]{1,0:T(8,128)(2,1)S(1)} %get-tuple-element.47), channel_id=1, source_target_pairs={{0,16},{1,17},{8,24},{9,25},{16,0},{17,1},{24,8},{25,9},{2,18},{3,... | collective-permute-start | bytes 196616 | tf_op jit(solution)/shard_map/ppermute | solution.py:838
  19.9 5.2 %collective-permute-start.8 = (bf16[256,128]{1,0:T(8,128)(2,1)S(1)}, bf16[256,128]{1,0:T(8,128)(2,1)S(1)}, u32[]{:S(2)}, u32[]{:S(2)}) collective-permute-start(bf16[256,128]{1,0:T(8,128)(2,1)S(1)} %get-tuple-element.48), channel_id=1, source_target_pairs={{0,17},{1,16},{8,25},{9,24},{16,1},{17,0},{24,9},{25,8},{2,19},{3,... | collective-permute-start | bytes 196616 | tf_op jit(solution)/shard_map/ppermute | solution.py:838
  27.6 1.4 %collective-permute-start.9 = (bf16[4,2,64,128]{3,2,1,0:T(8,128)(2,1)S(1)}, bf16[4,2,64,128]{3,2,1,0:T(8,128)(2,1)S(1)}, u32[]{:S(2)}, u32[]{:S(2)}) collective-permute-start(bf16[4,2,64,128]{3,2,1,0:T(8,128)(2,1)S(1)} %get-tuple-element.49), channel_id=1, source_target_pairs={{0,8},{8,0},{16,24},{24,16},{1,9},{9,1},{17,25},{25,17},{2,10},{10... | collective-permute-start | bytes 393224 | tf_op jit(solution)/shard_map/ppermute | solution.py:853
  29.0 4.3 %collective-permute-start.10 = (bf16[2,2,64,128]{3,2,1,0:T(8,128)(2,1)S(1)}, bf16[2,2,64,128]{3,2,1,0:T(8,128)(2,1)S(1)}, u32[]{:S(2)}, u32[]{:S(2)}) collective-permute-start(bf16[2,2,64,128]{3,2,1,0:T(8,128)(2,1)S(1)} %get-tuple-element.58), channel_id=1, source_target_pairs={{0,1},{1,0},{8,9},{9,8},{16,17},{17,16},{24,25},{25,24},{2,3},{3,2... | collective-permute-start | bytes 196616 | tf_op jit(solution)/shard_map/ppermute | solution.py:838
  30.1 4.6 %collective-permute-start.11 = (bf16[2,2,64,128]{3,2,1,0:T(8,128)(2,1)S(1)}, bf16[2,2,64,128]{3,2,1,0:T(8,128)(2,1)S(1)}, u32[]{:S(2)}, u32[]{:S(2)}) collective-permute-start(bf16[2,2,64,128]{3,2,1,0:T(8,128)(2,1)S(1)} %get-tuple-element.59), channel_id=1, source_target_pairs={{0,16},{1,17},{8,24},{9,25},{16,0},{17,1},{24,8},{25,9},{2,18},{3,... | collective-permute-start | bytes 196616 | tf_op jit(solution)/shard_map/ppermute | solution.py:838
  30.7 5.2 %collective-permute-start.12 = (bf16[2,2,64,128]{3,2,1,0:T(8,128)(2,1)S(1)}, bf16[2,2,64,128]{3,2,1,0:T(8,128)(2,1)S(1)}, u32[]{:S(2)}, u32[]{:S(2)}) collective-permute-start(bf16[2,2,64,128]{3,2,1,0:T(8,128)(2,1)S(1)} %get-tuple-element.60), channel_id=1, source_target_pairs={{0,17},{1,16},{8,25},{9,24},{16,1},{17,0},{24,9},{25,8},{2,19},{3,... | collective-permute-start | bytes 196616 | tf_op jit(solution)/shard_map/ppermute | solution.py:838

commit v6 on v5

--- a/solution.py
+++ b/solution.py
@@ -443,7 +443,28 @@
     lax.fori_loop(0, EXTENT // (2 * OCTET), step, 0)
 
 
-def inner_kernel(s, _, __, side_ref, field_ref, winds_ref, first_ref, second_ref):
+def inner_kernel(s, field_ref, winds_ref, first_ref, second_ref):
+    refs = (field_ref, first_ref, second_ref, first_ref)
+    for stage in range(3):
+        wanted = (HALO + 1 + stage, DOMAIN - 1 - stage)
+        run_stage(s, field_ref, winds_ref, refs[stage], refs[stage + 1], stage, wanted)
+
+
+def run_ends_stage(s, field_ref, winds_ref, from_ref, to_ref, stage, wanted):
+    def step(i, carry):
+        for k in range(2):
+            start = LANES * i + OCTET * k
+
+            def emit(layer, j, value):
+                to_ref[pl.ds(s.field_at(layer, j) + start, OCTET), :] = value
+
+            evaluate(s, field_ref, winds_ref, from_ref, stage, start, wanted, emit)
+        return carry
+
+    lax.fori_loop(0, 2, step, 0)
+
+
+def ends_kernel(s, _, __, ___, ____, side_ref, field_ref, winds_ref, first_ref, second_ref, ends1_ref, ends2_ref):
     odd = lax.rem(lax.axis_index("mem"), 2)
     for layer in range(s.layers):
         edges = side_ref[pl.ds(layer * 2 * HALO * OCTET, 2 * HALO * OCTET), :].astype(jnp.float32)
@@ -459,10 +480,22 @@
         for row in range(s.rows):
             at = s.wind_at(block // s.layers, block % s.layers, domain_row(odd, row))
             set_wind_edges(winds_ref, beside, block * s.rows + row, pl.multiple_of(at, OCTET))
-    refs = (field_ref, first_ref, second_ref, first_ref)
+    refs = (field_ref, ends1_ref, ends2_ref, ends1_ref)
     for stage in range(3):
         wanted = (HALO + 1 + stage, DOMAIN - 1 - stage)
-        run_stage(s, field_ref, winds_ref, refs[stage], refs[stage + 1], stage, wanted)
+        run_ends_stage(s, field_ref, winds_ref, refs[stage], refs[stage + 1], stage, wanted)
+    near = lax.broadcasted_iota(jnp.int32, (OCTET, LANES), 0) < HALO
+    for to_ref, from_ref, wanted in (
+        (first_ref, ends1_ref, (HALO + 1, HALO + 5)),
+        (second_ref, ends2_ref, (HALO + 2, HALO + 4)),
+    ):
+        for layer in range(s.layers):
+            for j in range(*wanted):
+                at = s.field_at(layer, j)
+                for start, choose in ((0, None), (OCTET, near), (LANES, ~near), (LANES + OCTET, None)):
+                    part = pl.ds(at + start, OCTET)
+                    value = from_ref[part, :]
+                    to_ref[part, :] = value if choose is None else jnp.where(choose, value, to_ref[part, :])
 
 
 def forecast_kernel(
@@ -811,12 +844,13 @@
     winds = vmem_call(functools.partial(spread_winds_kernel, s), winds_shape, [], wind)
     side = lax.ppermute(side_out, "gy", across)
     corner = lax.ppermute(corner_out, ("mem", "gx", "gy"), diagonal)
+    first, second = vmem_call(functools.partial(inner_kernel, s), (field_shape, field_shape), [], field, winds)
     field, winds, first, second = vmem_call(
-        functools.partial(inner_kernel, s),
+        functools.partial(ends_kernel, s),
         (field_shape, winds_shape, field_shape, field_shape),
-        [],
-        field, winds, side,
-        aliases={0: 0, 1: 1},
+        [((layers * DOMAIN * EXTENT, LANES), f32)] * 2,
+        field, winds, first, second, side,
+        aliases={0: 0, 1: 1, 2: 2, 3: 3},
     )
     piece = shaped((s.piece_rows, s.members), bf16)
     piece_obs = shaped((s.piece_rows + 3 * s.obs_rows, s.members), bf16)

time: 36.9 us -> 37 us (level)
    pallas_call x7 -> x8, Pallas kernels: 6.9 us -> 7.12 us  [vmem_call(): pl.pallas_call(kernel, out_shape=outs, in_specs=[spec] * len(args), out_s...]
  transfers between devices with their start and end apart: 13 -> 13, of which waited for: 8 -> 8; matrix products, arithmetic and copies ran while one was open for 0% -> 0% of each run, Pallas kernels for 11% -> 12%
where the time goes in v6:
time: 37 us; the launch traced here: 36.9 us
  starting transfers between devices  15.7 us (42%)
  waiting for transfers between devices  11.6 us (31%)
  Pallas kernels  9.41 us (25%)
    ppermute x6, waiting for transfers between devices, exchange(): arrived.append(lax.ppermute(parts[d], ('mem', 'gy'), flip(d)))  7.61 us
    pallas_call x8, Pallas kernels, vmem_call(): pl.pallas_call(kernel, out_shape=outs, in_specs=[spec] * len(args), out_s...  7.12 us
    ppermute x6, starting transfers between devices, exchange(): arrived.append(lax.ppermute(parts[d], ('mem', 'gy'), flip(d)))  7.11 us
    ppermute x1, waiting for transfers between devices, on_device_tile(): lax.ppermute(other_out.astype(jnp.float16), ('mem', 'gx'), along_other)  2.78 us
    ppermute x1, starting transfers between devices, on_device_tile(): lax.ppermute(same_out.astype(jnp.float16), ('mem', 'gx'), along).astype(f32)  2.62 us
    ppermute x1, starting transfers between devices, on_device_tile(): lax.ppermute(other_out.astype(jnp.float16), ('mem', 'gx'), along_other)  2.37 us
    ppermute x1, starting transfers between devices, on_device_tile(): side = lax.ppermute(side_out, 'gy', across)  1.53 us
    ppermute x1, starting transfers between devices, on_device_tile(): corner = lax.ppermute(corner_out, ('mem', 'gx', 'gy'), diagonal)  1.52 us
  transfers between devices with their start and end apart: 13, of which 8 were waited for; matrix products, arithmetic and copies ran while one was open for 0% of the time, Pallas kernels for 12%

profile of v6, /device:TPU:0, one launch (start us, length us, event | category | flops | bytes accessed | tf_op | source)
XLA Modules:
  0.0 36.9 jit_solution(14524909882252112577)
XLA Ops:
  0.0 0.5 %collective-permute-start = (f32[64,2,8,128]{3,2,1,0:T(8,128)}, f32[64,2,8,128]{3,2,1,0:T(8,128)S(1)}, u32[]{:S(2)}, u32[]{:S(2)}) collective-permute-start(f32[64,2,8,128]{3,2,1,0:T(8,128)} %param.5), channel_id=1, source_target_pairs={{0,8},{8,0},{16,24},{24,16},{1,9},{9,1},{17,25},{25,17},{2,10},{10... | collective-permute-start | bytes 1572872 | tf_op jit(solution)/shard_map/ppermute | solution.py:794
  0.5 1.4 %shard_map.55 = (f32[1024,128]{1,0:T(8,128)S(1)}, f32[32,128]{1,0:T(8,128)S(1)}, f32[16,128]{1,0:T(8,128)S(1)}, f32[560,128]{1,0:T(8,128)S(1)}, f32[512,128]{1,0:T(8,128)S(1)}) custom-call(f32[1024,128]{1,0:T(8,128)} %bitcast.7, f32[32,128]{1,0:T(8,128)} %bitcast.8, s32[1,128]{1,0:T(1,128)} %bitcast.9, f32[1,128]{1,0:T(1,128)} %bitcast.10, f32[1,128]{1,0:T(1,128)} %bitcast.11), custom_call_target="tpu_custom_call" | custom-call | tf_op jit(solution)/shard_map/pallas_call | solution.py:797
  2.0 2.6 %collective-permute-start.2 = (f16[560,128]{1,0:T(8,128)(2,1)S(1)}, f16[560,128]{1,0:T(8,128)(2,1)S(1)}, u32[]{:S(2)}, u32[]{:S(2)}) collective-permute-start(f16[560,128]{1,0:T(8,128)(2,1)S(1)} %convert_element_type.12), channel_id=1, source_target_pairs={{0,2},{2,4},{4,6},{6,0},{8,14},{10,8},{12,10},{14,12},{16,18},{18,... | collective-permute-start | bytes 430088 | tf_op jit(solution)/shard_map/ppermute | solution.py:832
  4.6 2.4 %collective-permute-start.3 = (f16[512,128]{1,0:T(8,128)(2,1)S(1)}, f16[512,128]{1,0:T(8,128)(2,1)S(1)}, u32[]{:S(2)}, u32[]{:S(2)}) collective-permute-start(f16[512,128]{1,0:T(8,128)(2,1)S(1)} %convert_element_type.14), channel_id=1, source_target_pairs={{0,14},{2,8},{4,10},{6,12},{8,2},{10,4},{12,6},{14,0},{16,30},{18,... | collective-permute-start | bytes 393224 | tf_op jit(solution)/shard_map/ppermute | solution.py:833
  7.0 0.7 %shard_map.56 = (f32[3456,128]{1,0:T(8,128)S(1)}, bf16[208,128]{1,0:T(8,128)(2,1)S(1)}, bf16[80,128]{1,0:T(8,128)(2,1)S(1)}) custom-call(f32[1024,128]{1,0:T(8,128)S(1)} %get-tuple-element.35.own_ref, f32[1024,128]{1,0:T(8,128)S(1)} %bitcast.6, f32[32,128]{1,0:T(8,128)S(1)} %get-tuple-element.36.wind_ref, f32[560,128]{1,0:T(8,128)S(1)} %get-tuple-element.37.same_ref), custom_call_target="tpu_custom_call" | custom-call | tf_op jit(solution)/shard_map/pallas_call | solution.py:761
  7.7 1.5 %collective-permute-start.1 = (bf16[208,128]{1,0:T(8,128)(2,1)S(1)}, bf16[208,128]{1,0:T(8,128)(2,1)S(1)}, u32[]{:S(2)}, u32[]{:S(2)}) collective-permute-start(bf16[208,128]{1,0:T(8,128)(2,1)S(1)} %get-tuple-element.41), channel_id=1, source_target_pairs={{0,1},{1,0},{2,3},{3,2},{4,5},{5,4},{6,7},{7,6},{8,9},{9,8},{10,11... | collective-permute-start | bytes 159752 | tf_op jit(solution)/shard_map/ppermute | solution.py:845
  9.2 1.5 %collective-permute-start.4 = (bf16[80,128]{1,0:T(8,128)(2,1)S(1)}, bf16[80,128]{1,0:T(8,128)(2,1)S(1)}, u32[]{:S(2)}, u32[]{:S(2)}) collective-permute-start(bf16[80,128]{1,0:T(8,128)(2,1)S(1)} %get-tuple-element.47), channel_id=1, source_target_pairs={{0,3},{1,2},{2,5},{3,4},{4,7},{5,6},{6,1},{7,0},{8,15},{9,14},{10,... | collective-permute-start | bytes 61448 | tf_op jit(solution)/shard_map/ppermute | solution.py:846
  10.7 0.0 collective-permute-start.5
  10.7 0.5 %shard_map.57.winds_ref.__ = f32[6912,128]{1,0:T(8,128)S(1)} custom-call(f32[32,128]{1,0:T(8,128)S(1)} %get-tuple-element.36.wind_ref), custom_call_target="tpu_custom_call" | custom-call | tf_op jit(solution)/shard_map/pallas_call | solution.py:761
  11.2 2.8 %collective-permute-done.3 = f16[512,128]{1,0:T(8,128)(2,1)S(1)} collective-permute-done((f16[512,128]{1,0:T(8,128)(2,1)S(1)}, f16[512,128]{1,0:T(8,128)(2,1)S(1)}, u32[]{:S(2)}, u32[]{:S(2)}) %collective-permute-start.3) | collective-permute-done | bytes 131104 | tf_op jit(solution)/shard_map/ppermute | solution.py:833
  14.0 0.0 collective-permute-done.2
  14.0 1.0 %shard_map.58 = (f32[3456,128]{1,0:T(8,128)S(1)}, f32[3456,128]{1,0:T(8,128)S(1)}) custom-call(f32[3456,128]{1,0:T(8,128)S(1)} %get-tuple-element.38.field_ref._, f32[6912,128]{1,0:T(8,128)S(1)} %shard_map.57.winds_ref.__), custom_call_target="tpu_custom_call" | custom-call | tf_op jit(solution)/shard_map/pallas_call | solution.py:761
  15.1 0.4 %shard_map.59 = (f32[3456,128]{1,0:T(8,128)S(1)}, f32[6912,128]{1,0:T(8,128)S(1)}, f32[3456,128]{1,0:T(8,128)S(1)}, f32[3456,128]{1,0:T(8,128)S(1)}) custom-call(f32[3456,128]{1,0:T(8,128)S(1)} %get-tuple-element.38.field_ref._, f32[6912,128]{1,0:T(8,128)S(1)} %shard_map.57.winds_ref.__, ...), custom_call_target="tpu_custom_call", output_to_operand_aliasing={{0}: (0, {}), {1}: (1, {}), {2}: (2, {}), {3}: (3, {})} | custom-call | tf_op jit(solution)/shard_map/pallas_call | solution.py:761
  15.6 0.0 collective-permute-done.5.obs_ref
  15.6 0.1 collective-permute-done.4.corner_ref
  15.7 1.7 %shard_map.60 = (bf16[256,128]{1,0:T(8,128)(2,1)S(1)}, bf16[304,128]{1,0:T(8,128)(2,1)S(1)}, bf16[256,128]{1,0:T(8,128)(2,1)S(1)}, bf16[256,128]{1,0:T(8,128)(2,...) custom-call(f32[3456,128]{1,0:T(8,128)S(1)} %get-tuple-element.42._,, ...), custom_call_target="tpu_custom_call", output_to_operand_aliasing={{4}: (0, {}), {5}: (1, {}), {6}: (2, {}), {7}: (3, {})} | custom-call | tf_op jit(solution)/shard_map/pallas_call | solution.py:761
  17.4 1.3 %collective-permute-start.6 = (bf16[304,128]{1,0:T(8,128)(2,1)S(1)}, bf16[304,128]{1,0:T(8,128)(2,1)S(1)}, u32[]{:S(2)}, u32[]{:S(2)}) collective-permute-start(bf16[304,128]{1,0:T(8,128)(2,1)S(1)} %get-tuple-element.50), channel_id=1, source_target_pairs={{0,1},{1,0},{8,9},{9,8},{16,17},{17,16},{24,25},{25,24},{2,3},{3,2... | collective-permute-start | bytes 233480 | tf_op jit(solution)/shard_map/ppermute | solution.py:872
  18.6 1.5 %collective-permute-start.7 = (bf16[256,128]{1,0:T(8,128)(2,1)S(1)}, bf16[256,128]{1,0:T(8,128)(2,1)S(1)}, u32[]{:S(2)}, u32[]{:S(2)}) collective-permute-start(bf16[256,128]{1,0:T(8,128)(2,1)S(1)} %get-tuple-element.51), channel_id=1, source_target_pairs={{0,16},{1,17},{8,24},{9,25},{16,0},{17,1},{24,8},{25,9},{2,18},{3,... | collective-permute-start | bytes 196616 | tf_op jit(solution)/shard_map/ppermute | solution.py:872
  20.1 0.8 %collective-permute-start.8 = (bf16[256,128]{1,0:T(8,128)(2,1)S(1)}, bf16[256,128]{1,0:T(8,128)(2,1)S(1)}, u32[]{:S(2)}, u32[]{:S(2)}) collective-permute-start(bf16[256,128]{1,0:T(8,128)(2,1)S(1)} %get-tuple-element.52), channel_id=1, source_target_pairs={{0,17},{1,16},{8,25},{9,24},{16,1},{17,0},{24,9},{25,8},{2,19},{3,... | collective-permute-start | bytes 196616 | tf_op jit(solution)/shard_map/ppermute | solution.py:872
  20.9 2.6 %collective-permute-done.7.piece2_ref = bf16[256,128]{1,0:T(8,128)(2,1)S(1)} collective-permute-done((bf16[256,128]{1,0:T(8,128)(2,1)S(1)}, bf16[256,128]{1,0:T(8,128)(2,1)S(1)}, u32[]{:S(2)}, u32[]{:S(2)}) %collective-permute-start.7) | collective-permute-done | bytes 65568 | tf_op jit(solution)/shard_map/ppermute | solution.py:872
  23.6 1.7 %collective-permute-done.8.piece3_ref = bf16[256,128]{1,0:T(8,128)(2,1)S(1)} collective-permute-done((bf16[256,128]{1,0:T(8,128)(2,1)S(1)}, bf16[256,128]{1,0:T(8,128)(2,1)S(1)}, u32[]{:S(2)}, u32[]{:S(2)}) %collective-permute-start.8) | collective-permute-done | bytes 65568 | tf_op jit(solution)/shard_map/ppermute | solution.py:872
  25.3 2.5 %shard_map.61 = (bf16[4,2,64,128]{3,2,1,0:T(8,128)(2,1)S(1)}, bf16[512,256]{1,0:T(8,128)(2,1)S(1)}, bf16[256,256]{1,0:T(8,128)(2,1)S(1)}, f32[8,512]{1,0:T(8,128)S(1)}) custom-call(bf16[256,128]{1,0:T(8,128)(2,1)S(1)} %get-tuple-element.49.piece0_ref, bf16[304,128]{1,0:T(8,128)(2,1)S(1)} %collective-permute-done.6.piece1_ref, ...), custom_call_target="tpu_custom_call" | custom-call | tf_op jit(solution)/shard_map/pallas_call | solution.py:761
  27.8 0.1 collective-permute-start.9
  27.9 0.3 shard_map.62
  28.2 1.1 %collective-permute-done.9.received_ref = bf16[4,2,64,128]{3,2,1,0:T(8,128)(2,1)S(1)} collective-permute-done((bf16[4,2,64,128]{3,2,1,0:T(8,128)(2,1)S(1)}, bf16[4,2,64,128]{3,2,1,0:T(8,128)(2,1)S(1)}, u32[]{:S(2)}, u32[]{:S(2)}) %collective-permute-start.9) | collective-permute-done | bytes 131104 | tf_op jit(solution)/shard_map/ppermute | solution.py:887
  29.2 0.9 %collective-permute-start.10 = (bf16[2,2,64,128]{3,2,1,0:T(8,128)(2,1)S(1)}, bf16[2,2,64,128]{3,2,1,0:T(8,128)(2,1)S(1)}, u32[]{:S(2)}, u32[]{:S(2)}) collective-permute-start(bf16[2,2,64,128]{3,2,1,0:T(8,128)(2,1)S(1)} %get-tuple-element.62), channel_id=1, source_target_pairs={{0,1},{1,0},{8,9},{9,8},{16,17},{17,16},{24,25},{25,24},{2,3},{3,2... | collective-permute-start | bytes 196616 | tf_op jit(solution)/shard_map/ppermute | solution.py:872
  30.1 0.7 %collective-permute-start.11 = (bf16[2,2,64,128]{3,2,1,0:T(8,128)(2,1)S(1)}, bf16[2,2,64,128]{3,2,1,0:T(8,128)(2,1)S(1)}, u32[]{:S(2)}, u32[]{:S(2)}) collective-permute-start(bf16[2,2,64,128]{3,2,1,0:T(8,128)(2,1)S(1)} %get-tuple-element.63), channel_id=1, source_target_pairs={{0,16},{1,17},{8,24},{9,25},{16,0},{17,1},{24,8},{25,9},{2,18},{3,... | collective-permute-start | bytes 196616 | tf_op jit(solution)/shard_map/ppermute | solution.py:872
  30.8 1.9 %collective-permute-start.12 = (bf16[2,2,64,128]{3,2,1,0:T(8,128)(2,1)S(1)}, bf16[2,2,64,128]{3,2,1,0:T(8,128)(2,1)S(1)}, u32[]{:S(2)}, u32[]{:S(2)}) collective-permute-start(bf16[2,2,64,128]{3,2,1,0:T(8,128)(2,1)S(1)} %get-tuple-element.64), channel_id=1, source_target_pairs={{0,17},{1,16},{8,25},{9,24},{16,1},{17,0},{24,9},{25,8},{2,19},{3,... | collective-permute-start | bytes 196616 | tf_op jit(solution)/shard_map/ppermute | solution.py:872
  32.8 0.8 %collective-permute-done.10.refs_1_ = bf16[2,2,64,128]{3,2,1,0:T(8,128)(2,1)S(1)} collective-permute-done((bf16[2,2,64,128]{3,2,1,0:T(8,128)(2,1)S(1)}, bf16[2,2,64,128]{3,2,1,0:T(8,128)(2,1)S(1)}, u32[]{:S(2)}, u32[]{:S(2)}) %collective-permute-start.10) | collective-permute-done | bytes 65568 | tf_op jit(solution)/shard_map/ppermute | solution.py:872
  33.6 1.3 %collective-permute-done.11.refs_2_ = bf16[2,2,64,128]{3,2,1,0:T(8,128)(2,1)S(1)} collective-permute-done((bf16[2,2,64,128]{3,2,1,0:T(8,128)(2,1)S(1)}, bf16[2,2,64,128]{3,2,1,0:T(8,128)(2,1)S(1)}, u32[]{:S(2)}, u32[]{:S(2)}) %collective-permute-start.11) | collective-permute-done | bytes 65568 | tf_op jit(solution)/shard_map/ppermute | solution.py:872
  34.9 1.1 %collective-permute-done.12.refs_3_ = bf16[2,2,64,128]{3,2,1,0:T(8,128)(2,1)S(1)} collective-permute-done((bf16[2,2,64,128]{3,2,1,0:T(8,128)(2,1)S(1)}, bf16[2,2,64,128]{3,2,1,0:T(8,128)(2,1)S(1)}, u32[]{:S(2)}, u32[]{:S(2)}) %collective-permute-start.12) | collective-permute-done | bytes 65568 | tf_op jit(solution)/shard_map/ppermute | solution.py:872
  36.0 0.9 %shard_map.64 = bf16[64,2,8,128]{3,2,1,0:T(8,128)(2,1)} custom-call(bf16[2,2,64,128]{3,2,1,0:T(8,128)(2,1)S(1)} %get-tuple-element.61.refs_0_, bf16[2,2,64,128]{3,2,1,0:T(8,128)(2,1)S(1)} %collective-permute-done.10.refs_1_, bf16[2,2,64,128]{3,2,1,0:T(8,128)(2,1)S(1)} %collective-permute-done.11.refs_2_, ...), custom_call_target="tpu_custom_call" | custom-call | tf_op jit(solution)/shard_map/pallas_call | solution.py:895
  (8 shorter events, 0.1 us)
Async XLA Ops:
  0.0 7.0 %collective-permute-start = (f32[64,2,8,128]{3,2,1,0:T(8,128)}, f32[64,2,8,128]{3,2,1,0:T(8,128)S(1)}, u32[]{:S(2)}, u32[]{:S(2)}) collective-permute-start(f32[64,2,8,128]{3,2,1,0:T(8,128)} %param.5), channel_id=1, source_target_pairs={{0,8},{8,0},{16,24},{24,16},{1,9},{9,1},{17,25},{25,17},{2,10},{10... | collective-permute-start | bytes 1572872 | tf_op jit(solution)/shard_map/ppermute | solution.py:794
  2.0 12.0 %collective-permute-start.2 = (f16[560,128]{1,0:T(8,128)(2,1)S(1)}, f16[560,128]{1,0:T(8,128)(2,1)S(1)}, u32[]{:S(2)}, u32[]{:S(2)}) collective-permute-start(f16[560,128]{1,0:T(8,128)(2,1)S(1)} %convert_element_type.12), channel_id=1, source_target_pairs={{0,2},{2,4},{4,6},{6,0},{8,14},{10,8},{12,10},{14,12},{16,18},{18,... | collective-permute-start | bytes 430088 | tf_op jit(solution)/shard_map/ppermute | solution.py:832
  4.6 9.4 %collective-permute-start.3 = (f16[512,128]{1,0:T(8,128)(2,1)S(1)}, f16[512,128]{1,0:T(8,128)(2,1)S(1)}, u32[]{:S(2)}, u32[]{:S(2)}) collective-permute-start(f16[512,128]{1,0:T(8,128)(2,1)S(1)} %convert_element_type.14), channel_id=1, source_target_pairs={{0,14},{2,8},{4,10},{6,12},{8,2},{10,4},{12,6},{14,0},{16,30},{18,... | collective-permute-start | bytes 393224 | tf_op jit(solution)/shard_map/ppermute | solution.py:833
  7.7 7.4 %collective-permute-start.1 = (bf16[208,128]{1,0:T(8,128)(2,1)S(1)}, bf16[208,128]{1,0:T(8,128)(2,1)S(1)}, u32[]{:S(2)}, u32[]{:S(2)}) collective-permute-start(bf16[208,128]{1,0:T(8,128)(2,1)S(1)} %get-tuple-element.41), channel_id=1, source_target_pairs={{0,1},{1,0},{2,3},{3,2},{4,5},{5,4},{6,7},{7,6},{8,9},{9,8},{10,11... | collective-permute-start | bytes 159752 | tf_op jit(solution)/shard_map/ppermute | solution.py:845
  9.2 6.5 %collective-permute-start.4 = (bf16[80,128]{1,0:T(8,128)(2,1)S(1)}, bf16[80,128]{1,0:T(8,128)(2,1)S(1)}, u32[]{:S(2)}, u32[]{:S(2)}) collective-permute-start(bf16[80,128]{1,0:T(8,128)(2,1)S(1)} %get-tuple-element.47), channel_id=1, source_target_pairs={{0,3},{1,2},{2,5},{3,4},{4,7},{5,6},{6,1},{7,0},{8,15},{9,14},{10,... | collective-permute-start | bytes 61448 | tf_op jit(solution)/shard_map/ppermute | solution.py:846
  10.7 4.8 %collective-permute-start.5 = (f32[16,128]{1,0:T(8,128)S(1)}, f32[16,128]{1,0:T(8,128)S(1)}, u32[]{:S(2)}, u32[]{:S(2)}) collective-permute-start(f32[16,128]{1,0:T(8,128)S(1)} %get-tuple-element.48.obs_ref), channel_id=1, source_target_pairs={{0,8},{8,0},{16,24},{24,16},{1,9},{9,1},{17,25},{25,17},{2,10},{10... | collective-permute-start | bytes 24584 | tf_op jit(solution)/shard_map/ppermute | solution.py:828
  17.4 7.9 %collective-permute-start.6 = (bf16[304,128]{1,0:T(8,128)(2,1)S(1)}, bf16[304,128]{1,0:T(8,128)(2,1)S(1)}, u32[]{:S(2)}, u32[]{:S(2)}) collective-permute-start(bf16[304,128]{1,0:T(8,128)(2,1)S(1)} %get-tuple-element.50), channel_id=1, source_target_pairs={{0,1},{1,0},{8,9},{9,8},{16,17},{17,16},{24,25},{25,24},{2,3},{3,2... | collective-permute-start | bytes 233480 | tf_op jit(solution)/shard_map/ppermute | solution.py:872
  18.6 4.9 %collective-permute-start.7 = (bf16[256,128]{1,0:T(8,128)(2,1)S(1)}, bf16[256,128]{1,0:T(8,128)(2,1)S(1)}, u32[]{:S(2)}, u32[]{:S(2)}) collective-permute-start(bf16[256,128]{1,0:T(8,128)(2,1)S(1)} %get-tuple-element.51), channel_id=1, source_target_pairs={{0,16},{1,17},{8,24},{9,25},{16,0},{17,1},{24,8},{25,9},{2,18},{3,... | collective-permute-start | bytes 196616 | tf_op jit(solution)/shard_map/ppermute | solution.py:872
  20.1 5.2 %collective-permute-start.8 = (bf16[256,128]{1,0:T(8,128)(2,1)S(1)}, bf16[256,128]{1,0:T(8,128)(2,1)S(1)}, u32[]{:S(2)}, u32[]{:S(2)}) collective-permute-start(bf16[256,128]{1,0:T(8,128)(2,1)S(1)} %get-tuple-element.52), channel_id=1, source_target_pairs={{0,17},{1,16},{8,25},{9,24},{16,1},{17,0},{24,9},{25,8},{2,19},{3,... | collective-permute-start | bytes 196616 | tf_op jit(solution)/shard_map/ppermute | solution.py:872
  27.8 1.4 %collective-permute-start.9 = (bf16[4,2,64,128]{3,2,1,0:T(8,128)(2,1)S(1)}, bf16[4,2,64,128]{3,2,1,0:T(8,128)(2,1)S(1)}, u32[]{:S(2)}, u32[]{:S(2)}) collective-permute-start(bf16[4,2,64,128]{3,2,1,0:T(8,128)(2,1)S(1)} %get-tuple-element.53), channel_id=1, source_target_pairs={{0,8},{8,0},{16,24},{24,16},{1,9},{9,1},{17,25},{25,17},{2,10},{10... | collective-permute-start | bytes 393224 | tf_op jit(solution)/shard_map/ppermute | solution.py:887
  29.2 4.3 %collective-permute-start.10 = (bf16[2,2,64,128]{3,2,1,0:T(8,128)(2,1)S(1)}, bf16[2,2,64,128]{3,2,1,0:T(8,128)(2,1)S(1)}, u32[]{:S(2)}, u32[]{:S(2)}) collective-permute-start(bf16[2,2,64,128]{3,2,1,0:T(8,128)(2,1)S(1)} %get-tuple-element.62), channel_id=1, source_target_pairs={{0,1},{1,0},{8,9},{9,8},{16,17},{17,16},{24,25},{25,24},{2,3},{3,2... | collective-permute-start | bytes 196616 | tf_op jit(solution)/shard_map/ppermute | solution.py:872
  30.1 4.8 %collective-permute-start.11 = (bf16[2,2,64,128]{3,2,1,0:T(8,128)(2,1)S(1)}, bf16[2,2,64,128]{3,2,1,0:T(8,128)(2,1)S(1)}, u32[]{:S(2)}, u32[]{:S(2)}) collective-permute-start(bf16[2,2,64,128]{3,2,1,0:T(8,128)(2,1)S(1)} %get-tuple-element.63), channel_id=1, source_target_pairs={{0,16},{1,17},{8,24},{9,25},{16,0},{17,1},{24,8},{25,9},{2,18},{3,... | collective-permute-start | bytes 196616 | tf_op jit(solution)/shard_map/ppermute | solution.py:872
  30.8 5.2 %collective-permute-start.12 = (bf16[2,2,64,128]{3,2,1,0:T(8,128)(2,1)S(1)}, bf16[2,2,64,128]{3,2,1,0:T(8,128)(2,1)S(1)}, u32[]{:S(2)}, u32[]{:S(2)}) collective-permute-start(bf16[2,2,64,128]{3,2,1,0:T(8,128)(2,1)S(1)} %get-tuple-element.64), channel_id=1, source_target_pairs={{0,17},{1,16},{8,25},{9,24},{16,1},{17,0},{24,9},{25,8},{2,19},{3,... | collective-permute-start | bytes 196616 | tf_op jit(solution)/shard_map/ppermute | solution.py:872

commit v7 on v6

--- a/solution.py
+++ b/solution.py
@@ -213,6 +213,7 @@
 OCTET = 8
 GROUP = 32
 DOMAIN = 3 * HALO
+TOGETHER = 6
 EXTENT = LANES + 2 * OCTET
 VMEM_GRANT = 24 << 20
 LARGEST = 6.0
@@ -431,8 +432,8 @@
 
 def run_stage(s, field_ref, winds_ref, from_ref, to_ref, stage, wanted):
     def step(i, carry):
-        for k in range(2):
-            start = 2 * OCTET * i + OCTET * k
+        for k in range(TOGETHER):
+            start = TOGETHER * OCTET * i + OCTET * k
 
             def emit(layer, j, value):
                 to_ref[pl.ds(s.field_at(layer, j) + start, OCTET), :] = value
@@ -440,7 +441,7 @@
             evaluate(s, field_ref, winds_ref, from_ref, stage, start, wanted, emit)
         return carry
 
-    lax.fori_loop(0, EXTENT // (2 * OCTET), step, 0)
+    lax.fori_loop(0, EXTENT // (TOGETHER * OCTET), step, 0)
 
 
 def inner_kernel(s, field_ref, winds_ref, first_ref, second_ref):

time: 37 us -> 36.7 us (level)
  transfers between devices with their start and end apart: 13 -> 13, of which waited for: 8 -> 8; matrix products, arithmetic and copies ran while one was open for 0% -> 0% of each run, Pallas kernels for 12% -> 11%
where the time goes in v7:
time: 36.7 us; the launch traced here: 36.6 us
  starting transfers between devices  15.7 us (43%)
  waiting for transfers between devices  11.6 us (32%)
  Pallas kernels  9.08 us (25%)
    ppermute x6, waiting for transfers between devices, exchange(): arrived.append(lax.ppermute(parts[d], ('mem', 'gy'), flip(d)))  7.45 us
    ppermute x6, starting transfers between devices, exchange(): arrived.append(lax.ppermute(parts[d], ('mem', 'gy'), flip(d)))  7.11 us
    pallas_call x8, Pallas kernels, vmem_call(): pl.pallas_call(kernel, out_shape=outs, in_specs=[spec] * len(args), out_s...  6.79 us
    ppermute x1, waiting for transfers between devices, on_device_tile(): lax.ppermute(other_out.astype(jnp.float16), ('mem', 'gx'), along_other)  2.78 us
    ppermute x1, starting transfers between devices, on_device_tile(): lax.ppermute(same_out.astype(jnp.float16), ('mem', 'gx'), along).astype(f32)  2.62 us
    ppermute x1, starting transfers between devices, on_device_tile(): lax.ppermute(other_out.astype(jnp.float16), ('mem', 'gx'), along_other)  2.37 us
    ppermute x1, starting transfers between devices, on_device_tile(): side = lax.ppermute(side_out, 'gy', across)  1.53 us
    ppermute x1, starting transfers between devices, on_device_tile(): corner = lax.ppermute(corner_out, ('mem', 'gx', 'gy'), diagonal)  1.52 us
  transfers between devices with their start and end apart: 13, of which 8 were waited for; matrix products, arithmetic and copies ran while one was open for 0% of the time, Pallas kernels for 11%

profile of v7, /device:TPU:0, one launch (start us, length us, event | category | flops | bytes accessed | tf_op | source)
XLA Modules:
  0.0 36.6 jit_solution(11849268515493491001)
XLA Ops:
  0.0 0.5 %collective-permute-start = (f32[64,2,8,128]{3,2,1,0:T(8,128)}, f32[64,2,8,128]{3,2,1,0:T(8,128)S(1)}, u32[]{:S(2)}, u32[]{:S(2)}) collective-permute-start(f32[64,2,8,128]{3,2,1,0:T(8,128)} %param.5), channel_id=1, source_target_pairs={{0,8},{8,0},{16,24},{24,16},{1,9},{9,1},{17,25},{25,17},{2,10},{10... | collective-permute-start | bytes 1572872 | tf_op jit(solution)/shard_map/ppermute | solution.py:795
  0.5 1.4 %shard_map.55 = (f32[1024,128]{1,0:T(8,128)S(1)}, f32[32,128]{1,0:T(8,128)S(1)}, f32[16,128]{1,0:T(8,128)S(1)}, f32[560,128]{1,0:T(8,128)S(1)}, f32[512,128]{1,0:T(8,128)S(1)}) custom-call(f32[1024,128]{1,0:T(8,128)} %bitcast.7, f32[32,128]{1,0:T(8,128)} %bitcast.8, s32[1,128]{1,0:T(1,128)} %bitcast.9, f32[1,128]{1,0:T(1,128)} %bitcast.10, f32[1,128]{1,0:T(1,128)} %bitcast.11), custom_call_target="tpu_custom_call" | custom-call | tf_op jit(solution)/shard_map/pallas_call | solution.py:798
  2.0 2.6 %collective-permute-start.2 = (f16[560,128]{1,0:T(8,128)(2,1)S(1)}, f16[560,128]{1,0:T(8,128)(2,1)S(1)}, u32[]{:S(2)}, u32[]{:S(2)}) collective-permute-start(f16[560,128]{1,0:T(8,128)(2,1)S(1)} %convert_element_type.12), channel_id=1, source_target_pairs={{0,2},{2,4},{4,6},{6,0},{8,14},{10,8},{12,10},{14,12},{16,18},{18,... | collective-permute-start | bytes 430088 | tf_op jit(solution)/shard_map/ppermute | solution.py:833
  4.6 2.4 %collective-permute-start.3 = (f16[512,128]{1,0:T(8,128)(2,1)S(1)}, f16[512,128]{1,0:T(8,128)(2,1)S(1)}, u32[]{:S(2)}, u32[]{:S(2)}) collective-permute-start(f16[512,128]{1,0:T(8,128)(2,1)S(1)} %convert_element_type.14), channel_id=1, source_target_pairs={{0,14},{2,8},{4,10},{6,12},{8,2},{10,4},{12,6},{14,0},{16,30},{18,... | collective-permute-start | bytes 393224 | tf_op jit(solution)/shard_map/ppermute | solution.py:834
  7.0 0.7 %shard_map.56 = (f32[3456,128]{1,0:T(8,128)S(1)}, bf16[208,128]{1,0:T(8,128)(2,1)S(1)}, bf16[80,128]{1,0:T(8,128)(2,1)S(1)}) custom-call(f32[1024,128]{1,0:T(8,128)S(1)} %get-tuple-element.35.own_ref, f32[1024,128]{1,0:T(8,128)S(1)} %bitcast.6, f32[32,128]{1,0:T(8,128)S(1)} %get-tuple-element.36.wind_ref, f32[560,128]{1,0:T(8,128)S(1)} %get-tuple-element.37.same_ref), custom_call_target="tpu_custom_call" | custom-call | tf_op jit(solution)/shard_map/pallas_call | solution.py:762
  7.7 1.5 %collective-permute-start.1 = (bf16[208,128]{1,0:T(8,128)(2,1)S(1)}, bf16[208,128]{1,0:T(8,128)(2,1)S(1)}, u32[]{:S(2)}, u32[]{:S(2)}) collective-permute-start(bf16[208,128]{1,0:T(8,128)(2,1)S(1)} %get-tuple-element.41), channel_id=1, source_target_pairs={{0,1},{1,0},{2,3},{3,2},{4,5},{5,4},{6,7},{7,6},{8,9},{9,8},{10,11... | collective-permute-start | bytes 159752 | tf_op jit(solution)/shard_map/ppermute | solution.py:846
  9.2 1.5 %collective-permute-start.4 = (bf16[80,128]{1,0:T(8,128)(2,1)S(1)}, bf16[80,128]{1,0:T(8,128)(2,1)S(1)}, u32[]{:S(2)}, u32[]{:S(2)}) collective-permute-start(bf16[80,128]{1,0:T(8,128)(2,1)S(1)} %get-tuple-element.47), channel_id=1, source_target_pairs={{0,3},{1,2},{2,5},{3,4},{4,7},{5,6},{6,1},{7,0},{8,15},{9,14},{10,... | collective-permute-start | bytes 61448 | tf_op jit(solution)/shard_map/ppermute | solution.py:847
  10.7 0.0 collective-permute-start.5
  10.7 0.5 %shard_map.57.winds_ref.__ = f32[6912,128]{1,0:T(8,128)S(1)} custom-call(f32[32,128]{1,0:T(8,128)S(1)} %get-tuple-element.36.wind_ref), custom_call_target="tpu_custom_call" | custom-call | tf_op jit(solution)/shard_map/pallas_call | solution.py:762
  11.2 2.8 %collective-permute-done.3 = f16[512,128]{1,0:T(8,128)(2,1)S(1)} collective-permute-done((f16[512,128]{1,0:T(8,128)(2,1)S(1)}, f16[512,128]{1,0:T(8,128)(2,1)S(1)}, u32[]{:S(2)}, u32[]{:S(2)}) %collective-permute-start.3) | collective-permute-done | bytes 131104 | tf_op jit(solution)/shard_map/ppermute | solution.py:834
  14.0 0.0 collective-permute-done.2
  14.0 0.9 %shard_map.58 = (f32[3456,128]{1,0:T(8,128)S(1)}, f32[3456,128]{1,0:T(8,128)S(1)}) custom-call(f32[3456,128]{1,0:T(8,128)S(1)} %get-tuple-element.38.field_ref._, f32[6912,128]{1,0:T(8,128)S(1)} %shard_map.57.winds_ref.__), custom_call_target="tpu_custom_call" | custom-call | tf_op jit(solution)/shard_map/pallas_call | solution.py:762
  14.9 0.0 collective-permute-done.1.side_ref
  14.9 0.4 %shard_map.59 = (f32[3456,128]{1,0:T(8,128)S(1)}, f32[6912,128]{1,0:T(8,128)S(1)}, f32[3456,128]{1,0:T(8,128)S(1)}, f32[3456,128]{1,0:T(8,128)S(1)}) custom-call(f32[3456,128]{1,0:T(8,128)S(1)} %get-tuple-element.38.field_ref._, f32[6912,128]{1,0:T(8,128)S(1)} %shard_map.57.winds_ref.__, ...), custom_call_target="tpu_custom_call", output_to_operand_aliasing={{0}: (0, {}), {1}: (1, {}), {2}: (2, {}), {3}: (3, {})} | custom-call | tf_op jit(solution)/shard_map/pallas_call | solution.py:762
  15.4 0.3 collective-permute-done.4.corner_ref
  15.7 1.5 %shard_map.60 = (bf16[256,128]{1,0:T(8,128)(2,1)S(1)}, bf16[304,128]{1,0:T(8,128)(2,1)S(1)}, bf16[256,128]{1,0:T(8,128)(2,1)S(1)}, bf16[256,128]{1,0:T(8,128)(2,...) custom-call(f32[3456,128]{1,0:T(8,128)S(1)} %get-tuple-element.42._,, ...), custom_call_target="tpu_custom_call", output_to_operand_aliasing={{4}: (0, {}), {5}: (1, {}), {6}: (2, {}), {7}: (3, {})} | custom-call | tf_op jit(solution)/shard_map/pallas_call | solution.py:762
  17.2 1.1 %collective-permute-start.6 = (bf16[304,128]{1,0:T(8,128)(2,1)S(1)}, bf16[304,128]{1,0:T(8,128)(2,1)S(1)}, u32[]{:S(2)}, u32[]{:S(2)}) collective-permute-start(bf16[304,128]{1,0:T(8,128)(2,1)S(1)} %get-tuple-element.50), channel_id=1, source_target_pairs={{0,1},{1,0},{8,9},{9,8},{16,17},{17,16},{24,25},{25,24},{2,3},{3,2... | collective-permute-start | bytes 233480 | tf_op jit(solution)/shard_map/ppermute | solution.py:873
  18.3 1.5 %collective-permute-start.7 = (bf16[256,128]{1,0:T(8,128)(2,1)S(1)}, bf16[256,128]{1,0:T(8,128)(2,1)S(1)}, u32[]{:S(2)}, u32[]{:S(2)}) collective-permute-start(bf16[256,128]{1,0:T(8,128)(2,1)S(1)} %get-tuple-element.51), channel_id=1, source_target_pairs={{0,16},{1,17},{8,24},{9,25},{16,0},{17,1},{24,8},{25,9},{2,18},{3,... | collective-permute-start | bytes 196616 | tf_op jit(solution)/shard_map/ppermute | solution.py:873
  19.8 1.0 %collective-permute-start.8 = (bf16[256,128]{1,0:T(8,128)(2,1)S(1)}, bf16[256,128]{1,0:T(8,128)(2,1)S(1)}, u32[]{:S(2)}, u32[]{:S(2)}) collective-permute-start(bf16[256,128]{1,0:T(8,128)(2,1)S(1)} %get-tuple-element.52), channel_id=1, source_target_pairs={{0,17},{1,16},{8,25},{9,24},{16,1},{17,0},{24,9},{25,8},{2,19},{3,... | collective-permute-start | bytes 196616 | tf_op jit(solution)/shard_map/ppermute | solution.py:873
  20.8 2.5 %collective-permute-done.7.piece2_ref = bf16[256,128]{1,0:T(8,128)(2,1)S(1)} collective-permute-done((bf16[256,128]{1,0:T(8,128)(2,1)S(1)}, bf16[256,128]{1,0:T(8,128)(2,1)S(1)}, u32[]{:S(2)}, u32[]{:S(2)}) %collective-permute-start.7) | collective-permute-done | bytes 65568 | tf_op jit(solution)/shard_map/ppermute | solution.py:873
  23.3 1.7 %collective-permute-done.8.piece3_ref = bf16[256,128]{1,0:T(8,128)(2,1)S(1)} collective-permute-done((bf16[256,128]{1,0:T(8,128)(2,1)S(1)}, bf16[256,128]{1,0:T(8,128)(2,1)S(1)}, u32[]{:S(2)}, u32[]{:S(2)}) %collective-permute-start.8) | collective-permute-done | bytes 65568 | tf_op jit(solution)/shard_map/ppermute | solution.py:873
  25.0 2.5 %shard_map.61 = (bf16[4,2,64,128]{3,2,1,0:T(8,128)(2,1)S(1)}, bf16[512,256]{1,0:T(8,128)(2,1)S(1)}, bf16[256,256]{1,0:T(8,128)(2,1)S(1)}, f32[8,512]{1,0:T(8,128)S(1)}) custom-call(bf16[256,128]{1,0:T(8,128)(2,1)S(1)} %get-tuple-element.49.piece0_ref, bf16[304,128]{1,0:T(8,128)(2,1)S(1)} %collective-permute-done.6.piece1_ref, ...), custom_call_target="tpu_custom_call" | custom-call | tf_op jit(solution)/shard_map/pallas_call | solution.py:762
  27.5 0.1 collective-permute-start.9
  27.5 0.3 shard_map.62
  27.8 1.1 %collective-permute-done.9.received_ref = bf16[4,2,64,128]{3,2,1,0:T(8,128)(2,1)S(1)} collective-permute-done((bf16[4,2,64,128]{3,2,1,0:T(8,128)(2,1)S(1)}, bf16[4,2,64,128]{3,2,1,0:T(8,128)(2,1)S(1)}, u32[]{:S(2)}, u32[]{:S(2)}) %collective-permute-start.9) | collective-permute-done | bytes 131104 | tf_op jit(solution)/shard_map/ppermute | solution.py:888
  28.9 1.1 %collective-permute-start.10 = (bf16[2,2,64,128]{3,2,1,0:T(8,128)(2,1)S(1)}, bf16[2,2,64,128]{3,2,1,0:T(8,128)(2,1)S(1)}, u32[]{:S(2)}, u32[]{:S(2)}) collective-permute-start(bf16[2,2,64,128]{3,2,1,0:T(8,128)(2,1)S(1)} %get-tuple-element.62), channel_id=1, source_target_pairs={{0,1},{1,0},{8,9},{9,8},{16,17},{17,16},{24,25},{25,24},{2,3},{3,2... | collective-permute-start | bytes 196616 | tf_op jit(solution)/shard_map/ppermute | solution.py:873
  30.0 0.6 %collective-permute-start.11 = (bf16[2,2,64,128]{3,2,1,0:T(8,128)(2,1)S(1)}, bf16[2,2,64,128]{3,2,1,0:T(8,128)(2,1)S(1)}, u32[]{:S(2)}, u32[]{:S(2)}) collective-permute-start(bf16[2,2,64,128]{3,2,1,0:T(8,128)(2,1)S(1)} %get-tuple-element.63), channel_id=1, source_target_pairs={{0,16},{1,17},{8,24},{9,25},{16,0},{17,1},{24,8},{25,9},{2,18},{3,... | collective-permute-start | bytes 196616 | tf_op jit(solution)/shard_map/ppermute | solution.py:873
  30.5 1.9 %collective-permute-start.12 = (bf16[2,2,64,128]{3,2,1,0:T(8,128)(2,1)S(1)}, bf16[2,2,64,128]{3,2,1,0:T(8,128)(2,1)S(1)}, u32[]{:S(2)}, u32[]{:S(2)}) collective-permute-start(bf16[2,2,64,128]{3,2,1,0:T(8,128)(2,1)S(1)} %get-tuple-element.64), channel_id=1, source_target_pairs={{0,17},{1,16},{8,25},{9,24},{16,1},{17,0},{24,9},{25,8},{2,19},{3,... | collective-permute-start | bytes 196616 | tf_op jit(solution)/shard_map/ppermute | solution.py:873
  32.4 0.8 %collective-permute-done.10.refs_1_ = bf16[2,2,64,128]{3,2,1,0:T(8,128)(2,1)S(1)} collective-permute-done((bf16[2,2,64,128]{3,2,1,0:T(8,128)(2,1)S(1)}, bf16[2,2,64,128]{3,2,1,0:T(8,128)(2,1)S(1)}, u32[]{:S(2)}, u32[]{:S(2)}) %collective-permute-start.10) | collective-permute-done | bytes 65568 | tf_op jit(solution)/shard_map/ppermute | solution.py:873
  33.2 1.3 %collective-permute-done.11.refs_2_ = bf16[2,2,64,128]{3,2,1,0:T(8,128)(2,1)S(1)} collective-permute-done((bf16[2,2,64,128]{3,2,1,0:T(8,128)(2,1)S(1)}, bf16[2,2,64,128]{3,2,1,0:T(8,128)(2,1)S(1)}, u32[]{:S(2)}, u32[]{:S(2)}) %collective-permute-start.11) | collective-permute-done | bytes 65568 | tf_op jit(solution)/shard_map/ppermute | solution.py:873
  34.6 1.1 %collective-permute-done.12.refs_3_ = bf16[2,2,64,128]{3,2,1,0:T(8,128)(2,1)S(1)} collective-permute-done((bf16[2,2,64,128]{3,2,1,0:T(8,128)(2,1)S(1)}, bf16[2,2,64,128]{3,2,1,0:T(8,128)(2,1)S(1)}, u32[]{:S(2)}, u32[]{:S(2)}) %collective-permute-start.12) | collective-permute-done | bytes 65568 | tf_op jit(solution)/shard_map/ppermute | solution.py:873
  35.7 0.9 %shard_map.64 = bf16[64,2,8,128]{3,2,1,0:T(8,128)(2,1)} custom-call(bf16[2,2,64,128]{3,2,1,0:T(8,128)(2,1)S(1)} %get-tuple-element.61.refs_0_, bf16[2,2,64,128]{3,2,1,0:T(8,128)(2,1)S(1)} %collective-permute-done.10.refs_1_, bf16[2,2,64,128]{3,2,1,0:T(8,128)(2,1)S(1)} %collective-permute-done.11.refs_2_, ...), custom_call_target="tpu_custom_call" | custom-call | tf_op jit(solution)/shard_map/pallas_call | solution.py:896
  (8 shorter events, 0.1 us)
Async XLA Ops:
  0.0 7.0 %collective-permute-start = (f32[64,2,8,128]{3,2,1,0:T(8,128)}, f32[64,2,8,128]{3,2,1,0:T(8,128)S(1)}, u32[]{:S(2)}, u32[]{:S(2)}) collective-permute-start(f32[64,2,8,128]{3,2,1,0:T(8,128)} %param.5), channel_id=1, source_target_pairs={{0,8},{8,0},{16,24},{24,16},{1,9},{9,1},{17,25},{25,17},{2,10},{10... | collective-permute-start | bytes 1572872 | tf_op jit(solution)/shard_map/ppermute | solution.py:795
  2.0 12.0 %collective-permute-start.2 = (f16[560,128]{1,0:T(8,128)(2,1)S(1)}, f16[560,128]{1,0:T(8,128)(2,1)S(1)}, u32[]{:S(2)}, u32[]{:S(2)}) collective-permute-start(f16[560,128]{1,0:T(8,128)(2,1)S(1)} %convert_element_type.12), channel_id=1, source_target_pairs={{0,2},{2,4},{4,6},{6,0},{8,14},{10,8},{12,10},{14,12},{16,18},{18,... | collective-permute-start | bytes 430088 | tf_op jit(solution)/shard_map/ppermute | solution.py:833
  4.6 9.4 %collective-permute-start.3 = (f16[512,128]{1,0:T(8,128)(2,1)S(1)}, f16[512,128]{1,0:T(8,128)(2,1)S(1)}, u32[]{:S(2)}, u32[]{:S(2)}) collective-permute-start(f16[512,128]{1,0:T(8,128)(2,1)S(1)} %convert_element_type.14), channel_id=1, source_target_pairs={{0,14},{2,8},{4,10},{6,12},{8,2},{10,4},{12,6},{14,0},{16,30},{18,... | collective-permute-start | bytes 393224 | tf_op jit(solution)/shard_map/ppermute | solution.py:834
  7.7 7.3 %collective-permute-start.1 = (bf16[208,128]{1,0:T(8,128)(2,1)S(1)}, bf16[208,128]{1,0:T(8,128)(2,1)S(1)}, u32[]{:S(2)}, u32[]{:S(2)}) collective-permute-start(bf16[208,128]{1,0:T(8,128)(2,1)S(1)} %get-tuple-element.41), channel_id=1, source_target_pairs={{0,1},{1,0},{2,3},{3,2},{4,5},{5,4},{6,7},{7,6},{8,9},{9,8},{10,11... | collective-permute-start | bytes 159752 | tf_op jit(solution)/shard_map/ppermute | solution.py:846
  9.2 6.5 %collective-permute-start.4 = (bf16[80,128]{1,0:T(8,128)(2,1)S(1)}, bf16[80,128]{1,0:T(8,128)(2,1)S(1)}, u32[]{:S(2)}, u32[]{:S(2)}) collective-permute-start(bf16[80,128]{1,0:T(8,128)(2,1)S(1)} %get-tuple-element.47), channel_id=1, source_target_pairs={{0,3},{1,2},{2,5},{3,4},{4,7},{5,6},{6,1},{7,0},{8,15},{9,14},{10,... | collective-permute-start | bytes 61448 | tf_op jit(solution)/shard_map/ppermute | solution.py:847
  10.7 4.7 %collective-permute-start.5 = (f32[16,128]{1,0:T(8,128)S(1)}, f32[16,128]{1,0:T(8,128)S(1)}, u32[]{:S(2)}, u32[]{:S(2)}) collective-permute-start(f32[16,128]{1,0:T(8,128)S(1)} %get-tuple-element.48.obs_ref), channel_id=1, source_target_pairs={{0,8},{8,0},{16,24},{24,16},{1,9},{9,1},{17,25},{25,17},{2,10},{10... | collective-permute-start | bytes 24584 | tf_op jit(solution)/shard_map/ppermute | solution.py:829
  17.2 7.8 %collective-permute-start.6 = (bf16[304,128]{1,0:T(8,128)(2,1)S(1)}, bf16[304,128]{1,0:T(8,128)(2,1)S(1)}, u32[]{:S(2)}, u32[]{:S(2)}) collective-permute-start(bf16[304,128]{1,0:T(8,128)(2,1)S(1)} %get-tuple-element.50), channel_id=1, source_target_pairs={{0,1},{1,0},{8,9},{9,8},{16,17},{17,16},{24,25},{25,24},{2,3},{3,2... | collective-permute-start | bytes 233480 | tf_op jit(solution)/shard_map/ppermute | solution.py:873
  18.3 4.9 %collective-permute-start.7 = (bf16[256,128]{1,0:T(8,128)(2,1)S(1)}, bf16[256,128]{1,0:T(8,128)(2,1)S(1)}, u32[]{:S(2)}, u32[]{:S(2)}) collective-permute-start(bf16[256,128]{1,0:T(8,128)(2,1)S(1)} %get-tuple-element.51), channel_id=1, source_target_pairs={{0,16},{1,17},{8,24},{9,25},{16,0},{17,1},{24,8},{25,9},{2,18},{3,... | collective-permute-start | bytes 196616 | tf_op jit(solution)/shard_map/ppermute | solution.py:873
  19.8 5.2 %collective-permute-start.8 = (bf16[256,128]{1,0:T(8,128)(2,1)S(1)}, bf16[256,128]{1,0:T(8,128)(2,1)S(1)}, u32[]{:S(2)}, u32[]{:S(2)}) collective-permute-start(bf16[256,128]{1,0:T(8,128)(2,1)S(1)} %get-tuple-element.52), channel_id=1, source_target_pairs={{0,17},{1,16},{8,25},{9,24},{16,1},{17,0},{24,9},{25,8},{2,19},{3,... | collective-permute-start | bytes 196616 | tf_op jit(solution)/shard_map/ppermute | solution.py:873
  27.5 1.4 %collective-permute-start.9 = (bf16[4,2,64,128]{3,2,1,0:T(8,128)(2,1)S(1)}, bf16[4,2,64,128]{3,2,1,0:T(8,128)(2,1)S(1)}, u32[]{:S(2)}, u32[]{:S(2)}) collective-permute-start(bf16[4,2,64,128]{3,2,1,0:T(8,128)(2,1)S(1)} %get-tuple-element.53), channel_id=1, source_target_pairs={{0,8},{8,0},{16,24},{24,16},{1,9},{9,1},{17,25},{25,17},{2,10},{10... | collective-permute-start | bytes 393224 | tf_op jit(solution)/shard_map/ppermute | solution.py:888
  28.9 4.3 %collective-permute-start.10 = (bf16[2,2,64,128]{3,2,1,0:T(8,128)(2,1)S(1)}, bf16[2,2,64,128]{3,2,1,0:T(8,128)(2,1)S(1)}, u32[]{:S(2)}, u32[]{:S(2)}) collective-permute-start(bf16[2,2,64,128]{3,2,1,0:T(8,128)(2,1)S(1)} %get-tuple-element.62), channel_id=1, source_target_pairs={{0,1},{1,0},{8,9},{9,8},{16,17},{17,16},{24,25},{25,24},{2,3},{3,2... | collective-permute-start | bytes 196616 | tf_op jit(solution)/shard_map/ppermute | solution.py:873
  30.0 4.6 %collective-permute-start.11 = (bf16[2,2,64,128]{3,2,1,0:T(8,128)(2,1)S(1)}, bf16[2,2,64,128]{3,2,1,0:T(8,128)(2,1)S(1)}, u32[]{:S(2)}, u32[]{:S(2)}) collective-permute-start(bf16[2,2,64,128]{3,2,1,0:T(8,128)(2,1)S(1)} %get-tuple-element.63), channel_id=1, source_target_pairs={{0,16},{1,17},{8,24},{9,25},{16,0},{17,1},{24,8},{25,9},{2,18},{3,... | collective-permute-start | bytes 196616 | tf_op jit(solution)/shard_map/ppermute | solution.py:873
  30.5 5.2 %collective-permute-start.12 = (bf16[2,2,64,128]{3,2,1,0:T(8,128)(2,1)S(1)}, bf16[2,2,64,128]{3,2,1,0:T(8,128)(2,1)S(1)}, u32[]{:S(2)}, u32[]{:S(2)}) collective-permute-start(bf16[2,2,64,128]{3,2,1,0:T(8,128)(2,1)S(1)} %get-tuple-element.64), channel_id=1, source_target_pairs={{0,17},{1,16},{8,25},{9,24},{16,1},{17,0},{24,9},{25,8},{2,19},{3,... | collective-permute-start | bytes 196616 | tf_op jit(solution)/shard_map/ppermute | solution.py:873

commit v8 on v7

--- a/solution.py
+++ b/solution.py
@@ -213,7 +213,7 @@
 OCTET = 8
 GROUP = 32
 DOMAIN = 3 * HALO
-TOGETHER = 6
+TOGETHER = 9
 EXTENT = LANES + 2 * OCTET
 VMEM_GRANT = 24 << 20
 LARGEST = 6.0
@@ -550,7 +550,7 @@
     swap_two = jnp.bitwise_xor(place // 2, odd) == 1
     outs = (out0_ref, out1_ref, out2_ref, out3_ref)
 
-    def last_step(i, carry):
+    def last_group(i):
         results = [{}, {}]
         for k in range(2):
             start = OCTET + 2 * OCTET * i + OCTET * k
@@ -566,9 +566,13 @@
             rows = [jnp.where(swap_two, rows[t ^ 2], rows[t]) for t in range(HALO)]
             for d, out_ref in enumerate(outs):
                 out_ref[pl.ds(layer * LANES + at, 2 * OCTET), :] = rows[d]
+
+    def last_step(i, carry):
+        for k in range(2):
+            last_group(2 * i + k)
         return carry
 
-    lax.fori_loop(0, LANES // (2 * OCTET), last_step, 0)
+    lax.fori_loop(0, LANES // (4 * OCTET), last_step, 0)
 
 
 def dot(a, b, contract):

time: 36.7 us -> 36.6 us (level)
  no operation moved by 1% of the time
where the time goes in v8:
time: 36.6 us; the launch traced here: 36.5 us
  starting transfers between devices  15.7 us (43%)
  waiting for transfers between devices  11.6 us (32%)
  Pallas kernels  9 us (25%)
    ppermute x6, waiting for transfers between devices, exchange(): arrived.append(lax.ppermute(parts[d], ('mem', 'gy'), flip(d)))  7.43 us
    ppermute x6, starting transfers between devices, exchange(): arrived.append(lax.ppermute(parts[d], ('mem', 'gy'), flip(d)))  7.11 us
    pallas_call x8, Pallas kernels, vmem_call(): pl.pallas_call(kernel, out_shape=outs, in_specs=[spec] * len(args), out_s...  6.71 us
    ppermute x1, waiting for transfers between devices, on_device_tile(): lax.ppermute(other_out.astype(jnp.float16), ('mem', 'gx'), along_other)  2.78 us
    ppermute x1, starting transfers between devices, on_device_tile(): lax.ppermute(same_out.astype(jnp.float16), ('mem', 'gx'), along).astype(f32)  2.62 us
    ppermute x1, starting transfers between devices, on_device_tile(): lax.ppermute(other_out.astype(jnp.float16), ('mem', 'gx'), along_other)  2.37 us
    ppermute x1, starting transfers between devices, on_device_tile(): side = lax.ppermute(side_out, 'gy', across)  1.53 us
    ppermute x1, starting transfers between devices, on_device_tile(): corner = lax.ppermute(corner_out, ('mem', 'gx', 'gy'), diagonal)  1.52 us
  transfers between devices with their start and end apart: 13, of which 8 were waited for; matrix products, arithmetic and copies ran while one was open for 0% of the time, Pallas kernels for 11%

profile of v8, /device:TPU:0, one launch (start us, length us, event | category | flops | bytes accessed | tf_op | source)
XLA Modules:
  0.0 36.5 jit_solution(6042801448356706976)
XLA Ops:
  0.0 0.5 %collective-permute-start = (f32[64,2,8,128]{3,2,1,0:T(8,128)}, f32[64,2,8,128]{3,2,1,0:T(8,128)S(1)}, u32[]{:S(2)}, u32[]{:S(2)}) collective-permute-start(f32[64,2,8,128]{3,2,1,0:T(8,128)} %param.5), channel_id=1, source_target_pairs={{0,8},{8,0},{16,24},{24,16},{1,9},{9,1},{17,25},{25,17},{2,10},{10... | collective-permute-start | bytes 1572872 | tf_op jit(solution)/shard_map/ppermute | solution.py:799
  0.5 1.4 %shard_map.55 = (f32[1024,128]{1,0:T(8,128)S(1)}, f32[32,128]{1,0:T(8,128)S(1)}, f32[16,128]{1,0:T(8,128)S(1)}, f32[560,128]{1,0:T(8,128)S(1)}, f32[512,128]{1,0:T(8,128)S(1)}) custom-call(f32[1024,128]{1,0:T(8,128)} %bitcast.7, f32[32,128]{1,0:T(8,128)} %bitcast.8, s32[1,128]{1,0:T(1,128)} %bitcast.9, f32[1,128]{1,0:T(1,128)} %bitcast.10, f32[1,128]{1,0:T(1,128)} %bitcast.11), custom_call_target="tpu_custom_call" | custom-call | tf_op jit(solution)/shard_map/pallas_call | solution.py:802
  2.0 2.6 %collective-permute-start.2 = (f16[560,128]{1,0:T(8,128)(2,1)S(1)}, f16[560,128]{1,0:T(8,128)(2,1)S(1)}, u32[]{:S(2)}, u32[]{:S(2)}) collective-permute-start(f16[560,128]{1,0:T(8,128)(2,1)S(1)} %convert_element_type.12), channel_id=1, source_target_pairs={{0,2},{2,4},{4,6},{6,0},{8,14},{10,8},{12,10},{14,12},{16,18},{18,... | collective-permute-start | bytes 430088 | tf_op jit(solution)/shard_map/ppermute | solution.py:837
  4.6 2.4 %collective-permute-start.3 = (f16[512,128]{1,0:T(8,128)(2,1)S(1)}, f16[512,128]{1,0:T(8,128)(2,1)S(1)}, u32[]{:S(2)}, u32[]{:S(2)}) collective-permute-start(f16[512,128]{1,0:T(8,128)(2,1)S(1)} %convert_element_type.14), channel_id=1, source_target_pairs={{0,14},{2,8},{4,10},{6,12},{8,2},{10,4},{12,6},{14,0},{16,30},{18,... | collective-permute-start | bytes 393224 | tf_op jit(solution)/shard_map/ppermute | solution.py:838
  7.0 0.7 %shard_map.56 = (f32[3456,128]{1,0:T(8,128)S(1)}, bf16[208,128]{1,0:T(8,128)(2,1)S(1)}, bf16[80,128]{1,0:T(8,128)(2,1)S(1)}) custom-call(f32[1024,128]{1,0:T(8,128)S(1)} %get-tuple-element.35.own_ref, f32[1024,128]{1,0:T(8,128)S(1)} %bitcast.6, f32[32,128]{1,0:T(8,128)S(1)} %get-tuple-element.36.wind_ref, f32[560,128]{1,0:T(8,128)S(1)} %get-tuple-element.37.same_ref), custom_call_target="tpu_custom_call" | custom-call | tf_op jit(solution)/shard_map/pallas_call | solution.py:766
  7.7 1.5 %collective-permute-start.1 = (bf16[208,128]{1,0:T(8,128)(2,1)S(1)}, bf16[208,128]{1,0:T(8,128)(2,1)S(1)}, u32[]{:S(2)}, u32[]{:S(2)}) collective-permute-start(bf16[208,128]{1,0:T(8,128)(2,1)S(1)} %get-tuple-element.41), channel_id=1, source_target_pairs={{0,1},{1,0},{2,3},{3,2},{4,5},{5,4},{6,7},{7,6},{8,9},{9,8},{10,11... | collective-permute-start | bytes 159752 | tf_op jit(solution)/shard_map/ppermute | solution.py:850
  9.2 1.5 %collective-permute-start.4 = (bf16[80,128]{1,0:T(8,128)(2,1)S(1)}, bf16[80,128]{1,0:T(8,128)(2,1)S(1)}, u32[]{:S(2)}, u32[]{:S(2)}) collective-permute-start(bf16[80,128]{1,0:T(8,128)(2,1)S(1)} %get-tuple-element.47), channel_id=1, source_target_pairs={{0,3},{1,2},{2,5},{3,4},{4,7},{5,6},{6,1},{7,0},{8,15},{9,14},{10,... | collective-permute-start | bytes 61448 | tf_op jit(solution)/shard_map/ppermute | solution.py:851
  10.7 0.0 collective-permute-start.5
  10.7 0.5 %shard_map.57.winds_ref.__ = f32[6912,128]{1,0:T(8,128)S(1)} custom-call(f32[32,128]{1,0:T(8,128)S(1)} %get-tuple-element.36.wind_ref), custom_call_target="tpu_custom_call" | custom-call | tf_op jit(solution)/shard_map/pallas_call | solution.py:766
  11.2 2.8 %collective-permute-done.3 = f16[512,128]{1,0:T(8,128)(2,1)S(1)} collective-permute-done((f16[512,128]{1,0:T(8,128)(2,1)S(1)}, f16[512,128]{1,0:T(8,128)(2,1)S(1)}, u32[]{:S(2)}, u32[]{:S(2)}) %collective-permute-start.3) | collective-permute-done | bytes 131104 | tf_op jit(solution)/shard_map/ppermute | solution.py:838
  14.0 0.0 collective-permute-done.2
  14.0 0.9 %shard_map.58 = (f32[3456,128]{1,0:T(8,128)S(1)}, f32[3456,128]{1,0:T(8,128)S(1)}) custom-call(f32[3456,128]{1,0:T(8,128)S(1)} %get-tuple-element.38.field_ref._, f32[6912,128]{1,0:T(8,128)S(1)} %shard_map.57.winds_ref.__), custom_call_target="tpu_custom_call" | custom-call | tf_op jit(solution)/shard_map/pallas_call | solution.py:766
  14.9 0.0 collective-permute-done.1.side_ref
  14.9 0.4 %shard_map.59 = (f32[3456,128]{1,0:T(8,128)S(1)}, f32[6912,128]{1,0:T(8,128)S(1)}, f32[3456,128]{1,0:T(8,128)S(1)}, f32[3456,128]{1,0:T(8,128)S(1)}) custom-call(f32[3456,128]{1,0:T(8,128)S(1)} %get-tuple-element.38.field_ref._, f32[6912,128]{1,0:T(8,128)S(1)} %shard_map.57.winds_ref.__, ...), custom_call_target="tpu_custom_call", output_to_operand_aliasing={{0}: (0, {}), {1}: (1, {}), {2}: (2, {}), {3}: (3, {})} | custom-call | tf_op jit(solution)/shard_map/pallas_call | solution.py:766
  15.4 0.3 collective-permute-done.4.corner_ref
  15.7 1.5 %shard_map.60 = (bf16[256,128]{1,0:T(8,128)(2,1)S(1)}, bf16[304,128]{1,0:T(8,128)(2,1)S(1)}, bf16[256,128]{1,0:T(8,128)(2,1)S(1)}, bf16[256,128]{1,0:T(8,128)(2,...) custom-call(f32[3456,128]{1,0:T(8,128)S(1)} %get-tuple-element.42._,, ...), custom_call_target="tpu_custom_call", output_to_operand_aliasing={{4}: (0, {}), {5}: (1, {}), {6}: (2, {}), {7}: (3, {})} | custom-call | tf_op jit(solution)/shard_map/pallas_call | solution.py:766
  17.2 1.1 %collective-permute-start.6 = (bf16[304,128]{1,0:T(8,128)(2,1)S(1)}, bf16[304,128]{1,0:T(8,128)(2,1)S(1)}, u32[]{:S(2)}, u32[]{:S(2)}) collective-permute-start(bf16[304,128]{1,0:T(8,128)(2,1)S(1)} %get-tuple-element.50), channel_id=1, source_target_pairs={{0,1},{1,0},{8,9},{9,8},{16,17},{17,16},{24,25},{25,24},{2,3},{3,2... | collective-permute-start | bytes 233480 | tf_op jit(solution)/shard_map/ppermute | solution.py:877
  18.2 1.5 %collective-permute-start.7 = (bf16[256,128]{1,0:T(8,128)(2,1)S(1)}, bf16[256,128]{1,0:T(8,128)(2,1)S(1)}, u32[]{:S(2)}, u32[]{:S(2)}) collective-permute-start(bf16[256,128]{1,0:T(8,128)(2,1)S(1)} %get-tuple-element.51), channel_id=1, source_target_pairs={{0,16},{1,17},{8,24},{9,25},{16,0},{17,1},{24,8},{25,9},{2,18},{3,... | collective-permute-start | bytes 196616 | tf_op jit(solution)/shard_map/ppermute | solution.py:877
  19.7 1.0 %collective-permute-start.8 = (bf16[256,128]{1,0:T(8,128)(2,1)S(1)}, bf16[256,128]{1,0:T(8,128)(2,1)S(1)}, u32[]{:S(2)}, u32[]{:S(2)}) collective-permute-start(bf16[256,128]{1,0:T(8,128)(2,1)S(1)} %get-tuple-element.52), channel_id=1, source_target_pairs={{0,17},{1,16},{8,25},{9,24},{16,1},{17,0},{24,9},{25,8},{2,19},{3,... | collective-permute-start | bytes 196616 | tf_op jit(solution)/shard_map/ppermute | solution.py:877
  20.7 2.5 %collective-permute-done.7.piece2_ref = bf16[256,128]{1,0:T(8,128)(2,1)S(1)} collective-permute-done((bf16[256,128]{1,0:T(8,128)(2,1)S(1)}, bf16[256,128]{1,0:T(8,128)(2,1)S(1)}, u32[]{:S(2)}, u32[]{:S(2)}) %collective-permute-start.7) | collective-permute-done | bytes 65568 | tf_op jit(solution)/shard_map/ppermute | solution.py:877
  23.2 1.7 %collective-permute-done.8.piece3_ref = bf16[256,128]{1,0:T(8,128)(2,1)S(1)} collective-permute-done((bf16[256,128]{1,0:T(8,128)(2,1)S(1)}, bf16[256,128]{1,0:T(8,128)(2,1)S(1)}, u32[]{:S(2)}, u32[]{:S(2)}) %collective-permute-start.8) | collective-permute-done | bytes 65568 | tf_op jit(solution)/shard_map/ppermute | solution.py:877
  24.9 2.5 %shard_map.61 = (bf16[4,2,64,128]{3,2,1,0:T(8,128)(2,1)S(1)}, bf16[512,256]{1,0:T(8,128)(2,1)S(1)}, bf16[256,256]{1,0:T(8,128)(2,1)S(1)}, f32[8,512]{1,0:T(8,128)S(1)}) custom-call(bf16[256,128]{1,0:T(8,128)(2,1)S(1)} %get-tuple-element.49.piece0_ref, bf16[304,128]{1,0:T(8,128)(2,1)S(1)} %collective-permute-done.6.piece1_ref, ...), custom_call_target="tpu_custom_call" | custom-call | tf_op jit(solution)/shard_map/pallas_call | solution.py:766
  27.4 0.1 collective-permute-start.9
  27.5 0.3 shard_map.62
  27.7 1.1 %collective-permute-done.9.received_ref = bf16[4,2,64,128]{3,2,1,0:T(8,128)(2,1)S(1)} collective-permute-done((bf16[4,2,64,128]{3,2,1,0:T(8,128)(2,1)S(1)}, bf16[4,2,64,128]{3,2,1,0:T(8,128)(2,1)S(1)}, u32[]{:S(2)}, u32[]{:S(2)}) %collective-permute-start.9) | collective-permute-done | bytes 131104 | tf_op jit(solution)/shard_map/ppermute | solution.py:892
  28.8 1.1 %collective-permute-start.10 = (bf16[2,2,64,128]{3,2,1,0:T(8,128)(2,1)S(1)}, bf16[2,2,64,128]{3,2,1,0:T(8,128)(2,1)S(1)}, u32[]{:S(2)}, u32[]{:S(2)}) collective-permute-start(bf16[2,2,64,128]{3,2,1,0:T(8,128)(2,1)S(1)} %get-tuple-element.62), channel_id=1, source_target_pairs={{0,1},{1,0},{8,9},{9,8},{16,17},{17,16},{24,25},{25,24},{2,3},{3,2... | collective-permute-start | bytes 196616 | tf_op jit(solution)/shard_map/ppermute | solution.py:877
  29.9 0.5 %collective-permute-start.11 = (bf16[2,2,64,128]{3,2,1,0:T(8,128)(2,1)S(1)}, bf16[2,2,64,128]{3,2,1,0:T(8,128)(2,1)S(1)}, u32[]{:S(2)}, u32[]{:S(2)}) collective-permute-start(bf16[2,2,64,128]{3,2,1,0:T(8,128)(2,1)S(1)} %get-tuple-element.63), channel_id=1, source_target_pairs={{0,16},{1,17},{8,24},{9,25},{16,0},{17,1},{24,8},{25,9},{2,18},{3,... | collective-permute-start | bytes 196616 | tf_op jit(solution)/shard_map/ppermute | solution.py:877
  30.4 1.9 %collective-permute-start.12 = (bf16[2,2,64,128]{3,2,1,0:T(8,128)(2,1)S(1)}, bf16[2,2,64,128]{3,2,1,0:T(8,128)(2,1)S(1)}, u32[]{:S(2)}, u32[]{:S(2)}) collective-permute-start(bf16[2,2,64,128]{3,2,1,0:T(8,128)(2,1)S(1)} %get-tuple-element.64), channel_id=1, source_target_pairs={{0,17},{1,16},{8,25},{9,24},{16,1},{17,0},{24,9},{25,8},{2,19},{3,... | collective-permute-start | bytes 196616 | tf_op jit(solution)/shard_map/ppermute | solution.py:877
  32.4 0.8 %collective-permute-done.10.refs_1_ = bf16[2,2,64,128]{3,2,1,0:T(8,128)(2,1)S(1)} collective-permute-done((bf16[2,2,64,128]{3,2,1,0:T(8,128)(2,1)S(1)}, bf16[2,2,64,128]{3,2,1,0:T(8,128)(2,1)S(1)}, u32[]{:S(2)}, u32[]{:S(2)}) %collective-permute-start.10) | collective-permute-done | bytes 65568 | tf_op jit(solution)/shard_map/ppermute | solution.py:877
  33.1 1.3 %collective-permute-done.11.refs_2_ = bf16[2,2,64,128]{3,2,1,0:T(8,128)(2,1)S(1)} collective-permute-done((bf16[2,2,64,128]{3,2,1,0:T(8,128)(2,1)S(1)}, bf16[2,2,64,128]{3,2,1,0:T(8,128)(2,1)S(1)}, u32[]{:S(2)}, u32[]{:S(2)}) %collective-permute-start.11) | collective-permute-done | bytes 65568 | tf_op jit(solution)/shard_map/ppermute | solution.py:877
  34.5 1.2 %collective-permute-done.12.refs_3_ = bf16[2,2,64,128]{3,2,1,0:T(8,128)(2,1)S(1)} collective-permute-done((bf16[2,2,64,128]{3,2,1,0:T(8,128)(2,1)S(1)}, bf16[2,2,64,128]{3,2,1,0:T(8,128)(2,1)S(1)}, u32[]{:S(2)}, u32[]{:S(2)}) %collective-permute-start.12) | collective-permute-done | bytes 65568 | tf_op jit(solution)/shard_map/ppermute | solution.py:877
  35.6 0.9 %shard_map.64 = bf16[64,2,8,128]{3,2,1,0:T(8,128)(2,1)} custom-call(bf16[2,2,64,128]{3,2,1,0:T(8,128)(2,1)S(1)} %get-tuple-element.61.refs_0_, bf16[2,2,64,128]{3,2,1,0:T(8,128)(2,1)S(1)} %collective-permute-done.10.refs_1_, bf16[2,2,64,128]{3,2,1,0:T(8,128)(2,1)S(1)} %collective-permute-done.11.refs_2_, ...), custom_call_target="tpu_custom_call" | custom-call | tf_op jit(solution)/shard_map/pallas_call | solution.py:900
  (8 shorter events, 0.1 us)
Async XLA Ops:
  0.0 7.0 %collective-permute-start = (f32[64,2,8,128]{3,2,1,0:T(8,128)}, f32[64,2,8,128]{3,2,1,0:T(8,128)S(1)}, u32[]{:S(2)}, u32[]{:S(2)}) collective-permute-start(f32[64,2,8,128]{3,2,1,0:T(8,128)} %param.5), channel_id=1, source_target_pairs={{0,8},{8,0},{16,24},{24,16},{1,9},{9,1},{17,25},{25,17},{2,10},{10... | collective-permute-start | bytes 1572872 | tf_op jit(solution)/shard_map/ppermute | solution.py:799
  2.0 12.0 %collective-permute-start.2 = (f16[560,128]{1,0:T(8,128)(2,1)S(1)}, f16[560,128]{1,0:T(8,128)(2,1)S(1)}, u32[]{:S(2)}, u32[]{:S(2)}) collective-permute-start(f16[560,128]{1,0:T(8,128)(2,1)S(1)} %convert_element_type.12), channel_id=1, source_target_pairs={{0,2},{2,4},{4,6},{6,0},{8,14},{10,8},{12,10},{14,12},{16,18},{18,... | collective-permute-start | bytes 430088 | tf_op jit(solution)/shard_map/ppermute | solution.py:837
  4.6 9.4 %collective-permute-start.3 = (f16[512,128]{1,0:T(8,128)(2,1)S(1)}, f16[512,128]{1,0:T(8,128)(2,1)S(1)}, u32[]{:S(2)}, u32[]{:S(2)}) collective-permute-start(f16[512,128]{1,0:T(8,128)(2,1)S(1)} %convert_element_type.14), channel_id=1, source_target_pairs={{0,14},{2,8},{4,10},{6,12},{8,2},{10,4},{12,6},{14,0},{16,30},{18,... | collective-permute-start | bytes 393224 | tf_op jit(solution)/shard_map/ppermute | solution.py:838
  7.7 7.2 %collective-permute-start.1 = (bf16[208,128]{1,0:T(8,128)(2,1)S(1)}, bf16[208,128]{1,0:T(8,128)(2,1)S(1)}, u32[]{:S(2)}, u32[]{:S(2)}) collective-permute-start(bf16[208,128]{1,0:T(8,128)(2,1)S(1)} %get-tuple-element.41), channel_id=1, source_target_pairs={{0,1},{1,0},{2,3},{3,2},{4,5},{5,4},{6,7},{7,6},{8,9},{9,8},{10,11... | collective-permute-start | bytes 159752 | tf_op jit(solution)/shard_map/ppermute | solution.py:850
  9.2 6.5 %collective-permute-start.4 = (bf16[80,128]{1,0:T(8,128)(2,1)S(1)}, bf16[80,128]{1,0:T(8,128)(2,1)S(1)}, u32[]{:S(2)}, u32[]{:S(2)}) collective-permute-start(bf16[80,128]{1,0:T(8,128)(2,1)S(1)} %get-tuple-element.47), channel_id=1, source_target_pairs={{0,3},{1,2},{2,5},{3,4},{4,7},{5,6},{6,1},{7,0},{8,15},{9,14},{10,... | collective-permute-start | bytes 61448 | tf_op jit(solution)/shard_map/ppermute | solution.py:851
  10.7 4.6 %collective-permute-start.5 = (f32[16,128]{1,0:T(8,128)S(1)}, f32[16,128]{1,0:T(8,128)S(1)}, u32[]{:S(2)}, u32[]{:S(2)}) collective-permute-start(f32[16,128]{1,0:T(8,128)S(1)} %get-tuple-element.48.obs_ref), channel_id=1, source_target_pairs={{0,8},{8,0},{16,24},{24,16},{1,9},{9,1},{17,25},{25,17},{2,10},{10... | collective-permute-start | bytes 24584 | tf_op jit(solution)/shard_map/ppermute | solution.py:833
  17.2 7.7 %collective-permute-start.6 = (bf16[304,128]{1,0:T(8,128)(2,1)S(1)}, bf16[304,128]{1,0:T(8,128)(2,1)S(1)}, u32[]{:S(2)}, u32[]{:S(2)}) collective-permute-start(bf16[304,128]{1,0:T(8,128)(2,1)S(1)} %get-tuple-element.50), channel_id=1, source_target_pairs={{0,1},{1,0},{8,9},{9,8},{16,17},{17,16},{24,25},{25,24},{2,3},{3,2... | collective-permute-start | bytes 233480 | tf_op jit(solution)/shard_map/ppermute | solution.py:877
  18.2 4.9 %collective-permute-start.7 = (bf16[256,128]{1,0:T(8,128)(2,1)S(1)}, bf16[256,128]{1,0:T(8,128)(2,1)S(1)}, u32[]{:S(2)}, u32[]{:S(2)}) collective-permute-start(bf16[256,128]{1,0:T(8,128)(2,1)S(1)} %get-tuple-element.51), channel_id=1, source_target_pairs={{0,16},{1,17},{8,24},{9,25},{16,0},{17,1},{24,8},{25,9},{2,18},{3,... | collective-permute-start | bytes 196616 | tf_op jit(solution)/shard_map/ppermute | solution.py:877
  19.7 5.2 %collective-permute-start.8 = (bf16[256,128]{1,0:T(8,128)(2,1)S(1)}, bf16[256,128]{1,0:T(8,128)(2,1)S(1)}, u32[]{:S(2)}, u32[]{:S(2)}) collective-permute-start(bf16[256,128]{1,0:T(8,128)(2,1)S(1)} %get-tuple-element.52), channel_id=1, source_target_pairs={{0,17},{1,16},{8,25},{9,24},{16,1},{17,0},{24,9},{25,8},{2,19},{3,... | collective-permute-start | bytes 196616 | tf_op jit(solution)/shard_map/ppermute | solution.py:877
  27.4 1.4 %collective-permute-start.9 = (bf16[4,2,64,128]{3,2,1,0:T(8,128)(2,1)S(1)}, bf16[4,2,64,128]{3,2,1,0:T(8,128)(2,1)S(1)}, u32[]{:S(2)}, u32[]{:S(2)}) collective-permute-start(bf16[4,2,64,128]{3,2,1,0:T(8,128)(2,1)S(1)} %get-tuple-element.53), channel_id=1, source_target_pairs={{0,8},{8,0},{16,24},{24,16},{1,9},{9,1},{17,25},{25,17},{2,10},{10... | collective-permute-start | bytes 393224 | tf_op jit(solution)/shard_map/ppermute | solution.py:892
  28.8 4.3 %collective-permute-start.10 = (bf16[2,2,64,128]{3,2,1,0:T(8,128)(2,1)S(1)}, bf16[2,2,64,128]{3,2,1,0:T(8,128)(2,1)S(1)}, u32[]{:S(2)}, u32[]{:S(2)}) collective-permute-start(bf16[2,2,64,128]{3,2,1,0:T(8,128)(2,1)S(1)} %get-tuple-element.62), channel_id=1, source_target_pairs={{0,1},{1,0},{8,9},{9,8},{16,17},{17,16},{24,25},{25,24},{2,3},{3,2... | collective-permute-start | bytes 196616 | tf_op jit(solution)/shard_map/ppermute | solution.py:877
  29.9 4.6 %collective-permute-start.11 = (bf16[2,2,64,128]{3,2,1,0:T(8,128)(2,1)S(1)}, bf16[2,2,64,128]{3,2,1,0:T(8,128)(2,1)S(1)}, u32[]{:S(2)}, u32[]{:S(2)}) collective-permute-start(bf16[2,2,64,128]{3,2,1,0:T(8,128)(2,1)S(1)} %get-tuple-element.63), channel_id=1, source_target_pairs={{0,16},{1,17},{8,24},{9,25},{16,0},{17,1},{24,8},{25,9},{2,18},{3,... | collective-permute-start | bytes 196616 | tf_op jit(solution)/shard_map/ppermute | solution.py:877
  30.4 5.2 %collective-permute-start.12 = (bf16[2,2,64,128]{3,2,1,0:T(8,128)(2,1)S(1)}, bf16[2,2,64,128]{3,2,1,0:T(8,128)(2,1)S(1)}, u32[]{:S(2)}, u32[]{:S(2)}) collective-permute-start(bf16[2,2,64,128]{3,2,1,0:T(8,128)(2,1)S(1)} %get-tuple-element.64), channel_id=1, source_target_pairs={{0,17},{1,16},{8,25},{9,24},{16,1},{17,0},{24,9},{25,8},{2,19},{3,... | collective-permute-start | bytes 196616 | tf_op jit(solution)/shard_map/ppermute | solution.py:877
